TPU v7x, 32 devices: a whole 2x2x4 slice. The times are simulated.
32 devices in a mesh: groups: 2 (over y), row: 4 (over x, core), col: 4 (over z).
Axes of the slice: x: 2, y: 2, z: 4, core: 2. Of those that a mesh axis runs over, the one named last changes fastest.
Arguments:
- features: bfloat16 [512, 256, 128], P(('groups', 'row'), 'col'), parts along dimension 0, may hold values from -6 to 6
- kernel_first: bfloat16 [3, 3, 128, 128], replicated, may hold values from -0.1875 to 0.1875
- bias_first: float32 [128], replicated, may hold values from -3 to 3
- mixer_first: bfloat16 [128, 128], replicated, may hold values from -0.5 to 0.5
- shift_first: float32 [128], replicated, may hold values from -3 to 3
- kernel_second: bfloat16 [3, 3, 128, 128], replicated, may hold values from -0.1875 to 0.1875
- bias_second: float32 [128], replicated, may hold values from -3 to 3
- mixer_second: bfloat16 [128, 128], replicated, may hold values from -0.5 to 0.5
- shift_second: float32 [128], replicated, may hold values from -3 to 3
Outputs:
- contacts: float32 [512, 256, 128], P(('groups', 'row'), 'col'), parts along dimension 0
There are 2 independent parts, one for each index of `groups`. A program takes and returns all parts, laid end to end along the dimension named above; an argument that names none is the same for every part. Nothing has to cross between parts.
All inputs are finite; a program needn't handle non-finite values.
Results may differ from a plain program's by a relative error of at most 0.0045.
Values may be sent and summed in bfloat16 or wider, within the bound.
No kernel may reach another device: no remote copies, remote signals or barrier semaphores. Data moves between devices by JAX's collectives and lax.ppermute only.
A program may use at most 64 MiB of HBM per device.

v0:
```python
import functools

import jax
import jax.numpy as jnp
from jax import lax
from jax.experimental import pallas as pl
from jax.experimental.pallas import tpu as pltpu
from jax.sharding import PartitionSpec as P


BF16 = jnp.bfloat16
F32 = jnp.float32
NEAR = 2
FAR = 4
HALO = NEAR + FAR
PAD = 8
LEAD = 16
GRANT = 28 << 20


def mirror_routes(count):
    straight, hop, onward = [], [], []
    for r in range(count):
        for c in range(count):
            if r == c:
                continue
            if r + c == count - 1:
                hop.append((r * count + c, c * count + c))
                onward.append((c * count + c, c * count + r))
            else:
                straight.append((r * count + c, c * count + r))
    return straight, hop, onward


def paired_taps(kernel):
    channels = kernel.shape[2]
    flat = kernel.reshape(3, 3 * channels, channels)
    zero = jnp.zeros((1, 3 * channels, channels), kernel.dtype)
    near = jnp.concatenate([flat, zero], axis=0)
    far = jnp.concatenate([zero, flat], axis=0)
    return jnp.concatenate([near, far], axis=2).reshape(12 * channels, 2 * channels)


def twice(matrix):
    zero = jnp.zeros_like(matrix)
    return jnp.concatenate(
        [
            jnp.concatenate([matrix, zero], axis=1),
            jnp.concatenate([zero, matrix], axis=1),
        ],
        axis=0,
    )


def fill_edges(ext, above, below, left, right, size):
    rows = size + 2 * HALO
    ext[:, 0 : LEAD - PAD, :] = jnp.zeros((rows, LEAD - PAD, ext.shape[2]), BF16)
    tail = LEAD + size + PAD
    ext[:, tail:, :] = jnp.zeros((rows, ext.shape[1] - tail, ext.shape[2]), BF16)
    ext[0:HALO, LEAD : LEAD + size, :] = above[...]
    ext[HALO + size :, LEAD : LEAD + size, :] = below[...]
    ext[:, LEAD - PAD : LEAD, :] = left[...]
    ext[:, LEAD + size : tail, :] = right[...]


def near_block(wide, taps, bias, mix, group, groups, width, channels):
    rows = groups * NEAR * width
    part = jnp.concatenate(
        [
            wide[pl.ds(group + tap // 2, groups), tap % 2].reshape(rows, 3 * channels)
            for tap in range(4)
        ],
        axis=1,
    )
    total = jnp.dot(part, taps[...], preferred_element_type=F32)
    active = jnp.maximum(total + bias[...], 0.0).astype(BF16)
    return jnp.dot(active, mix[...], preferred_element_type=F32)


def center_rows(wide, half, group, groups, channels):
    center = wide[pl.ds(group + half, groups), 1 - half]
    return center[..., channels : 2 * channels].astype(F32)


def widen(ext, wide, width, start, channels):
    for tap in range(3):
        begin = start + (tap - 1) * NEAR
        lanes = slice(tap * channels, (tap + 1) * channels)
        for row in range(ext.shape[0]):
            group, rest = divmod(row, 2 * NEAR)
            wide[group, rest // NEAR, rest % NEAR, :, lanes] = ext[
                row, begin : begin + width, :
            ]


def own_kernel(
    tile, above, below, left, right, taps, bias, mix, shift, out, ext, wide, *, steps
):
    size, channels = tile.shape[0], tile.shape[2]
    width = size + 2 * PAD
    fill_edges(ext, *(edge.at[0] for edge in (above, below, left, right)), size)
    ext[HALO : HALO + size, LEAD : LEAD + size, :] = tile[...]
    widen(ext, wide, width, LEAD - PAD, channels)
    groups = out.shape[0] // steps

    def step(k, carry):
        group = k * groups
        mixed = near_block(wide, taps, bias, mix, group, groups, width, channels)
        for half in range(2):
            part = mixed[:, half * channels : (half + 1) * channels]
            part = part.reshape(groups, NEAR, width, channels)
            value = center_rows(wide, half, group, groups, channels) * 0.5 + part
            out[pl.ds(group, groups), half] = (value + shift[...]).astype(BF16)
        return carry

    lax.fori_loop(0, steps, step, 0)


def place_mirror(ext, frame, inside, size):
    channels = ext.shape[2]
    high = size - 2 * HALO
    band, side = HALO * size, high * PAD
    top, low = 2 * HALO, HALO + size - HALO
    lead, tail = LEAD + PAD, LEAD + size - PAD
    ext[HALO:top, LEAD : LEAD + size, :] = frame[0:band].reshape(HALO, size, channels)
    ext[low : low + HALO, LEAD : LEAD + size, :] = frame[band : 2 * band].reshape(
        HALO, size, channels
    )
    ext[top:low, LEAD:lead, :] = frame[2 * band : 2 * band + side].reshape(
        high, PAD, channels
    )
    ext[top:low, tail : tail + PAD, :] = frame[2 * band + side :].reshape(
        high, PAD, channels
    )
    ext[top:low, lead:tail, :] = inside[...]


def main_kernel(
    frame,
    own,
    direct,
    relayed,
    rows_above,
    rows_below,
    columns_left,
    columns_right,
    summed,
    taps,
    bias,
    mix,
    far_taps,
    far_bias,
    far_mix,
    far_shift,
    out,
    ext,
    wide,
    first,
    far_wide,
    stage,
    sems,
    *,
    steps,
    far_rows,
):
    size, channels = out.shape[0], out.shape[2]
    width = size + 2 * PAD
    row, col = lax.axis_index("row"), lax.axis_index("col")
    last = lax.axis_size("row") - 1
    diagonal = row == col
    anti = jnp.logical_and(row + col == last, row != col)
    plain = jnp.logical_not(jnp.logical_or(diagonal, anti))

    edges = (rows_above, rows_below, columns_left, columns_right)
    fill_edges(ext, *(edge.at[1] for edge in edges), size)
    for source, chosen in ((own, diagonal), (direct, plain), (relayed, anti)):

        @pl.when(chosen)
        def _(source=source):
            place_mirror(ext, frame, source, size)

    widen(ext, wide, width, LEAD - PAD, channels)
    total_groups = summed.shape[0]
    groups = total_groups // steps

    def step(k, carry):
        group = k * groups
        mixed = near_block(wide, taps, bias, mix, group, groups, width, channels)
        for half in range(2):
            part = mixed[:, half * channels : (half + 1) * channels]
            part = part.reshape(groups, NEAR, width, channels)
            value = center_rows(wide, half, group, groups, channels) * 0.5 + part
            value = value + summed[pl.ds(group, groups), half].astype(F32)
            first[pl.ds(group, groups), half] = jnp.maximum(value, 0.0).astype(BF16)
        return carry

    lax.fori_loop(0, steps, step, 0)

    edge = FAR // (2 * NEAR)

    @pl.when(row == 0)
    def _():
        first[0:edge] = jnp.zeros((edge,) + first.shape[1:], BF16)

    @pl.when(row == last)
    def _():
        first[total_groups - edge :] = jnp.zeros((edge,) + first.shape[1:], BF16)

    @pl.when(col == 0)
    def _():
        first[:, :, :, 0:PAD, :] = jnp.zeros(
            first.shape[:3] + (PAD, channels), BF16
        )

    @pl.when(col == last)
    def _():
        first[:, :, :, PAD + size :, :] = jnp.zeros(
            first.shape[:3] + (PAD, channels), BF16
        )

    for tap in range(3):
        begin = PAD + (tap - 1) * FAR
        far_wide[:, :, tap * channels : (tap + 1) * channels] = first[
            :, :, :, begin : begin + size, :
        ].reshape(size + 2 * FAR, size, channels)

    def copy(slot, base):
        return pltpu.make_async_copy(
            stage.at[slot], out.at[pl.ds(base, far_rows)], sems.at[slot]
        )

    count = size // far_rows

    def far_step(k, carry):
        slot = lax.rem(k, 2)
        base = k * far_rows

        @pl.when(k >= 2)
        def _():
            copy(slot, base - 2 * far_rows).wait()

        rows = far_rows * size
        part = jnp.concatenate(
            [
                far_wide[pl.ds(base + tap * FAR, far_rows)].reshape(rows, 3 * channels)
                for tap in range(3)
            ],
            axis=1,
        )
        total = jnp.dot(part, far_taps[...], preferred_element_type=F32)
        active = jnp.maximum(total + far_bias[...], 0.0).astype(BF16)
        mixed = jnp.dot(active, far_mix[...], preferred_element_type=F32)
        center = far_wide[pl.ds(base + FAR, far_rows), :, channels : 2 * channels]
        center = center.reshape(rows, channels).astype(F32)
        value = jnp.maximum(center + far_shift[...] + mixed, 0.0)
        stage[slot] = value.reshape(far_rows, size, channels)
        copy(slot, base).start()
        return carry

    lax.fori_loop(0, count, far_step, 0)
    for k in range(max(count - 2, 0), count):
        copy(k % 2, k * far_rows).wait()


def edge_strips(frame, size):
    high = size - 2 * HALO
    channels = frame.shape[1]
    band, side = HALO * size, high * PAD
    top = frame[0:band].reshape(HALO, size, channels)
    low = frame[band : 2 * band].reshape(HALO, size, channels)
    left = frame[2 * band : 2 * band + side].reshape(high, PAD, channels)
    right = frame[2 * band + side :].reshape(high, PAD, channels)
    left = jnp.concatenate([top[:, :PAD], left, low[:, :PAD]], axis=0)
    right = jnp.concatenate([top[:, size - PAD :], right, low[:, size - PAD :]], axis=0)
    return top, low, left, right


def exchange(strips_low, strips_high, axis):
    count = lax.axis_size(axis)
    before = lax.ppermute(strips_high, axis, [(i, i + 1) for i in range(count - 1)])
    after = lax.ppermute(strips_low, axis, [(i + 1, i) for i in range(count - 1)])
    return before, after


def halo_pieces(top, low, left, right):
    size = top.shape[2]
    above, below = exchange(top, low, "row")
    start = jnp.concatenate([above[:, :, :PAD], left, below[:, :, :PAD]], axis=1)
    end = jnp.concatenate(
        [above[:, :, size - PAD :], right, below[:, :, size - PAD :]], axis=1
    )
    before, after = exchange(start, end, "col")
    return above, below, before, after


def compute(
    features,
    kernel_first,
    bias_first,
    mixer_first,
    shift_first,
    kernel_second,
    bias_second,
    mixer_second,
    shift_second,
):
    size, _, channels = features.shape
    count = lax.axis_size("row")
    rows = size + 2 * HALO
    width = size + 2 * PAD
    groups = (size + 2 * FAR) // (2 * NEAR)
    pair = ("row", "col")
    straight, hop, onward = mirror_routes(count)

    def send(value, route):
        return lax.ppermute(value, pair, route)

    turned = jnp.swapaxes(features, 0, 1)
    inner = turned[HALO : size - HALO]
    frame = jnp.concatenate(
        [
            piece.reshape(-1, channels)
            for piece in (
                turned[:HALO],
                turned[size - HALO :],
                inner[:, :PAD],
                inner[:, size - PAD :],
            )
        ],
        axis=0,
    )
    inside = inner[:, PAD : size - PAD]
    direct_frame = send(frame, straight + hop)
    hop_inside = send(inside, hop)
    direct = send(inside, straight)
    relayed_frame = send(direct_frame, onward)
    relayed = send(hop_inside, onward)

    row, col = lax.axis_index("row"), lax.axis_index("col")
    diagonal = row == col
    anti = row + col == count - 1
    mirror_frame = jnp.where(
        diagonal, frame, jnp.where(anti, relayed_frame, direct_frame)
    )
    own_edges = (
        features[:HALO],
        features[size - HALO :],
        features[:, :PAD],
        features[:, size - PAD :],
    )
    edges = [
        jnp.stack(both) for both in zip(own_edges, edge_strips(mirror_frame, size))
    ]
    halos = halo_pieces(*edges)

    whole = pl.BlockSpec(memory_space=pltpu.VMEM)
    double = lambda v: jnp.concatenate([v, v]).reshape(1, 2 * channels)
    half = lambda v: (v * 0.5).astype(v.dtype)
    mix_near = twice(half(mixer_first))
    ext = pltpu.VMEM((rows, 2 * LEAD + size, channels), BF16)
    wide = pltpu.VMEM(
        (rows // (2 * NEAR), 2, NEAR, width, 3 * channels), BF16
    )
    field = (groups, 2, NEAR, width, channels)
    near_flops = 2 * groups * 2 * NEAR * width * 10 * channels * channels
    own_block = pl.pallas_call(
        functools.partial(own_kernel, steps=2),
        out_shape=jax.ShapeDtypeStruct(field, BF16),
        in_specs=[whole] * 9,
        out_specs=whole,
        scratch_shapes=[ext, wide],
        cost_estimate=pl.CostEstimate(
            flops=2 * near_flops, bytes_accessed=8 << 20, transcendentals=0
        ),
        compiler_params=pltpu.CompilerParams(vmem_limit_bytes=GRANT),
        name="own_block",
    )
    own_operands = (
        features,
        *halos,
        paired_taps(kernel_first),
        double(bias_first),
        mix_near,
        shift_first.reshape(1, channels),
    )
    summed = own_block(*own_operands)

    upright = kernel_second.reshape(9 * channels, channels)
    crossed = jnp.swapaxes(kernel_second, 0, 1).reshape(9 * channels, channels)
    far_rows = size // 4
    return pl.pallas_call(
        functools.partial(
            main_kernel, steps=2, far_rows=far_rows
        ),
        out_shape=jax.ShapeDtypeStruct(features.shape, F32),
        in_specs=[whole] * 16,
        out_specs=pl.BlockSpec(memory_space=pl.ANY),
        scratch_shapes=[
            ext,
            wide,
            pltpu.VMEM(field, BF16),
            pltpu.VMEM((size + 2 * FAR, size, 3 * channels), BF16),
            pltpu.VMEM((2, far_rows, size, channels), F32),
            pltpu.SemaphoreType.DMA((2,)),
        ],
        cost_estimate=pl.CostEstimate(
            flops=4 * near_flops, bytes_accessed=16 << 20, transcendentals=0
        ),
        compiler_params=pltpu.CompilerParams(vmem_limit_bytes=GRANT),
        name="main_block",
    )(
        mirror_frame,
        inside,
        direct,
        relayed,
        *halos,
        summed,
        paired_taps(jnp.swapaxes(kernel_first, 0, 1)),
        double(bias_first),
        mix_near,
        jnp.concatenate([upright, crossed], axis=1),
        double(bias_second),
        half(jnp.concatenate([mixer_second, mixer_second], axis=0)),
        shift_second.reshape(1, channels),
    )


def solution(mesh):
    return jax.shard_map(
        compute,
        mesh=mesh,
        in_specs=(P(("groups", "row"), "col", None), P(), P(), P(), P(), P(), P(), P(), P()),
        out_specs=P(("groups", "row"), "col", None),
        check_vma=False,
    )
```

profile of v0, /device:TPU:2, one launch (start us, length us, event | category | flops | bytes accessed | tf_op | source)
XLA Modules:
  0.0 76.9 jit_solution(16185691732508624714)
XLA Ops:
  0.0 1.9 %copy.16 = bf16[64,64,128]{2,0,1:T(8,128)(2,1)S(1)} copy(bf16[64,64,128]{2,1,0:T(8,128)(2,1)} %tile.1) | data formatting | bytes 2097152 | tf_op args[0]
  1.9 0.0 copy-start
  1.9 0.0 copy-start.12
  1.9 0.0 copy-start.11
  1.9 0.0 copy-start.3
  2.0 0.1 slice.92.own
  2.0 1.6 %collective-permute-start.3 = (bf16[52,48,128]{2,1,0:T(8,128)(2,1)S(1)}, bf16[52,48,128]{2,1,0:T(8,128)(2,1)}, u32[]{:S(2)}, u32[]{:S(2)}) collective-permute-start(bf16[52,48,128]{2,1,0:T(8,128)(2,1)S(1)} %slice.92.own), channel_id=1, source_target_pairs={{3,15},{6,10},{9,5},{12,0},{19,31},{22,26},{25,21},{28,16}} | collective-permute-start | bytes 1916936 | tf_op jit(solution)/shard_map/ppermute | solution.py:316
  3.7 4.5 %collective-permute-start.2 = (bf16[52,48,128]{2,1,0:T(8,128)(2,1)S(1)}, bf16[52,48,128]{2,1,0:T(8,128)(2,1)S(1)}, u32[]{:S(2)}, u32[]{:S(2)}) collective-permute-start(bf16[52,48,128]{2,1,0:T(8,128)(2,1)S(1)} %slice.92.own), channel_id=1, source_target_pairs={{1,4},{2,8},{4,1},{7,13},{8,2},{11,14},{13,7},{14,11},{17,20},{18,... | collective-permute-start | bytes 1916936 | tf_op jit(solution)/shard_map/ppermute | solution.py:316
  8.1 0.0 copy-start.5
  8.2 0.0 copy-start.7
  8.2 0.0 copy-start.13
  8.3 3.2 %collective-permute-start = (bf16[1600,128]{1,0:T(8,128)(2,1)S(1)}, bf16[1600,128]{1,0:T(8,128)(2,1)}, u32[]{:S(2)}, u32[]{:S(2)}) collective-permute-start(bf16[1600,128]{1,0:T(8,128)(2,1)S(1)} %pad_maximum_fusion.1), channel_id=1, source_target_pairs={{1,4},{2,8},{4,1},{7,13},{8,2},{11,14},{13,7},{14,11},{3,15},{6,10... | collective-permute-start | bytes 1228808 | tf_op jit(solution)/shard_map/ppermute | solution.py:316
  11.4 0.0 copy-done
  11.4 0.7 slice_bitcast_fusion.6
  12.1 0.0 copy-done.5
  12.1 0.0 copy-done.7
  12.1 0.0 copy-done.12
  12.3 0.1 fusion.5
  12.3 21.0 %collective-permute-done = bf16[1600,128]{1,0:T(8,128)(2,1)} collective-permute-done((bf16[1600,128]{1,0:T(8,128)(2,1)S(1)}, bf16[1600,128]{1,0:T(8,128)(2,1)}, u32[]{:S(2)}, u32[]{:S(2)}) %collective-permute-start) | collective-permute-done | bytes 409632 | tf_op jit(solution)/shard_map/ppermute | solution.py:316
  33.4 1.4 %collective-permute-start.1 = (bf16[1600,128]{1,0:T(8,128)(2,1)}, bf16[1600,128]{1,0:T(8,128)(2,1)}, u32[]{:S(2)}, u32[]{:S(2)}) collective-permute-start(bf16[1600,128]{1,0:T(8,128)(2,1)} %collective-permute-done), channel_id=1, source_target_pairs={{15,12},{10,9},{5,6},{0,3},{31,28},{26,25},{21,22},{16,19}} | collective-permute-start | bytes 1228808 | tf_op jit(solution)/shard_map/ppermute | solution.py:316
  34.8 0.0 copy-start.8
  34.8 1.2 %fusion.4 = bf16[4,384,256]{2,1,0:T(8,128)(2,1)S(1)} fusion(bf16[3,384,128]{2,1,0:T(8,128)(2,1)} %bitcast.52), kind=kLoop, calls=%fused_computation.7 | loop fusion | flops 3145728 | bytes 1081344 | tf_op jit(solution)/shard_map/concatenate | solution.py:41
  36.0 0.0 copy-start.9
  36.0 0.0 collective-permute-done.3
  36.0 0.8 %collective-permute-start.4 = (bf16[52,48,128]{2,1,0:T(8,128)(2,1)}, bf16[52,48,128]{2,1,0:T(8,128)(2,1)S(1)}, u32[]{:S(2)}, u32[]{:S(2)}) collective-permute-start(bf16[52,48,128]{2,1,0:T(8,128)(2,1)} %collective-permute-done.3), channel_id=1, source_target_pairs={{15,12},{10,9},{5,6},{0,3},{31,28},{26,25},{21,22},{16,19}} | collective-permute-start | bytes 1916936 | tf_op jit(solution)/shard_map/ppermute | solution.py:316
  36.9 0.0 collective-permute-done.1
  36.9 1.2 %select_select_fusion.frame = bf16[1600,128]{1,0:T(8,128)(2,1)S(1)} fusion(bf16[1600,128]{1,0:T(8,128)(2,1)} %collective-permute-done.1, bf16[1600,128]{1,0:T(8,128)(2,1)} %collective-permute-done, pred[]{:T(512)S(6)} %eq.7, pred[]{:T(512)S(6)} %eq.6, bf16[416,128]{1,0:T(8,128)(2,1)S(1)} %get-tuple-element.12, bf16[416,128]{1,0:T(8,128)(2,1)S(1)} %get-tuple-element.11, ...), kind=kLoop, calls=%fused_computation.11 | loop fusion | flops 2048000 | bytes 1638402 | tf_op jit(solution)/shard_map/jit(_where)/select_n | solution.py:342
  38.1 0.0 copy-start.14
  38.1 0.0 copy-start.4
  38.2 0.0 copy-done.10
  38.2 1.9 %collective-permute-start.6 = (bf16[2,6,64,128]{3,2,1,0:T(8,128)(2,1)S(1)}, bf16[2,6,64,128]{3,2,1,0:T(8,128)(2,1)S(1)}, u32[]{:S(2)}, u32[]{:S(2)}) collective-permute-start(bf16[2,6,64,128]{3,2,1,0:T(8,128)(2,1)S(1)} %pad_maximum_fusion.5), channel_id=1, source_target_pairs={{4,0},{8,4},{12,8},{5,1},{9,5},{13,9},{6,2},{10,6},{14,10},{7,3},{... | collective-permute-start | bytes 589832 | tf_op jit(solution)/shard_map/ppermute | solution.py:281
  40.2 2.4 %collective-permute-start.5 = (bf16[2,6,64,128]{3,2,1,0:T(8,128)(2,1)S(1)}, bf16[2,6,64,128]{3,2,1,0:T(8,128)(2,1)S(1)}, u32[]{:S(2)}, u32[]{:S(2)}) collective-permute-start(bf16[2,6,64,128]{3,2,1,0:T(8,128)(2,1)S(1)} %pad_maximum_fusion.4), channel_id=1, source_target_pairs={{0,4},{4,8},{8,12},{1,5},{5,9},{9,13},{2,6},{6,10},{10,14},{3,7},{... | collective-permute-start | bytes 589832 | tf_op jit(solution)/shard_map/ppermute | solution.py:280
  42.7 0.6 collective-permute-done.6.below.rows_below
  43.4 0.0 copy-start.1
  43.4 3.8 %collective-permute-done.5.above.rows_above = bf16[2,6,64,128]{3,2,1,0:T(8,128)(2,1)S(1)} collective-permute-done((bf16[2,6,64,128]{3,2,1,0:T(8,128)(2,1)S(1)}, bf16[2,6,64,128]{3,2,1,0:T(8,128)(2,1)S(1)}, u32[]{:S(2)}, u32[]{:S(2)}) %collective-permute-start.5) | collective-permute-done | bytes 196640 | tf_op jit(solution)/shard_map/ppermute | solution.py:280
  47.2 0.1 pad_maximum_fusion.2
  47.3 5.3 %collective-permute-start.7 = (bf16[2,76,8,128]{3,2,1,0:T(8,128)(2,1)S(1)}, bf16[2,76,8,128]{3,2,1,0:T(8,128)(2,1)S(1)}, u32[]{:S(2)}, u32[]{:S(2)}) collective-permute-start(bf16[2,76,8,128]{3,2,1,0:T(8,128)(2,1)S(1)} %pad_maximum_fusion.2), channel_id=1, source_target_pairs={{0,1},{1,2},{2,3},{4,5},{5,6},{6,7},{8,9},{9,10},{10,11},{12,13},{... | collective-permute-start | bytes 933896 | tf_op jit(solution)/shard_map/ppermute | solution.py:280
  52.6 0.1 pad_maximum_fusion.3
  52.6 1.3 %collective-permute-start.8 = (bf16[2,76,8,128]{3,2,1,0:T(8,128)(2,1)S(1)}, bf16[2,76,8,128]{3,2,1,0:T(8,128)(2,1)S(1)}, u32[]{:S(2)}, u32[]{:S(2)}) collective-permute-start(bf16[2,76,8,128]{3,2,1,0:T(8,128)(2,1)S(1)} %pad_maximum_fusion.3), channel_id=1, source_target_pairs={{1,0},{2,1},{3,2},{5,4},{6,5},{7,6},{9,8},{10,9},{11,10},{13,12},{... | collective-permute-start | bytes 933896 | tf_op jit(solution)/shard_map/ppermute | solution.py:281
  53.9 0.0 copy-done.14
  54.0 0.1 pad_maximum_fusion.far_taps
  54.1 2.9 %collective-permute-done.7.left.columns_left = bf16[2,76,8,128]{3,2,1,0:T(8,128)(2,1)S(1)} collective-permute-done((bf16[2,76,8,128]{3,2,1,0:T(8,128)(2,1)S(1)}, bf16[2,76,8,128]{3,2,1,0:T(8,128)(2,1)S(1)}, u32[]{:S(2)}, u32[]{:S(2)}) %collective-permute-start.7) | collective-permute-done | bytes 311328 | tf_op jit(solution)/shard_map/ppermute | solution.py:280
  56.9 4.5 %collective-permute-done.8.right.columns_right = bf16[2,76,8,128]{3,2,1,0:T(8,128)(2,1)S(1)} collective-permute-done((bf16[2,76,8,128]{3,2,1,0:T(8,128)(2,1)S(1)}, bf16[2,76,8,128]{3,2,1,0:T(8,128)(2,1)S(1)}, u32[]{:S(2)}, u32[]{:S(2)}) %collective-permute-start.8) | collective-permute-done | bytes 311328 | tf_op jit(solution)/shard_map/ppermute | solution.py:281
  61.4 4.6 %own_block.1.summed = bf16[18,2,2,80,128]{4,3,2,1,0:T(8,128)(2,1)S(1)} custom-call(bf16[64,64,128]{2,1,0:T(8,128)(2,1)S(1)} %copy-done, bf16[2,6,64,128]{3,2,1,0:T(8,128)(2,1)S(1)} %collective-permute-done.5.above.rows_above, bf16[2,6,64,128]{3,2,1,0:T(8,128)(2,1)S(1)} %collective-permute-done.6.below.rows_below, ...), custom_call_target="tpu_custom_call" | custom-call | flops 3774873600 | bytes 8388608 | tf_op jit(solution)/shard_map/own_block/pallas_call | solution.py:386
  66.0 0.0 collective-permute-done.2.direct
  66.0 0.0 collective-permute-done.4.relayed
  66.0 0.0 copy-done.2
  66.0 10.9 %main_block.1 = f32[64,64,128]{2,1,0:T(8,128)} custom-call(bf16[1600,128]{1,0:T(8,128)(2,1)S(1)} %select_select_fusion.frame, bf16[52,48,128]{2,1,0:T(8,128)(2,1)S(1)} %slice.92.own, bf16[52,48,128]{2,1,0:T(8,128)(2,1)S(1)} %collective-permute-done.2.direct, bf16[52,48,128]{2,1,0:T(8,128)(2,1)S(1)} %collective-permute-done.4.relayed, ...), custom_call_target="tpu_custom_call" | custom-call | flops 7549747200 | bytes 16777216 | tf_op jit(solution)/shard_map/main_block/pallas_call | solution.py:391
  (32 shorter events, 0.4 us)
Async XLA Ops:
  1.9 9.5 %copy-start = (bf16[64,64,128]{2,1,0:T(8,128)(2,1)S(1)}, bf16[64,64,128]{2,1,0:T(8,128)(2,1)}, u32[]{:S(2)}) copy-start(bf16[64,64,128]{2,1,0:T(8,128)(2,1)} %tile.1) | copy-start | bytes 3145732
  1.9 10.2 %copy-start.12 = (bf16[128,128]{1,0:T(8,128)(2,1)S(1)}, bf16[128,128]{1,0:T(8,128)(2,1)}, u32[]{:S(2)}) copy-start(bf16[128,128]{1,0:T(8,128)(2,1)} %param.12) | copy-start | bytes 98308
  1.9 10.3 %copy-start.11 = (bf16[128,128]{1,0:T(8,128)(2,1)S(1)}, bf16[128,128]{1,0:T(8,128)(2,1)}, u32[]{:S(2)}) copy-start(bf16[128,128]{1,0:T(8,128)(2,1)} %param.16) | copy-start | bytes 98308
  1.9 10.3 %copy-start.3 = (bf16[3,3,128,128]{3,2,1,0:T(8,128)(2,1)S(1)}, bf16[3,3,128,128]{3,2,1,0:T(8,128)(2,1)}, u32[]{:S(2)}) copy-start(bf16[3,3,128,128]{3,2,1,0:T(8,128)(2,1)} %param.10) | copy-start | bytes 884740
  2.0 34.0 %collective-permute-start.3 = (bf16[52,48,128]{2,1,0:T(8,128)(2,1)S(1)}, bf16[52,48,128]{2,1,0:T(8,128)(2,1)}, u32[]{:S(2)}, u32[]{:S(2)}) collective-permute-start(bf16[52,48,128]{2,1,0:T(8,128)(2,1)S(1)} %slice.92.own), channel_id=1, source_target_pairs={{3,15},{6,10},{9,5},{12,0},{19,31},{22,26},{25,21},{28,16}} | collective-permute-start | bytes 1916936 | tf_op jit(solution)/shard_map/ppermute | solution.py:316
  3.7 62.3 %collective-permute-start.2 = (bf16[52,48,128]{2,1,0:T(8,128)(2,1)S(1)}, bf16[52,48,128]{2,1,0:T(8,128)(2,1)S(1)}, u32[]{:S(2)}, u32[]{:S(2)}) collective-permute-start(bf16[52,48,128]{2,1,0:T(8,128)(2,1)S(1)} %slice.92.own), channel_id=1, source_target_pairs={{1,4},{2,8},{4,1},{7,13},{8,2},{11,14},{13,7},{14,11},{17,20},{18,... | collective-permute-start | bytes 1916936 | tf_op jit(solution)/shard_map/ppermute | solution.py:316
  8.1 4.0 %copy-start.5 = (bf16[6,64,128]{2,1,0:T(8,128)(2,1)}, bf16[6,64,128]{2,1,0:T(8,128)(2,1)S(1)}, u32[]{:S(2)}) copy-start(bf16[6,64,128]{2,1,0:T(8,128)(2,1)S(1)} %get-tuple-element.9) | copy-start | bytes 294916
  8.2 4.0 %copy-start.7 = (bf16[6,64,128]{2,1,0:T(8,128)(2,1)}, bf16[6,64,128]{2,1,0:T(8,128)(2,1)S(1)}, u32[]{:S(2)}) copy-start(bf16[6,64,128]{2,1,0:T(8,128)(2,1)S(1)} %get-tuple-element.10) | copy-start | bytes 294916
  8.2 26.6 %copy-start.13 = (f32[128]{0:T(128)S(1)}, f32[128]{0:T(128)}, u32[]{:S(2)}) copy-start(f32[128]{0:T(128)} %param.11) | copy-start | bytes 1540
  8.3 25.1 %collective-permute-start = (bf16[1600,128]{1,0:T(8,128)(2,1)S(1)}, bf16[1600,128]{1,0:T(8,128)(2,1)}, u32[]{:S(2)}, u32[]{:S(2)}) collective-permute-start(bf16[1600,128]{1,0:T(8,128)(2,1)S(1)} %pad_maximum_fusion.1), channel_id=1, source_target_pairs={{1,4},{2,8},{4,1},{7,13},{8,2},{11,14},{13,7},{14,11},{3,15},{6,10... | collective-permute-start | bytes 1228808 | tf_op jit(solution)/shard_map/ppermute | solution.py:316
  33.4 3.5 %collective-permute-start.1 = (bf16[1600,128]{1,0:T(8,128)(2,1)}, bf16[1600,128]{1,0:T(8,128)(2,1)}, u32[]{:S(2)}, u32[]{:S(2)}) collective-permute-start(bf16[1600,128]{1,0:T(8,128)(2,1)} %collective-permute-done), channel_id=1, source_target_pairs={{15,12},{10,9},{5,6},{0,3},{31,28},{26,25},{21,22},{16,19}} | collective-permute-start | bytes 1228808 | tf_op jit(solution)/shard_map/ppermute | solution.py:316
  34.8 2.1 %copy-start.6 = (bf16[6,64,128]{2,1,0:T(8,128)(2,1)S(1)}, bf16[6,64,128]{2,1,0:T(8,128)(2,1)}, u32[]{:S(2)}) copy-start(bf16[6,64,128]{2,1,0:T(8,128)(2,1)} %copy-done.5) | copy-start | bytes 294916
  34.8 2.1 %copy-start.8 = (bf16[6,64,128]{2,1,0:T(8,128)(2,1)S(1)}, bf16[6,64,128]{2,1,0:T(8,128)(2,1)}, u32[]{:S(2)}) copy-start(bf16[6,64,128]{2,1,0:T(8,128)(2,1)} %copy-done.7) | copy-start | bytes 294916
  36.0 2.2 %copy-start.10 = (bf16[1,6,64,128]{3,2,1,0:T(8,128)(2,1)S(1)}, bf16[1,6,64,128]{3,2,1,0:T(8,128)(2,1)}, u32[]{:S(2)}) copy-start(bf16[1,6,64,128]{3,2,1,0:T(8,128)(2,1)} %get-tuple-element.7) | copy-start | bytes 294916
  36.0 4.1 %copy-start.9 = (bf16[1,6,64,128]{3,2,1,0:T(8,128)(2,1)S(1)}, bf16[1,6,64,128]{3,2,1,0:T(8,128)(2,1)}, u32[]{:S(2)}) copy-start(bf16[1,6,64,128]{3,2,1,0:T(8,128)(2,1)} %get-tuple-element.8) | copy-start | bytes 294916
  36.0 30.0 %collective-permute-start.4 = (bf16[52,48,128]{2,1,0:T(8,128)(2,1)}, bf16[52,48,128]{2,1,0:T(8,128)(2,1)S(1)}, u32[]{:S(2)}, u32[]{:S(2)}) collective-permute-start(bf16[52,48,128]{2,1,0:T(8,128)(2,1)} %collective-permute-done.3), channel_id=1, source_target_pairs={{15,12},{10,9},{5,6},{0,3},{31,28},{26,25},{21,22},{16,19}} | collective-permute-start | bytes 1916936 | tf_op jit(solution)/shard_map/ppermute | solution.py:316
  38.1 15.8 %copy-start.14 = (f32[128]{0:T(128)S(1)}, f32[128]{0:T(128)}, u32[]{:S(2)}) copy-start(f32[128]{0:T(128)} %param.15) | copy-start | bytes 1540
  38.1 15.8 %copy-start.4 = (bf16[3,3,128,128]{3,2,1,0:T(8,128)(2,1)S(1)}, bf16[3,3,128,128]{3,2,1,0:T(8,128)(2,1)}, u32[]{:S(2)}) copy-start(bf16[3,3,128,128]{3,2,1,0:T(8,128)(2,1)} %param.14) | copy-start | bytes 884740
  38.2 5.1 %collective-permute-start.6 = (bf16[2,6,64,128]{3,2,1,0:T(8,128)(2,1)S(1)}, bf16[2,6,64,128]{3,2,1,0:T(8,128)(2,1)S(1)}, u32[]{:S(2)}, u32[]{:S(2)}) collective-permute-start(bf16[2,6,64,128]{3,2,1,0:T(8,128)(2,1)S(1)} %pad_maximum_fusion.5), channel_id=1, source_target_pairs={{4,0},{8,4},{12,8},{5,1},{9,5},{13,9},{6,2},{10,6},{14,10},{7,3},{... | collective-permute-start | bytes 589832 | tf_op jit(solution)/shard_map/ppermute | solution.py:281
  40.2 7.0 %collective-permute-start.5 = (bf16[2,6,64,128]{3,2,1,0:T(8,128)(2,1)S(1)}, bf16[2,6,64,128]{3,2,1,0:T(8,128)(2,1)S(1)}, u32[]{:S(2)}, u32[]{:S(2)}) collective-permute-start(bf16[2,6,64,128]{3,2,1,0:T(8,128)(2,1)S(1)} %pad_maximum_fusion.4), channel_id=1, source_target_pairs={{0,4},{4,8},{8,12},{1,5},{5,9},{9,13},{2,6},{6,10},{10,14},{3,7},{... | collective-permute-start | bytes 589832 | tf_op jit(solution)/shard_map/ppermute | solution.py:280
  43.4 18.1 %copy-start.1 = (f32[128]{0:T(128)S(1)}, f32[128]{0:T(128)}, u32[]{:S(2)}) copy-start(f32[128]{0:T(128)} %param.13) | copy-start | bytes 1540
  47.3 9.7 %collective-permute-start.7 = (bf16[2,76,8,128]{3,2,1,0:T(8,128)(2,1)S(1)}, bf16[2,76,8,128]{3,2,1,0:T(8,128)(2,1)S(1)}, u32[]{:S(2)}, u32[]{:S(2)}) collective-permute-start(bf16[2,76,8,128]{3,2,1,0:T(8,128)(2,1)S(1)} %pad_maximum_fusion.2), channel_id=1, source_target_pairs={{0,1},{1,2},{2,3},{4,5},{5,6},{6,7},{8,9},{9,10},{10,11},{12,13},{... | collective-permute-start | bytes 933896 | tf_op jit(solution)/shard_map/ppermute | solution.py:280
  52.6 8.8 %collective-permute-start.8 = (bf16[2,76,8,128]{3,2,1,0:T(8,128)(2,1)S(1)}, bf16[2,76,8,128]{3,2,1,0:T(8,128)(2,1)S(1)}, u32[]{:S(2)}, u32[]{:S(2)}) collective-permute-start(bf16[2,76,8,128]{3,2,1,0:T(8,128)(2,1)S(1)} %pad_maximum_fusion.3), channel_id=1, source_target_pairs={{1,0},{2,1},{3,2},{5,4},{6,5},{7,6},{9,8},{10,9},{11,10},{13,12},{... | collective-permute-start | bytes 933896 | tf_op jit(solution)/shard_map/ppermute | solution.py:281
  61.4 4.6 %copy-start.2 = (f32[128]{0:T(128)S(1)}, f32[128]{0:T(128)}, u32[]{:S(2)}) copy-start(f32[128]{0:T(128)} %param.17) | copy-start | bytes 1540
where the time goes:
time: 77.3 us; the launch traced here: 76.9 us
  waiting for transfers between devices  32.9 us (43%)
  starting transfers between devices  22.4 us (29%)
  Pallas kernels  15.5 us (20%)
  local copies, waits for them, and re-layouts  2.93 us (4%)
  other arithmetic  2.73 us (4%)
    ppermute x5, waiting for transfers between devices, send(): return lax.ppermute(value, pair, route)  21 us
    ppermute x5, starting transfers between devices, send(): return lax.ppermute(value, pair, route)  11.5 us
    pallas_call x1, Pallas kernels, compute(): pl.pallas_call(functools.partial(main_kernel, steps=2, far_rows=far_rows)...  10.9 us
    ppermute x2, starting transfers between devices, exchange(): lax.ppermute(strips_high, axis, [(i, i + 1) for i in range(count - 1)])  7.68 us
    ppermute x2, waiting for transfers between devices, exchange(): lax.ppermute(strips_high, axis, [(i, i + 1) for i in range(count - 1)])  6.72 us
    ppermute x2, waiting for transfers between devices, exchange(): lax.ppermute(strips_low, axis, [(i + 1, i) for i in range(count - 1)])  5.12 us
    pallas_call x1, Pallas kernels, compute(): summed = own_block(*own_operands)  4.58 us
    ppermute x2, starting transfers between devices, exchange(): lax.ppermute(strips_low, axis, [(i + 1, i) for i in range(count - 1)])  3.21 us
  transfers between devices with their start and end apart: 9, of which 5 were waited for; matrix products, arithmetic and copies ran while one was open for 5% of the time, Pallas kernels for 6%

commit v1 on v0

--- a/solution.py
+++ b/solution.py
@@ -98,7 +98,7 @@
 ):
     size, channels = tile.shape[0], tile.shape[2]
     width = size + 2 * PAD
-    fill_edges(ext, *(edge.at[0] for edge in (above, below, left, right)), size)
+    fill_edges(ext, above, below, left, right, size)
     ext[HALO : HALO + size, LEAD : LEAD + size, :] = tile[...]
     widen(ext, wide, width, LEAD - PAD, channels)
     groups = out.shape[0] // steps
@@ -172,7 +172,7 @@
     plain = jnp.logical_not(jnp.logical_or(diagonal, anti))
 
     edges = (rows_above, rows_below, columns_left, columns_right)
-    fill_edges(ext, *(edge.at[1] for edge in edges), size)
+    fill_edges(ext, *edges, size)
     for source, chosen in ((own, diagonal), (direct, plain), (relayed, anti)):
 
         @pl.when(chosen)
@@ -283,11 +283,11 @@
 
 
 def halo_pieces(top, low, left, right):
-    size = top.shape[2]
+    size = top.shape[1]
     above, below = exchange(top, low, "row")
-    start = jnp.concatenate([above[:, :, :PAD], left, below[:, :, :PAD]], axis=1)
+    start = jnp.concatenate([above[:, :PAD], left, below[:, :PAD]], axis=0)
     end = jnp.concatenate(
-        [above[:, :, size - PAD :], right, below[:, :, size - PAD :]], axis=1
+        [above[:, size - PAD :], right, below[:, size - PAD :]], axis=0
     )
     before, after = exchange(start, end, "col")
     return above, below, before, after
@@ -342,16 +342,13 @@
     mirror_frame = jnp.where(
         diagonal, frame, jnp.where(anti, relayed_frame, direct_frame)
     )
-    own_edges = (
+    own_halos = halo_pieces(
         features[:HALO],
         features[size - HALO :],
         features[:, :PAD],
         features[:, size - PAD :],
     )
-    edges = [
-        jnp.stack(both) for both in zip(own_edges, edge_strips(mirror_frame, size))
-    ]
-    halos = halo_pieces(*edges)
+    halos = halo_pieces(*edge_strips(mirror_frame, size))
 
     whole = pl.BlockSpec(memory_space=pltpu.VMEM)
     double = lambda v: jnp.concatenate([v, v]).reshape(1, 2 * channels)
@@ -377,7 +374,7 @@
     )
     own_operands = (
         features,
-        *halos,
+        *own_halos,
         paired_taps(kernel_first),
         double(bias_first),
         mix_near,

time: 77.3 us -> 77.1 us (level)
  the two profiles are of different devices: /device:TPU:2 before, /device:TPU:0 now
where the time goes in v1:
time: 77.1 us; the launch traced here: 76.4 us
  starting transfers between devices  39.1 us (51%)
  Pallas kernels  17.4 us (23%)
  waiting for transfers between devices  7.25 us (9%)
  local copies, waits for them, and re-layouts  6.53 us (8%)
  other arithmetic  5.6 us (7%)
    ppermute x4, starting transfers between devices, exchange(): lax.ppermute(strips_high, axis, [(i, i + 1) for i in range(count - 1)])  19 us
    ppermute x5, starting transfers between devices, send(): return lax.ppermute(value, pair, route)  15 us
    pallas_call x1, Pallas kernels, compute(): pl.pallas_call(functools.partial(main_kernel, steps=2, far_rows=far_rows)...  12 us
    pallas_call x1, Pallas kernels, compute(): summed = own_block(*own_operands)  5.48 us
    ppermute x5, waiting for transfers between devices, send(): return lax.ppermute(value, pair, route)  5.43 us
    ppermute x4, starting transfers between devices, exchange(): lax.ppermute(strips_low, axis, [(i + 1, i) for i in range(count - 1)])  5.16 us
    unnamed x40, local copies, waits for them, and re-layouts  2.54 us
    ppermute x4, waiting for transfers between devices, exchange(): lax.ppermute(strips_low, axis, [(i + 1, i) for i in range(count - 1)])  1.81 us
  transfers between devices with their start and end apart: 13, of which 3 were waited for; matrix products, arithmetic and copies ran while one was open for 13% of the time, Pallas kernels for 7%

profile of v1, /device:TPU:0, one launch (start us, length us, event | category | flops | bytes accessed | tf_op | source)
XLA Modules:
  0.0 76.4 jit_solution(8178052555524519760)
XLA Ops:
  0.0 2.0 %copy.16 = bf16[64,64,128]{2,0,1:T(8,128)(2,1)S(1)} copy(bf16[64,64,128]{2,1,0:T(8,128)(2,1)} %tile.1) | data formatting | bytes 2097152 | tf_op args[0]
  2.0 0.1 slice.108.own
  2.1 0.0 copy-start.15
  2.1 0.0 copy-start.14
  2.1 0.0 copy-start.4
  2.1 1.4 %collective-permute-start.3 = (bf16[52,48,128]{2,1,0:T(8,128)(2,1)S(1)}, bf16[52,48,128]{2,1,0:T(8,128)(2,1)}, u32[]{:S(2)}, u32[]{:S(2)}) collective-permute-start(bf16[52,48,128]{2,1,0:T(8,128)(2,1)S(1)} %slice.108.own), channel_id=1, source_target_pairs={{3,15},{6,10},{9,5},{12,0},{19,31},{22,26},{25,21},{28,16}} | collective-permute-start | bytes 1916936 | tf_op jit(solution)/shard_map/ppermute | solution.py:316
  3.5 1.5 %collective-permute-start.2 = (bf16[52,48,128]{2,1,0:T(8,128)(2,1)S(1)}, bf16[52,48,128]{2,1,0:T(8,128)(2,1)}, u32[]{:S(2)}, u32[]{:S(2)}) collective-permute-start(bf16[52,48,128]{2,1,0:T(8,128)(2,1)S(1)} %slice.108.own), channel_id=1, source_target_pairs={{1,4},{2,8},{4,1},{7,13},{8,2},{11,14},{13,7},{14,11},{17,20},{18,... | collective-permute-start | bytes 1916936 | tf_op jit(solution)/shard_map/ppermute | solution.py:316
  5.0 0.7 fusion.12
  5.7 1.3 %collective-permute-start.10 = (bf16[6,64,128]{2,1,0:T(8,128)(2,1)}, bf16[6,64,128]{2,1,0:T(8,128)(2,1)S(1)}, u32[]{:S(2)}, u32[]{:S(2)}) collective-permute-start(bf16[6,64,128]{2,1,0:T(8,128)(2,1)} %get-tuple-element.7), channel_id=1, source_target_pairs={{4,0},{8,4},{12,8},{5,1},{9,5},{13,9},{6,2},{10,6},{14,10},{7,3},{... | collective-permute-start | bytes 294920 | tf_op jit(solution)/shard_map/ppermute | solution.py:281
  7.0 7.0 %collective-permute-start.9 = (bf16[6,64,128]{2,1,0:T(8,128)(2,1)}, bf16[6,64,128]{2,1,0:T(8,128)(2,1)}, u32[]{:S(2)}, u32[]{:S(2)}) collective-permute-start(bf16[6,64,128]{2,1,0:T(8,128)(2,1)} %get-tuple-element.8), channel_id=1, source_target_pairs={{0,4},{4,8},{8,12},{1,5},{5,9},{9,13},{2,6},{6,10},{10,14},{3,7},{... | collective-permute-start | bytes 294920 | tf_op jit(solution)/shard_map/ppermute | solution.py:280
  14.1 0.8 %pad_maximum_fusion.1 = bf16[1600,128]{1,0:T(8,128)(2,1)} fusion(bf16[416,128]{1,0:T(8,128)(2,1)S(1)} %get-tuple-element.12, bf16[416,128]{1,0:T(8,128)(2,1)S(1)} %get-tuple-element.11, bf16[384,128]{1,0:T(8,128)(2,1)S(1)} %bitcast.49, bf16[384,128]{1,0:T(8,128)(2,1)S(1)} %bitcast.47), kind=kLoop, calls=%fused_computation.10 | loop fusion | flops 1638400 | bytes 819200 | tf_op jit(solution)/shard_map/concatenate | solution.py:320
  14.9 1.3 %collective-permute-start = (bf16[1600,128]{1,0:T(8,128)(2,1)}, bf16[1600,128]{1,0:T(8,128)(2,1)}, u32[]{:S(2)}, u32[]{:S(2)}) collective-permute-start(bf16[1600,128]{1,0:T(8,128)(2,1)} %pad_maximum_fusion.1), channel_id=1, source_target_pairs={{1,4},{2,8},{4,1},{7,13},{8,2},{11,14},{13,7},{14,11},{3,15},{6,10... | collective-permute-start | bytes 1228808 | tf_op jit(solution)/shard_map/ppermute | solution.py:316
  16.2 0.7 fusion.11
  17.1 0.1 fusion.5
  17.1 0.1 fusion.4
  17.2 0.4 copy-done.16
  17.6 0.6 pad_maximum_fusion.4
  18.2 1.7 %copy.14 = bf16[3,3,128,128]{3,2,1,0:T(8,128)(2,1)} copy(bf16[3,3,128,128]{3,2,0,1:T(8,128)(2,1)} %bitcast.43) | data formatting | bytes 589824 | tf_op jit(solution)/shard_map/transpose | solution.py:386
  19.9 1.2 %pad_maximum_fusion.far_taps = bf16[1152,256]{1,0:T(8,128)(2,1)S(1)} fusion(bf16[1152,128]{1,0:T(8,128)(2,1)} %bitcast.45, bf16[1152,128]{1,0:T(8,128)(2,1)} %bitcast.44), kind=kLoop, calls=%fused_computation.9 | loop fusion | flops 1179648 | bytes 1179648 | tf_op jit(solution)/shard_map/concatenate | solution.py:418
  21.1 0.7 pad_maximum_fusion.5
  21.8 2.7 %collective-permute-done = bf16[1600,128]{1,0:T(8,128)(2,1)} collective-permute-done((bf16[1600,128]{1,0:T(8,128)(2,1)}, bf16[1600,128]{1,0:T(8,128)(2,1)}, u32[]{:S(2)}, u32[]{:S(2)}) %collective-permute-start) | collective-permute-done | bytes 409632 | tf_op jit(solution)/shard_map/ppermute | solution.py:316
  24.5 4.2 %collective-permute-start.1 = (bf16[1600,128]{1,0:T(8,128)(2,1)}, bf16[1600,128]{1,0:T(8,128)(2,1)S(1)}, u32[]{:S(2)}, u32[]{:S(2)}) collective-permute-start(bf16[1600,128]{1,0:T(8,128)(2,1)} %collective-permute-done), channel_id=1, source_target_pairs={{15,12},{10,9},{5,6},{0,3},{31,28},{26,25},{21,22},{16,19}} | collective-permute-start | bytes 1228808 | tf_op jit(solution)/shard_map/ppermute | solution.py:316
  28.7 0.0 collective-permute-done.10.below
  28.7 0.0 collective-permute-done.9.above
  28.8 0.7 fusion.15
  29.5 0.9 %pad_maximum_fusion.2 = bf16[76,8,128]{2,1,0:T(8,128)(2,1)S(1)} fusion(bf16[6,8,128]{2,1,0:T(8,128)(2,1)S(1)} %get-tuple-element.20, bf16[64,8,128]{2,1,0:T(8,128)(2,1)} %get-tuple-element.6, bf16[6,8,128]{2,1,0:T(8,128)(2,1)S(1)} %get-tuple-element.18), kind=kLoop, calls=%fused_computation.16 | loop fusion | flops 155648 | bytes 311296 | tf_op jit(solution)/shard_map/concatenate | solution.py:289
  30.4 0.0 copy-start.1
  30.4 1.3 %collective-permute-start.11 = (bf16[76,8,128]{2,1,0:T(8,128)(2,1)S(1)}, bf16[76,8,128]{2,1,0:T(8,128)(2,1)S(1)}, u32[]{:S(2)}, u32[]{:S(2)}) collective-permute-start(bf16[76,8,128]{2,1,0:T(8,128)(2,1)S(1)} %pad_maximum_fusion.2), channel_id=1, source_target_pairs={{0,1},{1,2},{2,3},{4,5},{5,6},{6,7},{8,9},{9,10},{10,11},{12,13},{... | collective-permute-start | bytes 466952 | tf_op jit(solution)/shard_map/ppermute | solution.py:280
  31.7 2.8 %collective-permute-done.1 = bf16[1600,128]{1,0:T(8,128)(2,1)S(1)} collective-permute-done((bf16[1600,128]{1,0:T(8,128)(2,1)}, bf16[1600,128]{1,0:T(8,128)(2,1)S(1)}, u32[]{:S(2)}, u32[]{:S(2)}) %collective-permute-start.1) | collective-permute-done | bytes 409632 | tf_op jit(solution)/shard_map/ppermute | solution.py:316
  34.5 1.2 %select_select_fusion.frame = bf16[1600,128]{1,0:T(8,128)(2,1)S(1)} fusion(bf16[1600,128]{1,0:T(8,128)(2,1)S(1)} %collective-permute-done.1, bf16[1600,128]{1,0:T(8,128)(2,1)} %collective-permute-done, pred[]{:T(512)S(6)} %eq.7, pred[]{:T(512)S(6)} %eq.6, bf16[416,128]{1,0:T(8,128)(2,1)S(1)} %copy-done.8, bf16[416,128]{1,0:T(8,128)(2,1)S(1)} %copy-done.6, ...), kind=kLoop, calls=%fused_computation.11 | loop fusion | flops 2048000 | bytes 1638402 | tf_op jit(solution)/shard_map/jit(_where)/select_n | solution.py:342
  35.7 6.1 %collective-permute-start.5 = (bf16[6,64,128]{2,1,0:T(8,128)(2,1)S(1)}, bf16[6,64,128]{2,1,0:T(8,128)(2,1)S(1)}, u32[]{:S(2)}, u32[]{:S(2)}) collective-permute-start(bf16[6,64,128]{2,1,0:T(8,128)(2,1)S(1)} %bitcast.53), channel_id=1, source_target_pairs={{0,4},{4,8},{8,12},{1,5},{5,9},{9,13},{2,6},{6,10},{10,14},{3,7},{... | collective-permute-start | bytes 294920 | tf_op jit(solution)/shard_map/ppermute | solution.py:280
  41.9 1.3 %collective-permute-start.12 = (bf16[76,8,128]{2,1,0:T(8,128)(2,1)S(1)}, bf16[76,8,128]{2,1,0:T(8,128)(2,1)S(1)}, u32[]{:S(2)}, u32[]{:S(2)}) collective-permute-start(bf16[76,8,128]{2,1,0:T(8,128)(2,1)S(1)} %pad_maximum_fusion.3), channel_id=1, source_target_pairs={{1,0},{2,1},{3,2},{5,4},{6,5},{7,6},{9,8},{10,9},{11,10},{13,12},{... | collective-permute-start | bytes 466952 | tf_op jit(solution)/shard_map/ppermute | solution.py:281
  43.2 0.0 collective-permute-done.3
  43.2 6.5 %collective-permute-start.4 = (bf16[52,48,128]{2,1,0:T(8,128)(2,1)}, bf16[52,48,128]{2,1,0:T(8,128)(2,1)S(1)}, u32[]{:S(2)}, u32[]{:S(2)}) collective-permute-start(bf16[52,48,128]{2,1,0:T(8,128)(2,1)} %collective-permute-done.3), channel_id=1, source_target_pairs={{15,12},{10,9},{5,6},{0,3},{31,28},{26,25},{21,22},{16,19}} | collective-permute-start | bytes 1916936 | tf_op jit(solution)/shard_map/ppermute | solution.py:316
  49.8 0.0 collective-permute-done.5.rows_above
  49.8 1.3 %collective-permute-start.6 = (bf16[6,64,128]{2,1,0:T(8,128)(2,1)S(1)}, bf16[6,64,128]{2,1,0:T(8,128)(2,1)S(1)}, u32[]{:S(2)}, u32[]{:S(2)}) collective-permute-start(bf16[6,64,128]{2,1,0:T(8,128)(2,1)S(1)} %bitcast.51), channel_id=1, source_target_pairs={{4,0},{8,4},{12,8},{5,1},{9,5},{13,9},{6,2},{10,6},{14,10},{7,3},{... | collective-permute-start | bytes 294920 | tf_op jit(solution)/shard_map/ppermute | solution.py:281
  51.2 1.8 %collective-permute-done.6.rows_below = bf16[6,64,128]{2,1,0:T(8,128)(2,1)S(1)} collective-permute-done((bf16[6,64,128]{2,1,0:T(8,128)(2,1)S(1)}, bf16[6,64,128]{2,1,0:T(8,128)(2,1)S(1)}, u32[]{:S(2)}, u32[]{:S(2)}) %collective-permute-start.6) | collective-permute-done | bytes 98336 | tf_op jit(solution)/shard_map/ppermute | solution.py:281
  53.0 1.3 %collective-permute-start.8 = (bf16[76,8,128]{2,1,0:T(8,128)(2,1)S(1)}, bf16[76,8,128]{2,1,0:T(8,128)(2,1)S(1)}, u32[]{:S(2)}, u32[]{:S(2)}) collective-permute-start(bf16[76,8,128]{2,1,0:T(8,128)(2,1)S(1)} %get-tuple-element.21), channel_id=1, source_target_pairs={{1,0},{2,1},{3,2},{5,4},{6,5},{7,6},{9,8},{10,9},{11,10},{13,12},{... | collective-permute-start | bytes 466952 | tf_op jit(solution)/shard_map/ppermute | solution.py:281
  54.3 0.0 collective-permute-done.11.left
  54.3 4.6 %collective-permute-start.7 = (bf16[76,8,128]{2,1,0:T(8,128)(2,1)S(1)}, bf16[76,8,128]{2,1,0:T(8,128)(2,1)S(1)}, u32[]{:S(2)}, u32[]{:S(2)}) collective-permute-start(bf16[76,8,128]{2,1,0:T(8,128)(2,1)S(1)} %get-tuple-element.22), channel_id=1, source_target_pairs={{0,1},{1,2},{2,3},{4,5},{5,6},{6,7},{8,9},{9,10},{10,11},{12,13},{... | collective-permute-start | bytes 466952 | tf_op jit(solution)/shard_map/ppermute | solution.py:280
  58.9 0.0 collective-permute-done.12.right
  58.9 0.0 copy-start.2
  58.9 5.5 %own_block.1.summed = bf16[18,2,2,80,128]{4,3,2,1,0:T(8,128)(2,1)S(1)} custom-call(bf16[64,64,128]{2,1,0:T(8,128)(2,1)S(1)} %copy-done, bf16[6,64,128]{2,1,0:T(8,128)(2,1)} %collective-permute-done.9.above, bf16[6,64,128]{2,1,0:T(8,128)(2,1)S(1)} %collective-permute-done.10.below, bf16[76,8,128]{2,1,0:T(8,128)(2,1)S(1)} %collective-permute-done.11.left, ...), custom_call_target="tpu_custom_call" | custom-call | flops 3774873600 | bytes 8388608 | tf_op jit(solution)/shard_map/own_block/pallas_call | solution.py:383
  64.4 0.0 collective-permute-done.2.direct
  64.4 0.0 collective-permute-done.8.columns_right
  64.4 0.0 collective-permute-done.7.columns_left
  64.4 0.0 collective-permute-done.4.relayed
  64.5 12.0 %main_block.1 = f32[64,64,128]{2,1,0:T(8,128)} custom-call(bf16[1600,128]{1,0:T(8,128)(2,1)S(1)} %select_select_fusion.frame, bf16[52,48,128]{2,1,0:T(8,128)(2,1)S(1)} %slice.108.own, bf16[52,48,128]{2,1,0:T(8,128)(2,1)} %collective-permute-done.2.direct, bf16[52,48,128]{2,1,0:T(8,128)(2,1)S(1)} %collective-permute-done.4.relayed, ...), custom_call_target="tpu_custom_call" | custom-call | flops 7549747200 | bytes 16777216 | tf_op jit(solution)/shard_map/main_block/pallas_call | solution.py:388
  (42 shorter events, 0.3 us)
Async XLA Ops:
  0.0 5.0 %copy-start = (bf16[64,64,128]{2,1,0:T(8,128)(2,1)S(1)}, bf16[64,64,128]{2,1,0:T(8,128)(2,1)}, u32[]{:S(2)}) copy-start(bf16[64,64,128]{2,1,0:T(8,128)(2,1)} %tile.1) | copy-start | bytes 3145732
  2.1 14.9 %copy-start.15 = (bf16[128,128]{1,0:T(8,128)(2,1)S(1)}, bf16[128,128]{1,0:T(8,128)(2,1)}, u32[]{:S(2)}) copy-start(bf16[128,128]{1,0:T(8,128)(2,1)} %param.12) | copy-start | bytes 98308
  2.1 14.9 %copy-start.14 = (bf16[128,128]{1,0:T(8,128)(2,1)S(1)}, bf16[128,128]{1,0:T(8,128)(2,1)}, u32[]{:S(2)}) copy-start(bf16[128,128]{1,0:T(8,128)(2,1)} %param.16) | copy-start | bytes 98308
  2.1 14.9 %copy-start.4 = (bf16[3,3,128,128]{3,2,1,0:T(8,128)(2,1)S(1)}, bf16[3,3,128,128]{3,2,1,0:T(8,128)(2,1)}, u32[]{:S(2)}) copy-start(bf16[3,3,128,128]{3,2,1,0:T(8,128)(2,1)} %param.10) | copy-start | bytes 884740
  2.1 41.1 %collective-permute-start.3 = (bf16[52,48,128]{2,1,0:T(8,128)(2,1)S(1)}, bf16[52,48,128]{2,1,0:T(8,128)(2,1)}, u32[]{:S(2)}, u32[]{:S(2)}) collective-permute-start(bf16[52,48,128]{2,1,0:T(8,128)(2,1)S(1)} %slice.108.own), channel_id=1, source_target_pairs={{3,15},{6,10},{9,5},{12,0},{19,31},{22,26},{25,21},{28,16}} | collective-permute-start | bytes 1916936 | tf_op jit(solution)/shard_map/ppermute | solution.py:316
  3.5 60.9 %collective-permute-start.2 = (bf16[52,48,128]{2,1,0:T(8,128)(2,1)S(1)}, bf16[52,48,128]{2,1,0:T(8,128)(2,1)}, u32[]{:S(2)}, u32[]{:S(2)}) collective-permute-start(bf16[52,48,128]{2,1,0:T(8,128)(2,1)S(1)} %slice.108.own), channel_id=1, source_target_pairs={{1,4},{2,8},{4,1},{7,13},{8,2},{11,14},{13,7},{14,11},{17,20},{18,... | collective-permute-start | bytes 1916936 | tf_op jit(solution)/shard_map/ppermute | solution.py:316
  5.7 23.0 %collective-permute-start.10 = (bf16[6,64,128]{2,1,0:T(8,128)(2,1)}, bf16[6,64,128]{2,1,0:T(8,128)(2,1)S(1)}, u32[]{:S(2)}, u32[]{:S(2)}) collective-permute-start(bf16[6,64,128]{2,1,0:T(8,128)(2,1)} %get-tuple-element.7), channel_id=1, source_target_pairs={{4,0},{8,4},{12,8},{5,1},{9,5},{13,9},{6,2},{10,6},{14,10},{7,3},{... | collective-permute-start | bytes 294920 | tf_op jit(solution)/shard_map/ppermute | solution.py:281
  7.0 21.7 %collective-permute-start.9 = (bf16[6,64,128]{2,1,0:T(8,128)(2,1)}, bf16[6,64,128]{2,1,0:T(8,128)(2,1)}, u32[]{:S(2)}, u32[]{:S(2)}) collective-permute-start(bf16[6,64,128]{2,1,0:T(8,128)(2,1)} %get-tuple-element.8), channel_id=1, source_target_pairs={{0,4},{4,8},{8,12},{1,5},{5,9},{9,13},{2,6},{6,10},{10,14},{3,7},{... | collective-permute-start | bytes 294920 | tf_op jit(solution)/shard_map/ppermute | solution.py:280
  14.0 3.1 %copy-start.9 = (bf16[6,64,128]{2,1,0:T(8,128)(2,1)}, bf16[6,64,128]{2,1,0:T(8,128)(2,1)S(1)}, u32[]{:S(2)}) copy-start(bf16[6,64,128]{2,1,0:T(8,128)(2,1)S(1)} %get-tuple-element.9) | copy-start | bytes 294916
  14.0 3.1 %copy-start.11 = (bf16[6,64,128]{2,1,0:T(8,128)(2,1)}, bf16[6,64,128]{2,1,0:T(8,128)(2,1)S(1)}, u32[]{:S(2)}) copy-start(bf16[6,64,128]{2,1,0:T(8,128)(2,1)S(1)} %get-tuple-element.10) | copy-start | bytes 294916
  14.1 2.9 %copy-start.5 = (bf16[416,128]{1,0:T(8,128)(2,1)}, bf16[416,128]{1,0:T(8,128)(2,1)S(1)}, u32[]{:S(2)}) copy-start(bf16[416,128]{1,0:T(8,128)(2,1)S(1)} %get-tuple-element.11) | copy-start | bytes 319492
  14.1 2.9 %copy-start.7 = (bf16[416,128]{1,0:T(8,128)(2,1)}, bf16[416,128]{1,0:T(8,128)(2,1)S(1)}, u32[]{:S(2)}) copy-start(bf16[416,128]{1,0:T(8,128)(2,1)S(1)} %get-tuple-element.12) | copy-start | bytes 319492
  14.9 9.6 %collective-permute-start = (bf16[1600,128]{1,0:T(8,128)(2,1)}, bf16[1600,128]{1,0:T(8,128)(2,1)}, u32[]{:S(2)}, u32[]{:S(2)}) collective-permute-start(bf16[1600,128]{1,0:T(8,128)(2,1)} %pad_maximum_fusion.1), channel_id=1, source_target_pairs={{1,4},{2,8},{4,1},{7,13},{8,2},{11,14},{13,7},{14,11},{3,15},{6,10... | collective-permute-start | bytes 1228808 | tf_op jit(solution)/shard_map/ppermute | solution.py:316
  16.9 0.7 copy-start.16
  19.9 14.6 %copy-start.6 = (bf16[416,128]{1,0:T(8,128)(2,1)S(1)}, bf16[416,128]{1,0:T(8,128)(2,1)}, u32[]{:S(2)}) copy-start(bf16[416,128]{1,0:T(8,128)(2,1)} %copy-done.5) | copy-start | bytes 319492
  19.9 14.6 %copy-start.8 = (bf16[416,128]{1,0:T(8,128)(2,1)S(1)}, bf16[416,128]{1,0:T(8,128)(2,1)}, u32[]{:S(2)}) copy-start(bf16[416,128]{1,0:T(8,128)(2,1)} %copy-done.7) | copy-start | bytes 319492
  19.9 14.6 %copy-start.10 = (bf16[6,64,128]{2,1,0:T(8,128)(2,1)S(1)}, bf16[6,64,128]{2,1,0:T(8,128)(2,1)}, u32[]{:S(2)}) copy-start(bf16[6,64,128]{2,1,0:T(8,128)(2,1)} %copy-done.9) | copy-start | bytes 294916
  19.9 14.6 %copy-start.12 = (bf16[6,64,128]{2,1,0:T(8,128)(2,1)S(1)}, bf16[6,64,128]{2,1,0:T(8,128)(2,1)}, u32[]{:S(2)}) copy-start(bf16[6,64,128]{2,1,0:T(8,128)(2,1)} %copy-done.11) | copy-start | bytes 294916
  19.9 22.0 %copy-start.13 = (bf16[64,8,128]{2,1,0:T(8,128)(2,1)S(1)}, bf16[64,8,128]{2,1,0:T(8,128)(2,1)}, u32[]{:S(2)}) copy-start(bf16[64,8,128]{2,1,0:T(8,128)(2,1)} %get-tuple-element.5) | copy-start | bytes 393220
  24.5 10.0 %collective-permute-start.1 = (bf16[1600,128]{1,0:T(8,128)(2,1)}, bf16[1600,128]{1,0:T(8,128)(2,1)S(1)}, u32[]{:S(2)}, u32[]{:S(2)}) collective-permute-start(bf16[1600,128]{1,0:T(8,128)(2,1)} %collective-permute-done), channel_id=1, source_target_pairs={{15,12},{10,9},{5,6},{0,3},{31,28},{26,25},{21,22},{16,19}} | collective-permute-start | bytes 1228808 | tf_op jit(solution)/shard_map/ppermute | solution.py:316
  30.4 28.5 %copy-start.1 = (f32[128]{0:T(128)S(1)}, f32[128]{0:T(128)}, u32[]{:S(2)}) copy-start(f32[128]{0:T(128)} %param.13) | copy-start | bytes 1540
  30.4 28.5 %copy-start.3 = (f32[256]{0:T(256)S(1)}, f32[256]{0:T(256)}, u32[]{:S(2)}) copy-start(f32[256]{0:T(256)} %pad_maximum_fusion.4) | copy-start | bytes 3076
  30.4 23.9 %collective-permute-start.11 = (bf16[76,8,128]{2,1,0:T(8,128)(2,1)S(1)}, bf16[76,8,128]{2,1,0:T(8,128)(2,1)S(1)}, u32[]{:S(2)}, u32[]{:S(2)}) collective-permute-start(bf16[76,8,128]{2,1,0:T(8,128)(2,1)S(1)} %pad_maximum_fusion.2), channel_id=1, source_target_pairs={{0,1},{1,2},{2,3},{4,5},{5,6},{6,7},{8,9},{9,10},{10,11},{12,13},{... | collective-permute-start | bytes 466952 | tf_op jit(solution)/shard_map/ppermute | solution.py:280
  35.7 14.1 %collective-permute-start.5 = (bf16[6,64,128]{2,1,0:T(8,128)(2,1)S(1)}, bf16[6,64,128]{2,1,0:T(8,128)(2,1)S(1)}, u32[]{:S(2)}, u32[]{:S(2)}) collective-permute-start(bf16[6,64,128]{2,1,0:T(8,128)(2,1)S(1)} %bitcast.53), channel_id=1, source_target_pairs={{0,4},{4,8},{8,12},{1,5},{5,9},{9,13},{2,6},{6,10},{10,14},{3,7},{... | collective-permute-start | bytes 294920 | tf_op jit(solution)/shard_map/ppermute | solution.py:280
  41.9 17.0 %collective-permute-start.12 = (bf16[76,8,128]{2,1,0:T(8,128)(2,1)S(1)}, bf16[76,8,128]{2,1,0:T(8,128)(2,1)S(1)}, u32[]{:S(2)}, u32[]{:S(2)}) collective-permute-start(bf16[76,8,128]{2,1,0:T(8,128)(2,1)S(1)} %pad_maximum_fusion.3), channel_id=1, source_target_pairs={{1,0},{2,1},{3,2},{5,4},{6,5},{7,6},{9,8},{10,9},{11,10},{13,12},{... | collective-permute-start | bytes 466952 | tf_op jit(solution)/shard_map/ppermute | solution.py:281
  43.2 21.2 %collective-permute-start.4 = (bf16[52,48,128]{2,1,0:T(8,128)(2,1)}, bf16[52,48,128]{2,1,0:T(8,128)(2,1)S(1)}, u32[]{:S(2)}, u32[]{:S(2)}) collective-permute-start(bf16[52,48,128]{2,1,0:T(8,128)(2,1)} %collective-permute-done.3), channel_id=1, source_target_pairs={{15,12},{10,9},{5,6},{0,3},{31,28},{26,25},{21,22},{16,19}} | collective-permute-start | bytes 1916936 | tf_op jit(solution)/shard_map/ppermute | solution.py:316
  49.8 3.2 %collective-permute-start.6 = (bf16[6,64,128]{2,1,0:T(8,128)(2,1)S(1)}, bf16[6,64,128]{2,1,0:T(8,128)(2,1)S(1)}, u32[]{:S(2)}, u32[]{:S(2)}) collective-permute-start(bf16[6,64,128]{2,1,0:T(8,128)(2,1)S(1)} %bitcast.51), channel_id=1, source_target_pairs={{4,0},{8,4},{12,8},{5,1},{9,5},{13,9},{6,2},{10,6},{14,10},{7,3},{... | collective-permute-start | bytes 294920 | tf_op jit(solution)/shard_map/ppermute | solution.py:281
  53.0 11.4 %collective-permute-start.8 = (bf16[76,8,128]{2,1,0:T(8,128)(2,1)S(1)}, bf16[76,8,128]{2,1,0:T(8,128)(2,1)S(1)}, u32[]{:S(2)}, u32[]{:S(2)}) collective-permute-start(bf16[76,8,128]{2,1,0:T(8,128)(2,1)S(1)} %get-tuple-element.21), channel_id=1, source_target_pairs={{1,0},{2,1},{3,2},{5,4},{6,5},{7,6},{9,8},{10,9},{11,10},{13,12},{... | collective-permute-start | bytes 466952 | tf_op jit(solution)/shard_map/ppermute | solution.py:281
  54.3 10.1 %collective-permute-start.7 = (bf16[76,8,128]{2,1,0:T(8,128)(2,1)S(1)}, bf16[76,8,128]{2,1,0:T(8,128)(2,1)S(1)}, u32[]{:S(2)}, u32[]{:S(2)}) collective-permute-start(bf16[76,8,128]{2,1,0:T(8,128)(2,1)S(1)} %get-tuple-element.22), channel_id=1, source_target_pairs={{0,1},{1,2},{2,3},{4,5},{5,6},{6,7},{8,9},{9,10},{10,11},{12,13},{... | collective-permute-start | bytes 466952 | tf_op jit(solution)/shard_map/ppermute | solution.py:280
  58.9 5.5 %copy-start.2 = (f32[128]{0:T(128)S(1)}, f32[128]{0:T(128)}, u32[]{:S(2)}) copy-start(f32[128]{0:T(128)} %param.17) | copy-start | bytes 1540

commit v2 on v1

--- a/solution.py
+++ b/solution.py
@@ -32,35 +32,72 @@
     return straight, hop, onward
 
 
-def paired_taps(kernel):
+def place_pairs(out, kernel, turned):
     channels = kernel.shape[2]
-    flat = kernel.reshape(3, 3 * channels, channels)
-    zero = jnp.zeros((1, 3 * channels, channels), kernel.dtype)
-    near = jnp.concatenate([flat, zero], axis=0)
-    far = jnp.concatenate([zero, flat], axis=0)
-    return jnp.concatenate([near, far], axis=2).reshape(12 * channels, 2 * channels)
-
-
-def twice(matrix):
-    zero = jnp.zeros_like(matrix)
-    return jnp.concatenate(
-        [
-            jnp.concatenate([matrix, zero], axis=1),
-            jnp.concatenate([zero, matrix], axis=1),
-        ],
-        axis=0,
-    )
-
-
-def fill_edges(ext, above, below, left, right, size):
+    for tap in range(4):
+        for half in range(2):
+            for side in range(3):
+                begin = (3 * tap + side) * channels
+                target = out.at[
+                    begin : begin + channels, half * channels : (half + 1) * channels
+                ]
+                down = tap - half
+                if 0 <= down < 3:
+                    place = (side, down) if turned else (down, side)
+                    target[...] = kernel[place]
+                else:
+                    target[...] = jnp.zeros((channels, channels), BF16)
+
+
+def place_both(out, kernel):
+    channels = kernel.shape[2]
+    for down in range(3):
+        for side in range(3):
+            begin = (3 * down + side) * channels
+            out[begin : begin + channels, :channels] = kernel[down, side]
+            out[begin : begin + channels, channels:] = kernel[side, down]
+
+
+def place_twice(out, matrix):
+    channels = matrix.shape[0]
+    value = (matrix[...].astype(F32) * 0.5).astype(BF16)
+    zero = jnp.zeros((channels, channels), BF16)
+    out[:channels, :channels] = value
+    out[channels:, channels:] = value
+    out[:channels, channels:] = zero
+    out[channels:, :channels] = zero
+
+
+def fill_edges(ext, row_near, row_far, col_near, col_far, size):
     rows = size + 2 * HALO
+    tail = LEAD + size + PAD
     ext[:, 0 : LEAD - PAD, :] = jnp.zeros((rows, LEAD - PAD, ext.shape[2]), BF16)
-    tail = LEAD + size + PAD
     ext[:, tail:, :] = jnp.zeros((rows, ext.shape[1] - tail, ext.shape[2]), BF16)
-    ext[0:HALO, LEAD : LEAD + size, :] = above[...]
-    ext[HALO + size :, LEAD : LEAD + size, :] = below[...]
-    ext[:, LEAD - PAD : LEAD, :] = left[...]
-    ext[:, LEAD + size : tail, :] = right[...]
+
+    def place(axis, near, far, low, high):
+        even = lax.rem(lax.axis_index(axis), 2) == 0
+
+        @pl.when(even)
+        def _():
+            low[...] = far[...]
+            high[...] = near[...]
+
+        @pl.when(jnp.logical_not(even))
+        def _():
+            low[...] = near[...]
+            high[...] = far[...]
+
+    within = slice(LEAD, LEAD + size)
+    place(
+        "row", row_near, row_far, ext.at[0:HALO, within], ext.at[HALO + size :, within]
+    )
+    place(
+        "col",
+        col_near,
+        col_far,
+        ext.at[:, LEAD - PAD : LEAD],
+        ext.at[:, LEAD + size : tail],
+    )
 
 
 def near_block(wide, taps, bias, mix, group, groups, width, channels):
@@ -73,7 +110,8 @@
         axis=1,
     )
     total = jnp.dot(part, taps[...], preferred_element_type=F32)
-    active = jnp.maximum(total + bias[...], 0.0).astype(BF16)
+    both = jnp.concatenate([bias[...], bias[...]], axis=1)
+    active = jnp.maximum(total + both, 0.0).astype(BF16)
     return jnp.dot(active, mix[...], preferred_element_type=F32)
 
 
@@ -94,11 +132,36 @@
 
 
 def own_kernel(
-    tile, above, below, left, right, taps, bias, mix, shift, out, ext, wide, *, steps
+    tile,
+    row_near,
+    row_far,
+    col_near,
+    col_far,
+    kernel,
+    bias,
+    mixer,
+    shift,
+    far_kernel,
+    far_mixer,
+    out,
+    mirror_taps,
+    mix,
+    far_taps,
+    far_mix,
+    ext,
+    wide,
+    taps,
+    *,
+    steps,
 ):
+    place_pairs(taps, kernel, False)
+    place_pairs(mirror_taps, kernel, True)
+    place_twice(mix, mixer)
+    place_both(far_taps, far_kernel)
+    place_twice(far_mix, far_mixer)
     size, channels = tile.shape[0], tile.shape[2]
     width = size + 2 * PAD
-    fill_edges(ext, above, below, left, right, size)
+    fill_edges(ext, row_near, row_far, col_near, col_far, size)
     ext[HALO : HALO + size, LEAD : LEAD + size, :] = tile[...]
     widen(ext, wide, width, LEAD - PAD, channels)
     groups = out.shape[0] // steps
@@ -140,10 +203,10 @@
     own,
     direct,
     relayed,
-    rows_above,
-    rows_below,
-    columns_left,
-    columns_right,
+    row_near,
+    row_far,
+    col_near,
+    col_far,
     summed,
     taps,
     bias,
@@ -171,8 +234,7 @@
     anti = jnp.logical_and(row + col == last, row != col)
     plain = jnp.logical_not(jnp.logical_or(diagonal, anti))
 
-    edges = (rows_above, rows_below, columns_left, columns_right)
-    fill_edges(ext, *edges, size)
+    fill_edges(ext, row_near, row_far, col_near, col_far, size)
     for source, chosen in ((own, diagonal), (direct, plain), (relayed, anti)):
 
         @pl.when(chosen)
@@ -248,8 +310,12 @@
             axis=1,
         )
         total = jnp.dot(part, far_taps[...], preferred_element_type=F32)
-        active = jnp.maximum(total + far_bias[...], 0.0).astype(BF16)
+        active = jnp.maximum(total[:, :channels] + far_bias[...], 0.0)
+        active = active + jnp.maximum(total[:, channels:] + far_bias[...], 0.0)
+        active = active.astype(BF16)
+        active = jnp.concatenate([active[: rows // 2], active[rows // 2 :]], axis=1)
         mixed = jnp.dot(active, far_mix[...], preferred_element_type=F32)
+        mixed = jnp.concatenate([mixed[:, :channels], mixed[:, channels:]], axis=0)
         center = far_wide[pl.ds(base + FAR, far_rows), :, channels : 2 * channels]
         center = center.reshape(rows, channels).astype(F32)
         value = jnp.maximum(center + far_shift[...] + mixed, 0.0)
@@ -275,22 +341,29 @@
     return top, low, left, right
 
 
-def exchange(strips_low, strips_high, axis):
+def exchange(low, high, axis):
     count = lax.axis_size(axis)
-    before = lax.ppermute(strips_high, axis, [(i, i + 1) for i in range(count - 1)])
-    after = lax.ppermute(strips_low, axis, [(i + 1, i) for i in range(count - 1)])
-    return before, after
+    even = lax.axis_index(axis) % 2 == 0
+
+    def swap(first, value):
+        pairs = [(i, i + 1) for i in range(first, count - 1, 2)]
+        return lax.ppermute(value, axis, pairs + [(j, i) for i, j in pairs])
+
+    near = swap(0, jnp.where(even, high, low))
+    far = swap(1, jnp.where(even, low, high))
+    return near, far
 
 
 def halo_pieces(top, low, left, right):
     size = top.shape[1]
-    above, below = exchange(top, low, "row")
+    near, far = exchange(top, low, "row")
+    even = lax.axis_index("row") % 2 == 0
+    above, below = jnp.where(even, far, near), jnp.where(even, near, far)
     start = jnp.concatenate([above[:, :PAD], left, below[:, :PAD]], axis=0)
     end = jnp.concatenate(
         [above[:, size - PAD :], right, below[:, size - PAD :]], axis=0
     )
-    before, after = exchange(start, end, "col")
-    return above, below, before, after
+    return (near, far) + exchange(start, end, "col")
 
 
 def compute(
@@ -351,21 +424,24 @@
     halos = halo_pieces(*edge_strips(mirror_frame, size))
 
     whole = pl.BlockSpec(memory_space=pltpu.VMEM)
-    double = lambda v: jnp.concatenate([v, v]).reshape(1, 2 * channels)
-    half = lambda v: (v * 0.5).astype(v.dtype)
-    mix_near = twice(half(mixer_first))
+    line = lambda v: v.reshape(1, channels)
     ext = pltpu.VMEM((rows, 2 * LEAD + size, channels), BF16)
     wide = pltpu.VMEM(
         (rows // (2 * NEAR), 2, NEAR, width, 3 * channels), BF16
     )
     field = (groups, 2, NEAR, width, channels)
+    pairs = (12 * channels, 2 * channels)
+    square = (2 * channels, 2 * channels)
     near_flops = 2 * groups * 2 * NEAR * width * 10 * channels * channels
     own_block = pl.pallas_call(
         functools.partial(own_kernel, steps=2),
-        out_shape=jax.ShapeDtypeStruct(field, BF16),
-        in_specs=[whole] * 9,
-        out_specs=whole,
-        scratch_shapes=[ext, wide],
+        out_shape=[
+            jax.ShapeDtypeStruct(shape, BF16)
+            for shape in (field, pairs, square, (9 * channels, 2 * channels), square)
+        ],
+        in_specs=[whole] * 11,
+        out_specs=[whole] * 5,
+        scratch_shapes=[ext, wide, pltpu.VMEM(pairs, BF16)],
         cost_estimate=pl.CostEstimate(
             flops=2 * near_flops, bytes_accessed=8 << 20, transcendentals=0
         ),
@@ -375,20 +451,18 @@
     own_operands = (
         features,
         *own_halos,
-        paired_taps(kernel_first),
-        double(bias_first),
-        mix_near,
-        shift_first.reshape(1, channels),
-    )
-    summed = own_block(*own_operands)
-
-    upright = kernel_second.reshape(9 * channels, channels)
-    crossed = jnp.swapaxes(kernel_second, 0, 1).reshape(9 * channels, channels)
+        kernel_first,
+        line(bias_first),
+        mixer_first,
+        line(shift_first),
+        kernel_second,
+        mixer_second,
+    )
+    summed, taps, mix, far_taps, far_mix = own_block(*own_operands)
+
     far_rows = size // 4
     return pl.pallas_call(
-        functools.partial(
-            main_kernel, steps=2, far_rows=far_rows
-        ),
+        functools.partial(main_kernel, steps=1, far_rows=far_rows),
         out_shape=jax.ShapeDtypeStruct(features.shape, F32),
         in_specs=[whole] * 16,
         out_specs=pl.BlockSpec(memory_space=pl.ANY),
@@ -412,13 +486,13 @@
         relayed,
         *halos,
         summed,
-        paired_taps(jnp.swapaxes(kernel_first, 0, 1)),
-        double(bias_first),
-        mix_near,
-        jnp.concatenate([upright, crossed], axis=1),
-        double(bias_second),
-        half(jnp.concatenate([mixer_second, mixer_second], axis=0)),
-        shift_second.reshape(1, channels),
+        taps,
+        line(bias_first),
+        mix,
+        far_taps,
+        line(bias_second),
+        far_mix,
+        line(shift_second),
     )
 
 

time: 77.1 us -> 71 us (0.921)
  the two profiles are of different devices: /device:TPU:0 before, /device:TPU:10 now
where the time goes in v2:
time: 71 us; the launch traced here: 70.7 us
  waiting for transfers between devices  29.5 us (42%)
  starting transfers between devices  23.1 us (33%)
  Pallas kernels  14.3 us (20%)
  local copies, waits for them, and re-layouts  2.29 us (3%)
  other arithmetic  1.1 us (2%)
    ppermute x8, waiting for transfers between devices, swap(): return lax.ppermute(value, axis, pairs + [(j, i) for i, j in pairs])  15.9 us
    ppermute x8, starting transfers between devices, swap(): return lax.ppermute(value, axis, pairs + [(j, i) for i, j in pairs])  15 us
    ppermute x5, waiting for transfers between devices, send(): return lax.ppermute(value, pair, route)  13.7 us
    pallas_call x1, Pallas kernels, compute(): pl.pallas_call(functools.partial(main_kernel, steps=1, far_rows=far_rows)...  9.37 us
    ppermute x5, starting transfers between devices, send(): return lax.ppermute(value, pair, route)  8.03 us
    pallas_call x1, Pallas kernels, compute(): summed, taps, mix, far_taps, far_mix = own_block(*own_operands)  4.93 us
    unnamed x23, local copies, waits for them, and re-layouts  2.11 us
  transfers between devices with their start and end apart: 13, of which 4 were waited for; matrix products, arithmetic and copies ran while one was open for 2% of the time, Pallas kernels for 7%

profile of v2, /device:TPU:10, one launch (start us, length us, event | category | flops | bytes accessed | tf_op | source)
XLA Modules:
  0.0 70.7 jit_solution(2710551564298875813)
XLA Ops:
  0.0 2.0 %copy.12 = bf16[64,64,128]{2,0,1:T(8,128)(2,1)S(1)} copy(bf16[64,64,128]{2,1,0:T(8,128)(2,1)} %tile.1) | data formatting | bytes 2097152 | tf_op args[0]
  2.0 0.1 slice.108.own
  2.1 2.7 %collective-permute-start.3 = (bf16[52,48,128]{2,1,0:T(8,128)(2,1)S(1)}, bf16[52,48,128]{2,1,0:T(8,128)(2,1)}, u32[]{:S(2)}, u32[]{:S(2)}) collective-permute-start(bf16[52,48,128]{2,1,0:T(8,128)(2,1)S(1)} %slice.108.own), channel_id=1, source_target_pairs={{3,15},{6,10},{9,5},{12,0},{19,31},{22,26},{25,21},{28,16}} | collective-permute-start | bytes 1916936 | tf_op jit(solution)/shard_map/ppermute | solution.py:389
  4.8 0.7 collective-permute-start.2
  5.5 0.8 %pad_maximum_fusion = bf16[1600,128]{1,0:T(8,128)(2,1)} fusion(bf16[416,128]{1,0:T(8,128)(2,1)S(1)} %get-tuple-element.22, bf16[416,128]{1,0:T(8,128)(2,1)S(1)} %get-tuple-element.21, bf16[384,128]{1,0:T(8,128)(2,1)S(1)} %bitcast.33, bf16[384,128]{1,0:T(8,128)(2,1)S(1)} %bitcast.31), kind=kLoop, calls=%fused_computation.1 | loop fusion | flops 1638400 | bytes 819200 | tf_op jit(solution)/shard_map/concatenate | solution.py:393
  6.3 2.0 %collective-permute-start = (bf16[1600,128]{1,0:T(8,128)(2,1)}, bf16[1600,128]{1,0:T(8,128)(2,1)}, u32[]{:S(2)}, u32[]{:S(2)}) collective-permute-start(bf16[1600,128]{1,0:T(8,128)(2,1)} %pad_maximum_fusion), channel_id=1, source_target_pairs={{1,4},{2,8},{4,1},{7,13},{8,2},{11,14},{13,7},{14,11},{3,15},{6,10... | collective-permute-start | bytes 1228808 | tf_op jit(solution)/shard_map/ppermute | solution.py:389
  8.4 0.0 copy-done
  8.4 1.9 %collective-permute-start.10 = (bf16[6,64,128]{2,1,0:T(8,128)(2,1)S(1)}, bf16[6,64,128]{2,1,0:T(8,128)(2,1)S(1)}, u32[]{:S(2)}, u32[]{:S(2)}) collective-permute-start(bf16[6,64,128]{2,1,0:T(8,128)(2,1)S(1)} %get-tuple-element.17), channel_id=1, source_target_pairs={{4,8},{8,4},{5,9},{9,5},{6,10},{10,6},{7,11},{11,7},{20,24},{24,20... | collective-permute-start | bytes 294920 | tf_op jit(solution)/shard_map/ppermute | solution.py:350
  10.3 1.8 %collective-permute-start.9 = (bf16[6,64,128]{2,1,0:T(8,128)(2,1)S(1)}, bf16[6,64,128]{2,1,0:T(8,128)(2,1)S(1)}, u32[]{:S(2)}, u32[]{:S(2)}) collective-permute-start(bf16[6,64,128]{2,1,0:T(8,128)(2,1)S(1)} %get-tuple-element.18), channel_id=1, source_target_pairs={{0,4},{8,12},{4,0},{12,8},{1,5},{9,13},{5,1},{13,9},{2,6},{10,14},... | collective-permute-start | bytes 294920 | tf_op jit(solution)/shard_map/ppermute | solution.py:350
  12.2 4.2 %collective-permute-done = bf16[1600,128]{1,0:T(8,128)(2,1)} collective-permute-done((bf16[1600,128]{1,0:T(8,128)(2,1)}, bf16[1600,128]{1,0:T(8,128)(2,1)}, u32[]{:S(2)}, u32[]{:S(2)}) %collective-permute-start) | collective-permute-done | bytes 409632 | tf_op jit(solution)/shard_map/ppermute | solution.py:389
  16.4 1.3 %collective-permute-start.1 = (bf16[1600,128]{1,0:T(8,128)(2,1)}, bf16[1600,128]{1,0:T(8,128)(2,1)S(1)}, u32[]{:S(2)}, u32[]{:S(2)}) collective-permute-start(bf16[1600,128]{1,0:T(8,128)(2,1)} %collective-permute-done), channel_id=1, source_target_pairs={{15,12},{10,9},{5,6},{0,3},{31,28},{26,25},{21,22},{16,19}} | collective-permute-start | bytes 1228808 | tf_op jit(solution)/shard_map/ppermute | solution.py:389
  17.6 4.4 %collective-permute-done.10.row_far = bf16[6,64,128]{2,1,0:T(8,128)(2,1)S(1)} collective-permute-done((bf16[6,64,128]{2,1,0:T(8,128)(2,1)S(1)}, bf16[6,64,128]{2,1,0:T(8,128)(2,1)S(1)}, u32[]{:S(2)}, u32[]{:S(2)}) %collective-permute-start.10) | collective-permute-done | bytes 98336 | tf_op jit(solution)/shard_map/ppermute | solution.py:350
  22.1 0.0 collective-permute-done.9.row_near
  22.1 0.0 copy-start.1
  22.1 0.0 copy-start.2
  22.1 0.0 copy-start.3
  22.1 0.0 copy-start.4
  22.2 0.0 copy-start.5
  22.2 0.0 copy-start.6
  22.2 9.5 %collective-permute-done.1 = bf16[1600,128]{1,0:T(8,128)(2,1)S(1)} collective-permute-done((bf16[1600,128]{1,0:T(8,128)(2,1)}, bf16[1600,128]{1,0:T(8,128)(2,1)S(1)}, u32[]{:S(2)}, u32[]{:S(2)}) %collective-permute-start.1) | collective-permute-done | bytes 409632 | tf_op jit(solution)/shard_map/ppermute | solution.py:389
  31.7 0.2 select_select_fusion.frame
  31.9 1.9 %collective-permute-start.6 = (bf16[6,64,128]{2,1,0:T(8,128)(2,1)S(1)}, bf16[6,64,128]{2,1,0:T(8,128)(2,1)S(1)}, u32[]{:S(2)}, u32[]{:S(2)}) collective-permute-start(bf16[6,64,128]{2,1,0:T(8,128)(2,1)S(1)} %get-tuple-element.35), channel_id=1, source_target_pairs={{4,8},{8,4},{5,9},{9,5},{6,10},{10,6},{7,11},{11,7},{20,24},{24,20... | collective-permute-start | bytes 294920 | tf_op jit(solution)/shard_map/ppermute | solution.py:350
  33.8 0.1 collective-permute-start.5
  33.9 2.7 %collective-permute-start.12 = (bf16[76,8,128]{2,1,0:T(8,128)(2,1)S(1)}, bf16[76,8,128]{2,1,0:T(8,128)(2,1)S(1)}, u32[]{:S(2)}, u32[]{:S(2)}) collective-permute-start(bf16[76,8,128]{2,1,0:T(8,128)(2,1)S(1)} %get-tuple-element.27), channel_id=1, source_target_pairs={{1,2},{2,1},{5,6},{6,5},{9,10},{10,9},{13,14},{14,13},{17,18},{18,... | collective-permute-start | bytes 466952 | tf_op jit(solution)/shard_map/ppermute | solution.py:350
  36.6 0.0 collective-permute-done.3
  36.6 2.0 %collective-permute-start.11 = (bf16[76,8,128]{2,1,0:T(8,128)(2,1)S(1)}, bf16[76,8,128]{2,1,0:T(8,128)(2,1)S(1)}, u32[]{:S(2)}, u32[]{:S(2)}) collective-permute-start(bf16[76,8,128]{2,1,0:T(8,128)(2,1)S(1)} %get-tuple-element.28), channel_id=1, source_target_pairs={{0,1},{2,3},{1,0},{3,2},{4,5},{6,7},{5,4},{7,6},{8,9},{10,11},{9,8... | collective-permute-start | bytes 466952 | tf_op jit(solution)/shard_map/ppermute | solution.py:350
  38.6 0.0 collective-permute-done.6.row_far
  38.6 1.3 %collective-permute-start.4 = (bf16[52,48,128]{2,1,0:T(8,128)(2,1)}, bf16[52,48,128]{2,1,0:T(8,128)(2,1)S(1)}, u32[]{:S(2)}, u32[]{:S(2)}) collective-permute-start(bf16[52,48,128]{2,1,0:T(8,128)(2,1)} %collective-permute-done.3), channel_id=1, source_target_pairs={{15,12},{10,9},{5,6},{0,3},{31,28},{26,25},{21,22},{16,19}} | collective-permute-start | bytes 1916936 | tf_op jit(solution)/shard_map/ppermute | solution.py:389
  39.9 0.0 collective-permute-done.5.row_near
  40.1 4.6 %collective-permute-start.8 = (bf16[76,8,128]{2,1,0:T(8,128)(2,1)S(1)}, bf16[76,8,128]{2,1,0:T(8,128)(2,1)S(1)}, u32[]{:S(2)}, u32[]{:S(2)}) collective-permute-start(bf16[76,8,128]{2,1,0:T(8,128)(2,1)S(1)} %get-tuple-element.29), channel_id=1, source_target_pairs={{1,2},{2,1},{5,6},{6,5},{9,10},{10,9},{13,14},{14,13},{17,18},{18,... | collective-permute-start | bytes 466952 | tf_op jit(solution)/shard_map/ppermute | solution.py:350
  44.7 0.0 collective-permute-done.12.col_far
  44.7 0.1 collective-permute-start.7
  44.8 0.0 collective-permute-done.11.col_near
  44.8 0.0 copy-done.1
  44.8 0.0 copy-done.2
  44.8 0.0 copy-done.3
  44.8 0.0 copy-done.4
  44.9 0.0 copy-done.5
  44.9 0.0 copy-done.6
  44.9 0.0 copy-start.7
  44.9 0.0 copy-start.8
  44.9 4.9 %own_block.1 = (bf16[18,2,2,80,128]{4,3,2,1,0:T(8,128)(2,1)S(1)}, bf16[1536,256]{1,0:T(8,128)(2,1)S(1)}, bf16[256,256]{1,0:T(8,128)(2,1)S(1)}, bf16[1152,256]{1,0:T(8,128)(2,1)S(1)}, bf16[256,256]{1,0:T(8,128)(2,1)S(1)}) custom-call(bf16[64,64,128]{2,1,0:T(8,128)(2,1)S(1)} %copy-done, bf16[6,64,128]{2,1,0:T(8,128)(2,1)S(1)} %collective-permute-done.9.row_near, ...), custom_call_target="tpu_custom_call" | custom-call | flops 3774873600 | bytes 8388608 | tf_op jit(solution)/shard_map/own_block/pallas_call | solution.py:461
  49.8 0.0 collective-permute-done.2.direct
  49.8 11.4 %collective-permute-done.8.col_far = bf16[76,8,128]{2,1,0:T(8,128)(2,1)S(1)} collective-permute-done((bf16[76,8,128]{2,1,0:T(8,128)(2,1)S(1)}, bf16[76,8,128]{2,1,0:T(8,128)(2,1)S(1)}, u32[]{:S(2)}, u32[]{:S(2)}) %collective-permute-start.8) | collective-permute-done | bytes 155680 | tf_op jit(solution)/shard_map/ppermute | solution.py:350
  61.3 0.0 collective-permute-done.7.col_near
  61.3 0.0 collective-permute-done.4.relayed
  61.3 0.0 copy-done.8
  61.3 9.4 %main_block.1 = f32[64,64,128]{2,1,0:T(8,128)} custom-call(bf16[1600,128]{1,0:T(8,128)(2,1)S(1)} %select_select_fusion.frame, bf16[52,48,128]{2,1,0:T(8,128)(2,1)S(1)} %slice.108.own, bf16[52,48,128]{2,1,0:T(8,128)(2,1)S(1)} %collective-permute-done.2.direct, bf16[52,48,128]{2,1,0:T(8,128)(2,1)S(1)} %collective-permute-done.4.relayed, ...), custom_call_target="tpu_custom_call" | custom-call | flops 7549747200 | bytes 16777216 | tf_op jit(solution)/shard_map/main_block/pallas_call | solution.py:464
  (18 shorter events, 0.3 us)
Async XLA Ops:
  0.0 8.4 %copy-start = (bf16[64,64,128]{2,1,0:T(8,128)(2,1)S(1)}, bf16[64,64,128]{2,1,0:T(8,128)(2,1)}, u32[]{:S(2)}) copy-start(bf16[64,64,128]{2,1,0:T(8,128)(2,1)} %tile.1) | copy-start | bytes 3145732
  2.1 34.5 %collective-permute-start.3 = (bf16[52,48,128]{2,1,0:T(8,128)(2,1)S(1)}, bf16[52,48,128]{2,1,0:T(8,128)(2,1)}, u32[]{:S(2)}, u32[]{:S(2)}) collective-permute-start(bf16[52,48,128]{2,1,0:T(8,128)(2,1)S(1)} %slice.108.own), channel_id=1, source_target_pairs={{3,15},{6,10},{9,5},{12,0},{19,31},{22,26},{25,21},{28,16}} | collective-permute-start | bytes 1916936 | tf_op jit(solution)/shard_map/ppermute | solution.py:389
  4.8 45.0 %collective-permute-start.2 = (bf16[52,48,128]{2,1,0:T(8,128)(2,1)S(1)}, bf16[52,48,128]{2,1,0:T(8,128)(2,1)S(1)}, u32[]{:S(2)}, u32[]{:S(2)}) collective-permute-start(bf16[52,48,128]{2,1,0:T(8,128)(2,1)S(1)} %slice.108.own), channel_id=1, source_target_pairs={{1,4},{2,8},{4,1},{7,13},{8,2},{11,14},{13,7},{14,11},{17,20},{18,... | collective-permute-start | bytes 1916936 | tf_op jit(solution)/shard_map/ppermute | solution.py:389
  6.3 10.0 %collective-permute-start = (bf16[1600,128]{1,0:T(8,128)(2,1)}, bf16[1600,128]{1,0:T(8,128)(2,1)}, u32[]{:S(2)}, u32[]{:S(2)}) collective-permute-start(bf16[1600,128]{1,0:T(8,128)(2,1)} %pad_maximum_fusion), channel_id=1, source_target_pairs={{1,4},{2,8},{4,1},{7,13},{8,2},{11,14},{13,7},{14,11},{3,15},{6,10... | collective-permute-start | bytes 1228808 | tf_op jit(solution)/shard_map/ppermute | solution.py:389
  8.4 13.7 %collective-permute-start.10 = (bf16[6,64,128]{2,1,0:T(8,128)(2,1)S(1)}, bf16[6,64,128]{2,1,0:T(8,128)(2,1)S(1)}, u32[]{:S(2)}, u32[]{:S(2)}) collective-permute-start(bf16[6,64,128]{2,1,0:T(8,128)(2,1)S(1)} %get-tuple-element.17), channel_id=1, source_target_pairs={{4,8},{8,4},{5,9},{9,5},{6,10},{10,6},{7,11},{11,7},{20,24},{24,20... | collective-permute-start | bytes 294920 | tf_op jit(solution)/shard_map/ppermute | solution.py:350
  10.3 11.7 %collective-permute-start.9 = (bf16[6,64,128]{2,1,0:T(8,128)(2,1)S(1)}, bf16[6,64,128]{2,1,0:T(8,128)(2,1)S(1)}, u32[]{:S(2)}, u32[]{:S(2)}) collective-permute-start(bf16[6,64,128]{2,1,0:T(8,128)(2,1)S(1)} %get-tuple-element.18), channel_id=1, source_target_pairs={{0,4},{8,12},{4,0},{12,8},{1,5},{9,13},{5,1},{13,9},{2,6},{10,14},... | collective-permute-start | bytes 294920 | tf_op jit(solution)/shard_map/ppermute | solution.py:350
  16.4 15.3 %collective-permute-start.1 = (bf16[1600,128]{1,0:T(8,128)(2,1)}, bf16[1600,128]{1,0:T(8,128)(2,1)S(1)}, u32[]{:S(2)}, u32[]{:S(2)}) collective-permute-start(bf16[1600,128]{1,0:T(8,128)(2,1)} %collective-permute-done), channel_id=1, source_target_pairs={{15,12},{10,9},{5,6},{0,3},{31,28},{26,25},{21,22},{16,19}} | collective-permute-start | bytes 1228808 | tf_op jit(solution)/shard_map/ppermute | solution.py:389
  22.1 22.7 %copy-start.1 = (bf16[3,3,128,128]{3,2,1,0:T(8,128)(2,1)S(1)}, bf16[3,3,128,128]{3,2,1,0:T(8,128)(2,1)}, u32[]{:S(2)}) copy-start(bf16[3,3,128,128]{3,2,1,0:T(8,128)(2,1)} %kernel.1) | copy-start | bytes 884740
  22.1 22.7 %copy-start.2 = (bf16[3,3,128,128]{3,2,1,0:T(8,128)(2,1)S(1)}, bf16[3,3,128,128]{3,2,1,0:T(8,128)(2,1)}, u32[]{:S(2)}) copy-start(bf16[3,3,128,128]{3,2,1,0:T(8,128)(2,1)} %far_kernel.1) | copy-start | bytes 884740
  22.1 22.7 %copy-start.3 = (bf16[128,128]{1,0:T(8,128)(2,1)S(1)}, bf16[128,128]{1,0:T(8,128)(2,1)}, u32[]{:S(2)}) copy-start(bf16[128,128]{1,0:T(8,128)(2,1)} %mixer.1) | copy-start | bytes 98308
  22.1 22.7 %copy-start.4 = (bf16[128,128]{1,0:T(8,128)(2,1)S(1)}, bf16[128,128]{1,0:T(8,128)(2,1)}, u32[]{:S(2)}) copy-start(bf16[128,128]{1,0:T(8,128)(2,1)} %far_mixer.1) | copy-start | bytes 98308
  22.2 22.7 %copy-start.5 = (f32[128]{0:T(128)S(1)}, f32[128]{0:T(128)}, u32[]{:S(2)}) copy-start(f32[128]{0:T(128)} %param.13) | copy-start | bytes 1540
  22.2 22.7 %copy-start.6 = (f32[128]{0:T(128)S(1)}, f32[128]{0:T(128)}, u32[]{:S(2)}) copy-start(f32[128]{0:T(128)} %param.11) | copy-start | bytes 1540
  31.9 6.8 %collective-permute-start.6 = (bf16[6,64,128]{2,1,0:T(8,128)(2,1)S(1)}, bf16[6,64,128]{2,1,0:T(8,128)(2,1)S(1)}, u32[]{:S(2)}, u32[]{:S(2)}) collective-permute-start(bf16[6,64,128]{2,1,0:T(8,128)(2,1)S(1)} %get-tuple-element.35), channel_id=1, source_target_pairs={{4,8},{8,4},{5,9},{9,5},{6,10},{10,6},{7,11},{11,7},{20,24},{24,20... | collective-permute-start | bytes 294920 | tf_op jit(solution)/shard_map/ppermute | solution.py:350
  33.8 6.1 %collective-permute-start.5 = (bf16[6,64,128]{2,1,0:T(8,128)(2,1)S(1)}, bf16[6,64,128]{2,1,0:T(8,128)(2,1)S(1)}, u32[]{:S(2)}, u32[]{:S(2)}) collective-permute-start(bf16[6,64,128]{2,1,0:T(8,128)(2,1)S(1)} %get-tuple-element.36), channel_id=1, source_target_pairs={{0,4},{8,12},{4,0},{12,8},{1,5},{9,13},{5,1},{13,9},{2,6},{10,14},... | collective-permute-start | bytes 294920 | tf_op jit(solution)/shard_map/ppermute | solution.py:350
  33.9 10.8 %collective-permute-start.12 = (bf16[76,8,128]{2,1,0:T(8,128)(2,1)S(1)}, bf16[76,8,128]{2,1,0:T(8,128)(2,1)S(1)}, u32[]{:S(2)}, u32[]{:S(2)}) collective-permute-start(bf16[76,8,128]{2,1,0:T(8,128)(2,1)S(1)} %get-tuple-element.27), channel_id=1, source_target_pairs={{1,2},{2,1},{5,6},{6,5},{9,10},{10,9},{13,14},{14,13},{17,18},{18,... | collective-permute-start | bytes 466952 | tf_op jit(solution)/shard_map/ppermute | solution.py:350
  36.6 8.2 %collective-permute-start.11 = (bf16[76,8,128]{2,1,0:T(8,128)(2,1)S(1)}, bf16[76,8,128]{2,1,0:T(8,128)(2,1)S(1)}, u32[]{:S(2)}, u32[]{:S(2)}) collective-permute-start(bf16[76,8,128]{2,1,0:T(8,128)(2,1)S(1)} %get-tuple-element.28), channel_id=1, source_target_pairs={{0,1},{2,3},{1,0},{3,2},{4,5},{6,7},{5,4},{7,6},{8,9},{10,11},{9,8... | collective-permute-start | bytes 466952 | tf_op jit(solution)/shard_map/ppermute | solution.py:350
  38.6 22.6 %collective-permute-start.4 = (bf16[52,48,128]{2,1,0:T(8,128)(2,1)}, bf16[52,48,128]{2,1,0:T(8,128)(2,1)S(1)}, u32[]{:S(2)}, u32[]{:S(2)}) collective-permute-start(bf16[52,48,128]{2,1,0:T(8,128)(2,1)} %collective-permute-done.3), channel_id=1, source_target_pairs={{15,12},{10,9},{5,6},{0,3},{31,28},{26,25},{21,22},{16,19}} | collective-permute-start | bytes 1916936 | tf_op jit(solution)/shard_map/ppermute | solution.py:389
  40.1 21.1 %collective-permute-start.8 = (bf16[76,8,128]{2,1,0:T(8,128)(2,1)S(1)}, bf16[76,8,128]{2,1,0:T(8,128)(2,1)S(1)}, u32[]{:S(2)}, u32[]{:S(2)}) collective-permute-start(bf16[76,8,128]{2,1,0:T(8,128)(2,1)S(1)} %get-tuple-element.29), channel_id=1, source_target_pairs={{1,2},{2,1},{5,6},{6,5},{9,10},{10,9},{13,14},{14,13},{17,18},{18,... | collective-permute-start | bytes 466952 | tf_op jit(solution)/shard_map/ppermute | solution.py:350
  44.7 16.5 %collective-permute-start.7 = (bf16[76,8,128]{2,1,0:T(8,128)(2,1)S(1)}, bf16[76,8,128]{2,1,0:T(8,128)(2,1)S(1)}, u32[]{:S(2)}, u32[]{:S(2)}) collective-permute-start(bf16[76,8,128]{2,1,0:T(8,128)(2,1)S(1)} %get-tuple-element.30), channel_id=1, source_target_pairs={{0,1},{2,3},{1,0},{3,2},{4,5},{6,7},{5,4},{7,6},{8,9},{10,11},{9,8... | collective-permute-start | bytes 466952 | tf_op jit(solution)/shard_map/ppermute | solution.py:350
  44.9 16.4 %copy-start.7 = (f32[128]{0:T(128)S(1)}, f32[128]{0:T(128)}, u32[]{:S(2)}) copy-start(f32[128]{0:T(128)} %param.15) | copy-start | bytes 1540
  44.9 16.4 %copy-start.8 = (f32[128]{0:T(128)S(1)}, f32[128]{0:T(128)}, u32[]{:S(2)}) copy-start(f32[128]{0:T(128)} %param.17) | copy-start | bytes 1540

commit v3 on v2

--- a/solution.py
+++ b/solution.py
@@ -218,7 +218,6 @@
     out,
     ext,
     wide,
-    first,
     far_wide,
     stage,
     sems,
@@ -242,8 +241,8 @@
             place_mirror(ext, frame, source, size)
 
     widen(ext, wide, width, LEAD - PAD, channels)
-    total_groups = summed.shape[0]
-    groups = total_groups // steps
+    groups = summed.shape[0] // steps
+    far_groups = far_wide.shape[0]
 
     def step(k, carry):
         group = k * groups
@@ -253,7 +252,13 @@
             part = part.reshape(groups, NEAR, width, channels)
             value = center_rows(wide, half, group, groups, channels) * 0.5 + part
             value = value + summed[pl.ds(group, groups), half].astype(F32)
-            first[pl.ds(group, groups), half] = jnp.maximum(value, 0.0).astype(BF16)
+            value = jnp.maximum(value, 0.0).astype(BF16)
+            for tap in range(3):
+                begin = PAD + (tap - 1) * FAR
+                lanes = slice(tap * channels, (tap + 1) * channels)
+                far_wide[pl.ds(group, groups), half, :, :, lanes] = value[
+                    :, :, begin : begin + size, :
+                ]
         return carry
 
     lax.fori_loop(0, steps, step, 0)
@@ -262,29 +267,21 @@
 
     @pl.when(row == 0)
     def _():
-        first[0:edge] = jnp.zeros((edge,) + first.shape[1:], BF16)
+        far_wide[0:edge] = jnp.zeros((edge,) + far_wide.shape[1:], BF16)
 
     @pl.when(row == last)
     def _():
-        first[total_groups - edge :] = jnp.zeros((edge,) + first.shape[1:], BF16)
+        far_wide[far_groups - edge :] = jnp.zeros((edge,) + far_wide.shape[1:], BF16)
+
+    outside = far_wide.shape[:3] + (FAR, channels)
 
     @pl.when(col == 0)
     def _():
-        first[:, :, :, 0:PAD, :] = jnp.zeros(
-            first.shape[:3] + (PAD, channels), BF16
-        )
+        far_wide[:, :, :, 0:FAR, :channels] = jnp.zeros(outside, BF16)
 
     @pl.when(col == last)
     def _():
-        first[:, :, :, PAD + size :, :] = jnp.zeros(
-            first.shape[:3] + (PAD, channels), BF16
-        )
-
-    for tap in range(3):
-        begin = PAD + (tap - 1) * FAR
-        far_wide[:, :, tap * channels : (tap + 1) * channels] = first[
-            :, :, :, begin : begin + size, :
-        ].reshape(size + 2 * FAR, size, channels)
+        far_wide[:, :, :, size - FAR :, 2 * channels :] = jnp.zeros(outside, BF16)
 
     def copy(slot, base):
         return pltpu.make_async_copy(
@@ -295,16 +292,16 @@
 
     def far_step(k, carry):
         slot = lax.rem(k, 2)
-        base = k * far_rows
+        base = k * (far_rows // FAR)
 
         @pl.when(k >= 2)
         def _():
-            copy(slot, base - 2 * far_rows).wait()
+            copy(slot, (k - 2) * far_rows).wait()
 
         rows = far_rows * size
         part = jnp.concatenate(
             [
-                far_wide[pl.ds(base + tap * FAR, far_rows)].reshape(rows, 3 * channels)
+                far_wide[pl.ds(base + tap, far_rows // FAR)].reshape(rows, 3 * channels)
                 for tap in range(3)
             ],
             axis=1,
@@ -316,11 +313,13 @@
         active = jnp.concatenate([active[: rows // 2], active[rows // 2 :]], axis=1)
         mixed = jnp.dot(active, far_mix[...], preferred_element_type=F32)
         mixed = jnp.concatenate([mixed[:, :channels], mixed[:, channels:]], axis=0)
-        center = far_wide[pl.ds(base + FAR, far_rows), :, channels : 2 * channels]
+        center = far_wide[
+            pl.ds(base + 1, far_rows // FAR), :, :, :, channels : 2 * channels
+        ]
         center = center.reshape(rows, channels).astype(F32)
         value = jnp.maximum(center + far_shift[...] + mixed, 0.0)
         stage[slot] = value.reshape(far_rows, size, channels)
-        copy(slot, base).start()
+        copy(slot, k * far_rows).start()
         return carry
 
     lax.fori_loop(0, count, far_step, 0)
@@ -388,21 +387,20 @@
     def send(value, route):
         return lax.ppermute(value, pair, route)
 
-    turned = jnp.swapaxes(features, 0, 1)
-    inner = turned[HALO : size - HALO]
+    turn = lambda part: jnp.swapaxes(part, 0, 1)
     frame = jnp.concatenate(
         [
-            piece.reshape(-1, channels)
+            turn(piece).reshape(-1, channels)
             for piece in (
-                turned[:HALO],
-                turned[size - HALO :],
-                inner[:, :PAD],
-                inner[:, size - PAD :],
+                features[:, :HALO],
+                features[:, size - HALO :],
+                features[:PAD, HALO : size - HALO],
+                features[size - PAD :, HALO : size - HALO],
             )
         ],
         axis=0,
     )
-    inside = inner[:, PAD : size - PAD]
+    inside = turn(features[PAD : size - PAD, HALO : size - HALO])
     direct_frame = send(frame, straight + hop)
     hop_inside = send(inside, hop)
     direct = send(inside, straight)
@@ -434,7 +432,7 @@
     square = (2 * channels, 2 * channels)
     near_flops = 2 * groups * 2 * NEAR * width * 10 * channels * channels
     own_block = pl.pallas_call(
-        functools.partial(own_kernel, steps=2),
+        functools.partial(own_kernel, steps=1),
         out_shape=[
             jax.ShapeDtypeStruct(shape, BF16)
             for shape in (field, pairs, square, (9 * channels, 2 * channels), square)
@@ -460,7 +458,7 @@
     )
     summed, taps, mix, far_taps, far_mix = own_block(*own_operands)
 
-    far_rows = size // 4
+    far_rows = size // 2
     return pl.pallas_call(
         functools.partial(main_kernel, steps=1, far_rows=far_rows),
         out_shape=jax.ShapeDtypeStruct(features.shape, F32),
@@ -469,8 +467,7 @@
         scratch_shapes=[
             ext,
             wide,
-            pltpu.VMEM(field, BF16),
-            pltpu.VMEM((size + 2 * FAR, size, 3 * channels), BF16),
+            pltpu.VMEM((groups, 2, NEAR, size, 3 * channels), BF16),
             pltpu.VMEM((2, far_rows, size, channels), F32),
             pltpu.SemaphoreType.DMA((2,)),
         ],

time: 71 us -> 69.6 us (0.980)
  the two profiles are of different devices: /device:TPU:10 before, /device:TPU:14 now
where the time goes in v3:
time: 69.6 us; the launch traced here: 69.3 us
  waiting for transfers between devices  30.5 us (44%)
  starting transfers between devices  23.1 us (33%)
  Pallas kernels  12.3 us (18%)
  local copies, waits for them, and re-layouts  1.95 us (3%)
  other arithmetic  1.1 us (2%)
    ppermute x8, waiting for transfers between devices, swap(): return lax.ppermute(value, axis, pairs + [(j, i) for i, j in pairs])  17 us
    ppermute x8, starting transfers between devices, swap(): return lax.ppermute(value, axis, pairs + [(j, i) for i, j in pairs])  15 us
    ppermute x5, waiting for transfers between devices, send(): return lax.ppermute(value, pair, route)  13.5 us
    pallas_call x1, Pallas kernels, compute(): pl.pallas_call(functools.partial(main_kernel, steps=1, far_rows=far_rows)...  8.51 us
    ppermute x5, starting transfers between devices, send(): return lax.ppermute(value, pair, route)  8.04 us
    pallas_call x1, Pallas kernels, compute(): summed, taps, mix, far_taps, far_mix = own_block(*own_operands)  3.75 us
    slice x1, local copies, waits for them, and re-layouts, compute(): inside = turn(features[PAD:size - PAD, HALO:size - HALO])  1.48 us
  transfers between devices with their start and end apart: 13, of which 4 were waited for; matrix products, arithmetic and copies ran while one was open for 2% of the time, Pallas kernels for 5%

profile of v3, /device:TPU:14, one launch (start us, length us, event | category | flops | bytes accessed | tf_op | source)
XLA Modules:
  0.0 69.3 jit_solution(12992036398005642281)
XLA Ops:
  0.0 1.5 %slice.79 = bf16[48,52,128]{2,1,0:T(8,128)(2,1)S(1)} slice(bf16[64,64,128]{2,1,0:T(8,128)(2,1)} %tile.1), slice={[8:56], [6:58], [0:128]} | slice | bytes 1277952 | tf_op jit(solution)/shard_map/slice | solution.py:403
  1.5 0.1 copy.19
  1.6 2.7 %collective-permute-start.3 = (bf16[52,48,128]{2,1,0:T(8,128)(2,1)S(1)}, bf16[52,48,128]{2,1,0:T(8,128)(2,1)}, u32[]{:S(2)}, u32[]{:S(2)}) collective-permute-start(bf16[52,48,128]{2,1,0:T(8,128)(2,1)S(1)} %bitcast.31), channel_id=1, source_target_pairs={{3,15},{6,10},{9,5},{12,0},{19,31},{22,26},{25,21},{28,16}} | collective-permute-start | bytes 1916936 | tf_op jit(solution)/shard_map/ppermute | solution.py:388
  4.3 0.7 collective-permute-start.2
  5.0 0.1 slice_bitcast_fusion.3
  5.1 0.1 slice_bitcast_fusion.1
  5.3 0.8 %pad_maximum_fusion = bf16[1600,128]{1,0:T(8,128)(2,1)} fusion(bf16[416,128]{1,0:T(8,128)(2,1)S(1)} %get-tuple-element.49, bf16[416,128]{1,0:T(8,128)(2,1)S(1)} %get-tuple-element.50, bf16[384,128]{1,0:T(8,128)(2,1)S(1)} %bitcast.41, bf16[384,128]{1,0:T(8,128)(2,1)S(1)} %bitcast.39), kind=kLoop, calls=%fused_computation.1 | loop fusion | flops 1638400 | bytes 819200 | tf_op jit(solution)/shard_map/concatenate | solution.py:391
  6.0 2.0 %collective-permute-start = (bf16[1600,128]{1,0:T(8,128)(2,1)}, bf16[1600,128]{1,0:T(8,128)(2,1)}, u32[]{:S(2)}, u32[]{:S(2)}) collective-permute-start(bf16[1600,128]{1,0:T(8,128)(2,1)} %pad_maximum_fusion), channel_id=1, source_target_pairs={{1,4},{2,8},{4,1},{7,13},{8,2},{11,14},{13,7},{14,11},{3,15},{6,10... | collective-permute-start | bytes 1228808 | tf_op jit(solution)/shard_map/ppermute | solution.py:388
  8.1 1.9 %collective-permute-start.10 = (bf16[6,64,128]{2,1,0:T(8,128)(2,1)S(1)}, bf16[6,64,128]{2,1,0:T(8,128)(2,1)S(1)}, u32[]{:S(2)}, u32[]{:S(2)}) collective-permute-start(bf16[6,64,128]{2,1,0:T(8,128)(2,1)S(1)} %get-tuple-element.17), channel_id=1, source_target_pairs={{4,8},{8,4},{5,9},{9,5},{6,10},{10,6},{7,11},{11,7},{20,24},{24,20... | collective-permute-start | bytes 294920 | tf_op jit(solution)/shard_map/ppermute | solution.py:349
  10.0 1.8 %collective-permute-start.9 = (bf16[6,64,128]{2,1,0:T(8,128)(2,1)S(1)}, bf16[6,64,128]{2,1,0:T(8,128)(2,1)S(1)}, u32[]{:S(2)}, u32[]{:S(2)}) collective-permute-start(bf16[6,64,128]{2,1,0:T(8,128)(2,1)S(1)} %get-tuple-element.18), channel_id=1, source_target_pairs={{0,4},{8,12},{4,0},{12,8},{1,5},{9,13},{5,1},{13,9},{2,6},{10,14},... | collective-permute-start | bytes 294920 | tf_op jit(solution)/shard_map/ppermute | solution.py:349
  11.9 4.0 %collective-permute-done = bf16[1600,128]{1,0:T(8,128)(2,1)} collective-permute-done((bf16[1600,128]{1,0:T(8,128)(2,1)}, bf16[1600,128]{1,0:T(8,128)(2,1)}, u32[]{:S(2)}, u32[]{:S(2)}) %collective-permute-start) | collective-permute-done | bytes 409632 | tf_op jit(solution)/shard_map/ppermute | solution.py:388
  15.9 1.3 %collective-permute-start.1 = (bf16[1600,128]{1,0:T(8,128)(2,1)}, bf16[1600,128]{1,0:T(8,128)(2,1)S(1)}, u32[]{:S(2)}, u32[]{:S(2)}) collective-permute-start(bf16[1600,128]{1,0:T(8,128)(2,1)} %collective-permute-done), channel_id=1, source_target_pairs={{15,12},{10,9},{5,6},{0,3},{31,28},{26,25},{21,22},{16,19}} | collective-permute-start | bytes 1228808 | tf_op jit(solution)/shard_map/ppermute | solution.py:388
  17.2 4.4 %collective-permute-done.10.row_far = bf16[6,64,128]{2,1,0:T(8,128)(2,1)S(1)} collective-permute-done((bf16[6,64,128]{2,1,0:T(8,128)(2,1)S(1)}, bf16[6,64,128]{2,1,0:T(8,128)(2,1)S(1)}, u32[]{:S(2)}, u32[]{:S(2)}) %collective-permute-start.10) | collective-permute-done | bytes 98336 | tf_op jit(solution)/shard_map/ppermute | solution.py:349
  21.6 0.0 collective-permute-done.9.row_near
  21.6 0.0 copy-start.1
  21.7 0.0 copy-start.2
  21.7 0.0 copy-start.3
  21.7 0.0 copy-start.4
  21.7 0.0 copy-start.5
  21.7 0.0 copy-start.6
  21.7 9.5 %collective-permute-done.1 = bf16[1600,128]{1,0:T(8,128)(2,1)S(1)} collective-permute-done((bf16[1600,128]{1,0:T(8,128)(2,1)}, bf16[1600,128]{1,0:T(8,128)(2,1)S(1)}, u32[]{:S(2)}, u32[]{:S(2)}) %collective-permute-start.1) | collective-permute-done | bytes 409632 | tf_op jit(solution)/shard_map/ppermute | solution.py:388
  31.2 0.2 select_select_fusion.frame
  31.4 1.9 %collective-permute-start.6 = (bf16[6,64,128]{2,1,0:T(8,128)(2,1)S(1)}, bf16[6,64,128]{2,1,0:T(8,128)(2,1)S(1)}, u32[]{:S(2)}, u32[]{:S(2)}) collective-permute-start(bf16[6,64,128]{2,1,0:T(8,128)(2,1)S(1)} %get-tuple-element.35), channel_id=1, source_target_pairs={{4,8},{8,4},{5,9},{9,5},{6,10},{10,6},{7,11},{11,7},{20,24},{24,20... | collective-permute-start | bytes 294920 | tf_op jit(solution)/shard_map/ppermute | solution.py:349
  33.3 0.1 collective-permute-start.5
  33.5 2.7 %collective-permute-start.12 = (bf16[76,8,128]{2,1,0:T(8,128)(2,1)S(1)}, bf16[76,8,128]{2,1,0:T(8,128)(2,1)S(1)}, u32[]{:S(2)}, u32[]{:S(2)}) collective-permute-start(bf16[76,8,128]{2,1,0:T(8,128)(2,1)S(1)} %get-tuple-element.27), channel_id=1, source_target_pairs={{1,2},{2,1},{5,6},{6,5},{9,10},{10,9},{13,14},{14,13},{17,18},{18,... | collective-permute-start | bytes 466952 | tf_op jit(solution)/shard_map/ppermute | solution.py:349
  36.1 0.0 collective-permute-done.3
  36.1 2.1 %collective-permute-start.11 = (bf16[76,8,128]{2,1,0:T(8,128)(2,1)S(1)}, bf16[76,8,128]{2,1,0:T(8,128)(2,1)S(1)}, u32[]{:S(2)}, u32[]{:S(2)}) collective-permute-start(bf16[76,8,128]{2,1,0:T(8,128)(2,1)S(1)} %get-tuple-element.28), channel_id=1, source_target_pairs={{0,1},{2,3},{1,0},{3,2},{4,5},{6,7},{5,4},{7,6},{8,9},{10,11},{9,8... | collective-permute-start | bytes 466952 | tf_op jit(solution)/shard_map/ppermute | solution.py:349
  38.2 0.0 collective-permute-done.6.row_far
  38.2 1.3 %collective-permute-start.4 = (bf16[52,48,128]{2,1,0:T(8,128)(2,1)}, bf16[52,48,128]{2,1,0:T(8,128)(2,1)S(1)}, u32[]{:S(2)}, u32[]{:S(2)}) collective-permute-start(bf16[52,48,128]{2,1,0:T(8,128)(2,1)} %collective-permute-done.3), channel_id=1, source_target_pairs={{15,12},{10,9},{5,6},{0,3},{31,28},{26,25},{21,22},{16,19}} | collective-permute-start | bytes 1916936 | tf_op jit(solution)/shard_map/ppermute | solution.py:388
  39.5 0.0 collective-permute-done.5.row_near
  39.7 4.6 %collective-permute-start.8 = (bf16[76,8,128]{2,1,0:T(8,128)(2,1)S(1)}, bf16[76,8,128]{2,1,0:T(8,128)(2,1)S(1)}, u32[]{:S(2)}, u32[]{:S(2)}) collective-permute-start(bf16[76,8,128]{2,1,0:T(8,128)(2,1)S(1)} %get-tuple-element.29), channel_id=1, source_target_pairs={{1,2},{2,1},{5,6},{6,5},{9,10},{10,9},{13,14},{14,13},{17,18},{18,... | collective-permute-start | bytes 466952 | tf_op jit(solution)/shard_map/ppermute | solution.py:349
  44.2 0.0 collective-permute-done.12.col_far
  44.3 0.1 collective-permute-start.7
  44.3 0.0 collective-permute-done.11.col_near
  44.3 0.0 copy-done.1
  44.4 0.0 copy-done.2
  44.4 0.0 copy-done.3
  44.4 0.0 copy-done.4
  44.4 0.0 copy-done.5
  44.4 0.0 copy-done.6
  44.4 0.0 copy-start.7
  44.4 0.0 copy-start.8
  44.4 3.8 %own_block.1 = (bf16[18,2,2,80,128]{4,3,2,1,0:T(8,128)(2,1)S(1)}, bf16[1536,256]{1,0:T(8,128)(2,1)S(1)}, bf16[256,256]{1,0:T(8,128)(2,1)S(1)}, bf16[1152,256]{1,0:T(8,128)(2,1)S(1)}, bf16[256,256]{1,0:T(8,128)(2,1)S(1)}) custom-call(bf16[64,64,128]{2,1,0:T(8,128)(2,1)S(1)} %copy-done, bf16[6,64,128]{2,1,0:T(8,128)(2,1)S(1)} %collective-permute-done.9.row_near, ...), custom_call_target="tpu_custom_call" | custom-call | flops 3774873600 | bytes 8388608 | tf_op jit(solution)/shard_map/own_block/pallas_call | solution.py:459
  48.2 0.0 collective-permute-done.2.direct
  48.2 12.6 %collective-permute-done.8.col_far = bf16[76,8,128]{2,1,0:T(8,128)(2,1)S(1)} collective-permute-done((bf16[76,8,128]{2,1,0:T(8,128)(2,1)S(1)}, bf16[76,8,128]{2,1,0:T(8,128)(2,1)S(1)}, u32[]{:S(2)}, u32[]{:S(2)}) %collective-permute-start.8) | collective-permute-done | bytes 155680 | tf_op jit(solution)/shard_map/ppermute | solution.py:349
  60.8 0.0 collective-permute-done.7.col_near
  60.8 0.0 collective-permute-done.4.relayed
  60.8 8.5 %main_block.1 = f32[64,64,128]{2,1,0:T(8,128)} custom-call(bf16[1600,128]{1,0:T(8,128)(2,1)S(1)} %select_select_fusion.frame, bf16[52,48,128]{2,1,0:T(8,128)(2,1)S(1)} %bitcast.33, bf16[52,48,128]{2,1,0:T(8,128)(2,1)S(1)} %collective-permute-done.2.direct, bf16[52,48,128]{2,1,0:T(8,128)(2,1)S(1)} %collective-permute-done.4.relayed, ...), custom_call_target="tpu_custom_call" | custom-call | flops 7549747200 | bytes 16777216 | tf_op jit(solution)/shard_map/main_block/pallas_call | solution.py:462
  (21 shorter events, 0.4 us)
Async XLA Ops:
  0.0 5.0 %copy-start = (bf16[64,64,128]{2,1,0:T(8,128)(2,1)S(1)}, bf16[64,64,128]{2,1,0:T(8,128)(2,1)}, u32[]{:S(2)}) copy-start(bf16[64,64,128]{2,1,0:T(8,128)(2,1)} %tile.1) | copy-start | bytes 3145732
  1.6 34.5 %collective-permute-start.3 = (bf16[52,48,128]{2,1,0:T(8,128)(2,1)S(1)}, bf16[52,48,128]{2,1,0:T(8,128)(2,1)}, u32[]{:S(2)}, u32[]{:S(2)}) collective-permute-start(bf16[52,48,128]{2,1,0:T(8,128)(2,1)S(1)} %bitcast.31), channel_id=1, source_target_pairs={{3,15},{6,10},{9,5},{12,0},{19,31},{22,26},{25,21},{28,16}} | collective-permute-start | bytes 1916936 | tf_op jit(solution)/shard_map/ppermute | solution.py:388
  4.3 43.9 %collective-permute-start.2 = (bf16[52,48,128]{2,1,0:T(8,128)(2,1)S(1)}, bf16[52,48,128]{2,1,0:T(8,128)(2,1)S(1)}, u32[]{:S(2)}, u32[]{:S(2)}) collective-permute-start(bf16[52,48,128]{2,1,0:T(8,128)(2,1)S(1)} %bitcast.32), channel_id=1, source_target_pairs={{1,4},{2,8},{4,1},{7,13},{8,2},{11,14},{13,7},{14,11},{17,20},{18,... | collective-permute-start | bytes 1916936 | tf_op jit(solution)/shard_map/ppermute | solution.py:388
  6.0 9.8 %collective-permute-start = (bf16[1600,128]{1,0:T(8,128)(2,1)}, bf16[1600,128]{1,0:T(8,128)(2,1)}, u32[]{:S(2)}, u32[]{:S(2)}) collective-permute-start(bf16[1600,128]{1,0:T(8,128)(2,1)} %pad_maximum_fusion), channel_id=1, source_target_pairs={{1,4},{2,8},{4,1},{7,13},{8,2},{11,14},{13,7},{14,11},{3,15},{6,10... | collective-permute-start | bytes 1228808 | tf_op jit(solution)/shard_map/ppermute | solution.py:388
  8.1 13.5 %collective-permute-start.10 = (bf16[6,64,128]{2,1,0:T(8,128)(2,1)S(1)}, bf16[6,64,128]{2,1,0:T(8,128)(2,1)S(1)}, u32[]{:S(2)}, u32[]{:S(2)}) collective-permute-start(bf16[6,64,128]{2,1,0:T(8,128)(2,1)S(1)} %get-tuple-element.17), channel_id=1, source_target_pairs={{4,8},{8,4},{5,9},{9,5},{6,10},{10,6},{7,11},{11,7},{20,24},{24,20... | collective-permute-start | bytes 294920 | tf_op jit(solution)/shard_map/ppermute | solution.py:349
  10.0 11.6 %collective-permute-start.9 = (bf16[6,64,128]{2,1,0:T(8,128)(2,1)S(1)}, bf16[6,64,128]{2,1,0:T(8,128)(2,1)S(1)}, u32[]{:S(2)}, u32[]{:S(2)}) collective-permute-start(bf16[6,64,128]{2,1,0:T(8,128)(2,1)S(1)} %get-tuple-element.18), channel_id=1, source_target_pairs={{0,4},{8,12},{4,0},{12,8},{1,5},{9,13},{5,1},{13,9},{2,6},{10,14},... | collective-permute-start | bytes 294920 | tf_op jit(solution)/shard_map/ppermute | solution.py:349
  15.9 15.3 %collective-permute-start.1 = (bf16[1600,128]{1,0:T(8,128)(2,1)}, bf16[1600,128]{1,0:T(8,128)(2,1)S(1)}, u32[]{:S(2)}, u32[]{:S(2)}) collective-permute-start(bf16[1600,128]{1,0:T(8,128)(2,1)} %collective-permute-done), channel_id=1, source_target_pairs={{15,12},{10,9},{5,6},{0,3},{31,28},{26,25},{21,22},{16,19}} | collective-permute-start | bytes 1228808 | tf_op jit(solution)/shard_map/ppermute | solution.py:388
  21.6 22.7 %copy-start.1 = (bf16[3,3,128,128]{3,2,1,0:T(8,128)(2,1)S(1)}, bf16[3,3,128,128]{3,2,1,0:T(8,128)(2,1)}, u32[]{:S(2)}) copy-start(bf16[3,3,128,128]{3,2,1,0:T(8,128)(2,1)} %kernel.1) | copy-start | bytes 884740
  21.7 22.7 %copy-start.2 = (bf16[3,3,128,128]{3,2,1,0:T(8,128)(2,1)S(1)}, bf16[3,3,128,128]{3,2,1,0:T(8,128)(2,1)}, u32[]{:S(2)}) copy-start(bf16[3,3,128,128]{3,2,1,0:T(8,128)(2,1)} %far_kernel.1) | copy-start | bytes 884740
  21.7 22.7 %copy-start.3 = (bf16[128,128]{1,0:T(8,128)(2,1)S(1)}, bf16[128,128]{1,0:T(8,128)(2,1)}, u32[]{:S(2)}) copy-start(bf16[128,128]{1,0:T(8,128)(2,1)} %mixer.1) | copy-start | bytes 98308
  21.7 22.7 %copy-start.4 = (bf16[128,128]{1,0:T(8,128)(2,1)S(1)}, bf16[128,128]{1,0:T(8,128)(2,1)}, u32[]{:S(2)}) copy-start(bf16[128,128]{1,0:T(8,128)(2,1)} %far_mixer.1) | copy-start | bytes 98308
  21.7 22.7 %copy-start.5 = (f32[128]{0:T(128)S(1)}, f32[128]{0:T(128)}, u32[]{:S(2)}) copy-start(f32[128]{0:T(128)} %param.13) | copy-start | bytes 1540
  21.7 22.7 %copy-start.6 = (f32[128]{0:T(128)S(1)}, f32[128]{0:T(128)}, u32[]{:S(2)}) copy-start(f32[128]{0:T(128)} %param.11) | copy-start | bytes 1540
  31.4 6.8 %collective-permute-start.6 = (bf16[6,64,128]{2,1,0:T(8,128)(2,1)S(1)}, bf16[6,64,128]{2,1,0:T(8,128)(2,1)S(1)}, u32[]{:S(2)}, u32[]{:S(2)}) collective-permute-start(bf16[6,64,128]{2,1,0:T(8,128)(2,1)S(1)} %get-tuple-element.35), channel_id=1, source_target_pairs={{4,8},{8,4},{5,9},{9,5},{6,10},{10,6},{7,11},{11,7},{20,24},{24,20... | collective-permute-start | bytes 294920 | tf_op jit(solution)/shard_map/ppermute | solution.py:349
  33.3 6.1 %collective-permute-start.5 = (bf16[6,64,128]{2,1,0:T(8,128)(2,1)S(1)}, bf16[6,64,128]{2,1,0:T(8,128)(2,1)S(1)}, u32[]{:S(2)}, u32[]{:S(2)}) collective-permute-start(bf16[6,64,128]{2,1,0:T(8,128)(2,1)S(1)} %get-tuple-element.36), channel_id=1, source_target_pairs={{0,4},{8,12},{4,0},{12,8},{1,5},{9,13},{5,1},{13,9},{2,6},{10,14},... | collective-permute-start | bytes 294920 | tf_op jit(solution)/shard_map/ppermute | solution.py:349
  33.5 10.8 %collective-permute-start.12 = (bf16[76,8,128]{2,1,0:T(8,128)(2,1)S(1)}, bf16[76,8,128]{2,1,0:T(8,128)(2,1)S(1)}, u32[]{:S(2)}, u32[]{:S(2)}) collective-permute-start(bf16[76,8,128]{2,1,0:T(8,128)(2,1)S(1)} %get-tuple-element.27), channel_id=1, source_target_pairs={{1,2},{2,1},{5,6},{6,5},{9,10},{10,9},{13,14},{14,13},{17,18},{18,... | collective-permute-start | bytes 466952 | tf_op jit(solution)/shard_map/ppermute | solution.py:349
  36.1 8.2 %collective-permute-start.11 = (bf16[76,8,128]{2,1,0:T(8,128)(2,1)S(1)}, bf16[76,8,128]{2,1,0:T(8,128)(2,1)S(1)}, u32[]{:S(2)}, u32[]{:S(2)}) collective-permute-start(bf16[76,8,128]{2,1,0:T(8,128)(2,1)S(1)} %get-tuple-element.28), channel_id=1, source_target_pairs={{0,1},{2,3},{1,0},{3,2},{4,5},{6,7},{5,4},{7,6},{8,9},{10,11},{9,8... | collective-permute-start | bytes 466952 | tf_op jit(solution)/shard_map/ppermute | solution.py:349
  38.2 22.6 %collective-permute-start.4 = (bf16[52,48,128]{2,1,0:T(8,128)(2,1)}, bf16[52,48,128]{2,1,0:T(8,128)(2,1)S(1)}, u32[]{:S(2)}, u32[]{:S(2)}) collective-permute-start(bf16[52,48,128]{2,1,0:T(8,128)(2,1)} %collective-permute-done.3), channel_id=1, source_target_pairs={{15,12},{10,9},{5,6},{0,3},{31,28},{26,25},{21,22},{16,19}} | collective-permute-start | bytes 1916936 | tf_op jit(solution)/shard_map/ppermute | solution.py:388
  39.7 21.1 %collective-permute-start.8 = (bf16[76,8,128]{2,1,0:T(8,128)(2,1)S(1)}, bf16[76,8,128]{2,1,0:T(8,128)(2,1)S(1)}, u32[]{:S(2)}, u32[]{:S(2)}) collective-permute-start(bf16[76,8,128]{2,1,0:T(8,128)(2,1)S(1)} %get-tuple-element.29), channel_id=1, source_target_pairs={{1,2},{2,1},{5,6},{6,5},{9,10},{10,9},{13,14},{14,13},{17,18},{18,... | collective-permute-start | bytes 466952 | tf_op jit(solution)/shard_map/ppermute | solution.py:349
  44.3 16.5 %collective-permute-start.7 = (bf16[76,8,128]{2,1,0:T(8,128)(2,1)S(1)}, bf16[76,8,128]{2,1,0:T(8,128)(2,1)S(1)}, u32[]{:S(2)}, u32[]{:S(2)}) collective-permute-start(bf16[76,8,128]{2,1,0:T(8,128)(2,1)S(1)} %get-tuple-element.30), channel_id=1, source_target_pairs={{0,1},{2,3},{1,0},{3,2},{4,5},{6,7},{5,4},{7,6},{8,9},{10,11},{9,8... | collective-permute-start | bytes 466952 | tf_op jit(solution)/shard_map/ppermute | solution.py:349
  44.4 16.4 %copy-start.7 = (f32[128]{0:T(128)S(1)}, f32[128]{0:T(128)}, u32[]{:S(2)}) copy-start(f32[128]{0:T(128)} %param.15) | copy-start | bytes 1540
  44.4 16.4 %copy-start.8 = (f32[128]{0:T(128)S(1)}, f32[128]{0:T(128)}, u32[]{:S(2)}) copy-start(f32[128]{0:T(128)} %param.17) | copy-start | bytes 1540

commit v4 on v3

--- a/solution.py
+++ b/solution.py
@@ -68,36 +68,44 @@
     out[channels:, :channels] = zero
 
 
-def fill_edges(ext, row_near, row_far, col_near, col_far, size):
+def fill_edges(ext, row_near, row_far, col_near, col_far, spread, dense, size):
     rows = size + 2 * HALO
+    channels = ext.shape[2]
     tail = LEAD + size + PAD
-    ext[:, 0 : LEAD - PAD, :] = jnp.zeros((rows, LEAD - PAD, ext.shape[2]), BF16)
-    ext[:, tail:, :] = jnp.zeros((rows, ext.shape[1] - tail, ext.shape[2]), BF16)
-
-    def place(axis, near, far, low, high):
-        even = lax.rem(lax.axis_index(axis), 2) == 0
-
-        @pl.when(even)
-        def _():
-            low[...] = far[...]
-            high[...] = near[...]
-
-        @pl.when(jnp.logical_not(even))
-        def _():
-            low[...] = near[...]
-            high[...] = far[...]
-
     within = slice(LEAD, LEAD + size)
-    place(
-        "row", row_near, row_far, ext.at[0:HALO, within], ext.at[HALO + size :, within]
-    )
-    place(
-        "col",
-        col_near,
-        col_far,
-        ext.at[:, LEAD - PAD : LEAD],
-        ext.at[:, LEAD + size : tail],
-    )
+    even_row = lax.rem(lax.axis_index("row"), 2) == 0
+    even_col = lax.rem(lax.axis_index("col"), 2) == 0
+    ext[:, 0 : LEAD - PAD, :] = jnp.zeros((rows, LEAD - PAD, channels), BF16)
+    ext[:, tail:, :] = jnp.zeros((rows, ext.shape[1] - tail, channels), BF16)
+
+    for even, above, below in ((True, row_far, row_near), (False, row_near, row_far)):
+
+        @pl.when(even_row if even else jnp.logical_not(even_row))
+        def _(above=above, below=below):
+            ext[0:HALO, within, :] = above[...]
+            ext[HALO + size :, within, :] = below[...]
+
+    for side in range(2):
+
+        @pl.when(even_col)
+        def _(side=side):
+            dense[...] = (col_near if side else col_far)[...].astype(F32)
+
+        @pl.when(jnp.logical_not(even_col))
+        def _(side=side):
+            dense[...] = (col_far if side else col_near)[...].astype(F32)
+
+        for c in range(PAD):
+            line = c - (PAD - HALO) * (1 - side)
+            if 0 <= line < HALO:
+                value = dense[line * rows : (line + 1) * rows, :]
+            else:
+                value = jnp.zeros((rows, channels), F32)
+            spread[pl.ds(c, rows, stride=PAD), :] = value
+        begin = LEAD + size if side else LEAD - PAD
+        ext[:, begin : begin + PAD, :] = (
+            spread[...].reshape(rows, PAD, channels).astype(BF16)
+        )
 
 
 def near_block(wide, taps, bias, mix, group, groups, width, channels):
@@ -151,6 +159,8 @@
     ext,
     wide,
     taps,
+    spread,
+    dense,
     *,
     steps,
 ):
@@ -161,7 +171,7 @@
     place_twice(far_mix, far_mixer)
     size, channels = tile.shape[0], tile.shape[2]
     width = size + 2 * PAD
-    fill_edges(ext, row_near, row_far, col_near, col_far, size)
+    fill_edges(ext, row_near, row_far, col_near, col_far, spread, dense, size)
     ext[HALO : HALO + size, LEAD : LEAD + size, :] = tile[...]
     widen(ext, wide, width, LEAD - PAD, channels)
     groups = out.shape[0] // steps
@@ -221,6 +231,8 @@
     far_wide,
     stage,
     sems,
+    spread,
+    dense,
     *,
     steps,
     far_rows,
@@ -233,7 +245,7 @@
     anti = jnp.logical_and(row + col == last, row != col)
     plain = jnp.logical_not(jnp.logical_or(diagonal, anti))
 
-    fill_edges(ext, row_near, row_far, col_near, col_far, size)
+    fill_edges(ext, row_near, row_far, col_near, col_far, spread, dense, size)
     for source, chosen in ((own, diagonal), (direct, plain), (relayed, anti)):
 
         @pl.when(chosen)
@@ -340,29 +352,83 @@
     return top, low, left, right
 
 
-def exchange(low, high, axis):
+def swap_pairs(near, far, axis):
     count = lax.axis_size(axis)
-    even = lax.axis_index(axis) % 2 == 0
 
     def swap(first, value):
         pairs = [(i, i + 1) for i in range(first, count - 1, 2)]
         return lax.ppermute(value, axis, pairs + [(j, i) for i, j in pairs])
 
-    near = swap(0, jnp.where(even, high, low))
-    far = swap(1, jnp.where(even, low, high))
+    near = swap(0, near)
+    far = swap(1, far)
     return near, far
 
 
+def exchange(low, high, axis):
+    even = lax.axis_index(axis) % 2 == 0
+    return swap_pairs(jnp.where(even, high, low), jnp.where(even, low, high), axis)
+
+
+def strip_kernel(left, right, row_near, row_far, near, far, wide, dense):
+    size, _, channels = left.shape
+    width = row_near.shape[1]
+    rows = size + 2 * HALO
+    head = HALO * PAD
+    even_row = lax.rem(lax.axis_index("row"), 2) == 0
+    even_col = lax.rem(lax.axis_index("col"), 2) == 0
+
+    for side, edge in enumerate((left, right)):
+        columns = slice(side * (width - PAD), side * (width - PAD) + PAD)
+        wide[head : head + size * PAD, :] = (
+            edge[...].reshape(size * PAD, channels).astype(F32)
+        )
+        for even, above, below in (
+            (True, row_far, row_near),
+            (False, row_near, row_far),
+        ):
+
+            @pl.when(even_row if even else jnp.logical_not(even_row))
+            def _(above=above, below=below, columns=columns):
+                wide[0:head, :] = (
+                    above[:, columns, :].reshape(head, channels).astype(F32)
+                )
+                wide[head + size * PAD :, :] = (
+                    below[:, columns, :].reshape(head, channels).astype(F32)
+                )
+
+        for c in range(HALO):
+            line = c + side * (PAD - HALO)
+            dense[c * rows : (c + 1) * rows, :] = wide[pl.ds(line, rows, stride=PAD), :]
+
+        packed = dense[...].astype(BF16)
+
+        @pl.when(even_col)
+        def _(side=side, packed=packed):
+            (near if side else far)[...] = packed
+
+        @pl.when(jnp.logical_not(even_col))
+        def _(side=side, packed=packed):
+            (far if side else near)[...] = packed
+
+
 def halo_pieces(top, low, left, right):
-    size = top.shape[1]
-    near, far = exchange(top, low, "row")
-    even = lax.axis_index("row") % 2 == 0
-    above, below = jnp.where(even, far, near), jnp.where(even, near, far)
-    start = jnp.concatenate([above[:, :PAD], left, below[:, :PAD]], axis=0)
-    end = jnp.concatenate(
-        [above[:, size - PAD :], right, below[:, size - PAD :]], axis=0
-    )
-    return (near, far) + exchange(start, end, "col")
+    size, channels = left.shape[0], left.shape[2]
+    rows = size + 2 * HALO
+    row_near, row_far = exchange(top, low, "row")
+    whole = pl.BlockSpec(memory_space=pltpu.VMEM)
+    strip = jax.ShapeDtypeStruct((HALO * rows, channels), BF16)
+    near, far = pl.pallas_call(
+        strip_kernel,
+        out_shape=[strip, strip],
+        in_specs=[whole] * 4,
+        out_specs=[whole] * 2,
+        scratch_shapes=[
+            pltpu.VMEM((PAD * rows, channels), F32),
+            pltpu.VMEM((HALO * rows, channels), F32),
+        ],
+        compiler_params=pltpu.CompilerParams(vmem_limit_bytes=GRANT // 4),
+    )(left, right, row_near, row_far)
+    return (row_near, row_far) + swap_pairs(near, far, "col")
 
 
 def compute(
@@ -427,6 +493,10 @@
     wide = pltpu.VMEM(
         (rows // (2 * NEAR), 2, NEAR, width, 3 * channels), BF16
     )
+    lines = [
+        pltpu.VMEM((PAD * rows, channels), F32),
+        pltpu.VMEM((HALO * rows, channels), F32),
+    ]
     field = (groups, 2, NEAR, width, channels)
     pairs = (12 * channels, 2 * channels)
     square = (2 * channels, 2 * channels)
@@ -439,7 +509,7 @@
         ],
         in_specs=[whole] * 11,
         out_specs=[whole] * 5,
-        scratch_shapes=[ext, wide, pltpu.VMEM(pairs, BF16)],
+        scratch_shapes=[ext, wide, pltpu.VMEM(pairs, BF16)] + lines,
         cost_estimate=pl.CostEstimate(
             flops=2 * near_flops, bytes_accessed=8 << 20, transcendentals=0
         ),
@@ -470,7 +540,8 @@
             pltpu.VMEM((groups, 2, NEAR, size, 3 * channels), BF16),
             pltpu.VMEM((2, far_rows, size, channels), F32),
             pltpu.SemaphoreType.DMA((2,)),
-        ],
+        ]
+        + lines,
         cost_estimate=pl.CostEstimate(
             flops=4 * near_flops, bytes_accessed=16 << 20, transcendentals=0
         ),

time: 69.6 us -> 63.8 us (0.917)
  the two profiles are of different devices: /device:TPU:14 before, /device:TPU:0 now
where the time goes in v4:
time: 63.8 us; the launch traced here: 63.5 us
  starting transfers between devices  38.6 us (61%)
  Pallas kernels  12.9 us (20%)
  waiting for transfers between devices  7.56 us (12%)
  local copies, waits for them, and re-layouts  2.68 us (4%)
  other arithmetic  1.29 us (2%)
    ppermute x8, starting transfers between devices, swap(): return lax.ppermute(value, axis, pairs + [(j, i) for i, j in pairs])  25.9 us
    ppermute x5, starting transfers between devices, send(): return lax.ppermute(value, pair, route)  12.7 us
    pallas_call x1, Pallas kernels, compute(): pl.pallas_call(functools.partial(main_kernel, steps=1, far_rows=far_rows)...  8.74 us
    ppermute x5, waiting for transfers between devices, send(): return lax.ppermute(value, pair, route)  5.74 us
    pallas_call x1, Pallas kernels, compute(): summed, taps, mix, far_taps, far_mix = own_block(*own_operands)  3.91 us
    transpose x4, local copies, waits for them, and re-layouts, compute(): turn = lambda part: jnp.swapaxes(part, 0, 1)  2.17 us
    ppermute x8, waiting for transfers between devices, swap(): return lax.ppermute(value, axis, pairs + [(j, i) for i, j in pairs])  1.82 us
  transfers between devices with their start and end apart: 13, of which 3 were waited for; matrix products, arithmetic and copies ran while one was open for 3% of the time, Pallas kernels for 7%

profile of v4, /device:TPU:0, one launch (start us, length us, event | category | flops | bytes accessed | tf_op | source)
XLA Modules:
  0.0 63.5 jit_solution(2312549168642267598)
XLA Ops:
  0.0 1.1 %slice_bitcast_fusion.3 = (bf16[52,8,128]{2,0,1:T(8,128)(2,1)S(1)}, bf16[52,8,128]{2,0,1:T(8,128)(2,1)S(1)}) fusion(bf16[64,64,128]{2,1,0:T(8,128)(2,1)} %tile.1), kind=kLoop, calls=%fused_computation.8 | loop fusion | bytes 425984 | tf_op jit(solution)/shard_map/transpose | solution.py:456
  1.1 1.0 %slice_bitcast_fusion.1 = (bf16[6,64,128]{2,0,1:T(8,128)(2,1)S(1)}, bf16[6,64,128]{2,0,1:T(8,128)(2,1)S(1)}) fusion(bf16[64,64,128]{2,1,0:T(8,128)(2,1)} %tile.1), kind=kLoop, calls=%fused_computation.6 | loop fusion | bytes 393216 | tf_op jit(solution)/shard_map/transpose | solution.py:456
  2.3 1.3 %collective-permute-start = (bf16[1600,128]{1,0:T(8,128)(2,1)S(1)}, bf16[1600,128]{1,0:T(8,128)(2,1)}, u32[]{:S(2)}, u32[]{:S(2)}) collective-permute-start(bf16[1600,128]{1,0:T(8,128)(2,1)S(1)} %pad_maximum_fusion), channel_id=1, source_target_pairs={{1,4},{2,8},{4,1},{7,13},{8,2},{11,14},{13,7},{14,11},{3,15},{6,10... | collective-permute-start | bytes 1228808 | tf_op jit(solution)/shard_map/ppermute | solution.py:454
  3.6 0.0 copy-done
  3.6 0.3 slice.55
  3.8 0.1 copy.19
  3.9 1.3 %collective-permute-start.3 = (bf16[52,48,128]{2,1,0:T(8,128)(2,1)S(1)}, bf16[52,48,128]{2,1,0:T(8,128)(2,1)}, u32[]{:S(2)}, u32[]{:S(2)}) collective-permute-start(bf16[52,48,128]{2,1,0:T(8,128)(2,1)S(1)} %bitcast.27), channel_id=1, source_target_pairs={{3,15},{6,10},{9,5},{12,0},{19,31},{22,26},{25,21},{28,16}} | collective-permute-start | bytes 1916936 | tf_op jit(solution)/shard_map/ppermute | solution.py:454
  5.2 0.7 %collective-permute-start.2 = (bf16[52,48,128]{2,1,0:T(8,128)(2,1)S(1)}, bf16[52,48,128]{2,1,0:T(8,128)(2,1)S(1)}, u32[]{:S(2)}, u32[]{:S(2)}) collective-permute-start(bf16[52,48,128]{2,1,0:T(8,128)(2,1)S(1)} %bitcast.28), channel_id=1, source_target_pairs={{1,4},{2,8},{4,1},{7,13},{8,2},{11,14},{13,7},{14,11},{17,20},{18,... | collective-permute-start | bytes 1916936 | tf_op jit(solution)/shard_map/ppermute | solution.py:454
  6.0 5.7 %collective-permute-done = bf16[1600,128]{1,0:T(8,128)(2,1)} collective-permute-done((bf16[1600,128]{1,0:T(8,128)(2,1)S(1)}, bf16[1600,128]{1,0:T(8,128)(2,1)}, u32[]{:S(2)}, u32[]{:S(2)}) %collective-permute-start) | collective-permute-done | bytes 409632 | tf_op jit(solution)/shard_map/ppermute | solution.py:454
  11.7 6.6 %collective-permute-start.1 = (bf16[1600,128]{1,0:T(8,128)(2,1)}, bf16[1600,128]{1,0:T(8,128)(2,1)}, u32[]{:S(2)}, u32[]{:S(2)}) collective-permute-start(bf16[1600,128]{1,0:T(8,128)(2,1)} %collective-permute-done), channel_id=1, source_target_pairs={{15,12},{10,9},{5,6},{0,3},{31,28},{26,25},{21,22},{16,19}} | collective-permute-start | bytes 1228808 | tf_op jit(solution)/shard_map/ppermute | solution.py:454
  18.3 0.7 %collective-permute-start.10 = (bf16[6,64,128]{2,1,0:T(8,128)(2,1)S(1)}, bf16[6,64,128]{2,1,0:T(8,128)(2,1)S(1)}, u32[]{:S(2)}, u32[]{:S(2)}) collective-permute-start(bf16[6,64,128]{2,1,0:T(8,128)(2,1)S(1)} %get-tuple-element.25), channel_id=1, source_target_pairs={{4,8},{8,4},{5,9},{9,5},{6,10},{10,6},{7,11},{11,7},{20,24},{24,20... | collective-permute-start | bytes 294920 | tf_op jit(solution)/shard_map/ppermute | solution.py:360
  19.0 12.7 %collective-permute-start.9 = (bf16[6,64,128]{2,1,0:T(8,128)(2,1)S(1)}, bf16[6,64,128]{2,1,0:T(8,128)(2,1)S(1)}, u32[]{:S(2)}, u32[]{:S(2)}) collective-permute-start(bf16[6,64,128]{2,1,0:T(8,128)(2,1)S(1)} %get-tuple-element.26), channel_id=1, source_target_pairs={{0,4},{8,12},{4,0},{12,8},{1,5},{9,13},{5,1},{13,9},{2,6},{10,14},... | collective-permute-start | bytes 294920 | tf_op jit(solution)/shard_map/ppermute | solution.py:360
  31.7 0.0 collective-permute-done.10.row_far
  31.7 0.9 %collective-permute-done.9.row_near = bf16[6,64,128]{2,1,0:T(8,128)(2,1)S(1)} collective-permute-done((bf16[6,64,128]{2,1,0:T(8,128)(2,1)S(1)}, bf16[6,64,128]{2,1,0:T(8,128)(2,1)S(1)}, u32[]{:S(2)}, u32[]{:S(2)}) %collective-permute-start.9) | collective-permute-done | bytes 98336 | tf_op jit(solution)/shard_map/ppermute | solution.py:360
  32.6 0.1 shard_map.92
  32.8 0.0 copy-start.1
  32.8 0.0 copy-start.2
  32.8 0.0 copy-start.3
  32.8 0.0 copy-start.4
  32.8 0.0 copy-start.5
  32.8 0.0 copy-start.6
  32.9 0.1 collective-permute-start.11
  32.9 0.8 %collective-permute-start.12 = (bf16[456,128]{1,0:T(8,128)(2,1)S(1)}, bf16[456,128]{1,0:T(8,128)(2,1)S(1)}, u32[]{:S(2)}, u32[]{:S(2)}) collective-permute-start(bf16[456,128]{1,0:T(8,128)(2,1)S(1)} %get-tuple-element.17), channel_id=1, source_target_pairs={{1,2},{2,1},{5,6},{6,5},{9,10},{10,9},{13,14},{14,13},{17,18},{18,... | collective-permute-start | bytes 350216 | tf_op jit(solution)/shard_map/ppermute | solution.py:360
  33.7 0.0 collective-permute-done.3
  33.8 2.8 %collective-permute-start.4 = (bf16[52,48,128]{2,1,0:T(8,128)(2,1)}, bf16[52,48,128]{2,1,0:T(8,128)(2,1)S(1)}, u32[]{:S(2)}, u32[]{:S(2)}) collective-permute-start(bf16[52,48,128]{2,1,0:T(8,128)(2,1)} %collective-permute-done.3), channel_id=1, source_target_pairs={{15,12},{10,9},{5,6},{0,3},{31,28},{26,25},{21,22},{16,19}} | collective-permute-start | bytes 1916936 | tf_op jit(solution)/shard_map/ppermute | solution.py:454
  36.5 0.0 collective-permute-done.1
  36.5 1.2 %select_select_fusion.frame = bf16[1600,128]{1,0:T(8,128)(2,1)S(1)} fusion(bf16[1600,128]{1,0:T(8,128)(2,1)} %collective-permute-done.1, bf16[1600,128]{1,0:T(8,128)(2,1)} %collective-permute-done, pred[]{:T(512)S(6)} %eq.14, pred[]{:T(512)S(6)} %eq.13, bf16[416,128]{1,0:T(8,128)(2,1)S(1)} %get-tuple-element.41, bf16[416,128]{1,0:T(8,128)(2,1)S(1)} %get-tuple-element.42, ...), kind=kLoop, calls=%fused_computation.2 | loop fusion | flops 2048000 | bytes 1638402 | tf_op jit(solution)/shard_map/jit(_where)/select_n | solution.py:479
  37.8 0.7 %collective-permute-start.6 = (bf16[6,64,128]{2,1,0:T(8,128)(2,1)S(1)}, bf16[6,64,128]{2,1,0:T(8,128)(2,1)S(1)}, u32[]{:S(2)}, u32[]{:S(2)}) collective-permute-start(bf16[6,64,128]{2,1,0:T(8,128)(2,1)S(1)} %get-tuple-element.35), channel_id=1, source_target_pairs={{4,8},{8,4},{5,9},{9,5},{6,10},{10,6},{7,11},{11,7},{20,24},{24,20... | collective-permute-start | bytes 294920 | tf_op jit(solution)/shard_map/ppermute | solution.py:360
  38.5 0.0 collective-permute-done.6.row_far
  38.5 4.9 %collective-permute-start.5 = (bf16[6,64,128]{2,1,0:T(8,128)(2,1)S(1)}, bf16[6,64,128]{2,1,0:T(8,128)(2,1)S(1)}, u32[]{:S(2)}, u32[]{:S(2)}) collective-permute-start(bf16[6,64,128]{2,1,0:T(8,128)(2,1)S(1)} %get-tuple-element.36), channel_id=1, source_target_pairs={{0,4},{8,12},{4,0},{12,8},{1,5},{9,13},{5,1},{13,9},{2,6},{10,14},... | collective-permute-start | bytes 294920 | tf_op jit(solution)/shard_map/ppermute | solution.py:360
  43.4 0.9 %collective-permute-done.5.row_near = bf16[6,64,128]{2,1,0:T(8,128)(2,1)S(1)} collective-permute-done((bf16[6,64,128]{2,1,0:T(8,128)(2,1)S(1)}, bf16[6,64,128]{2,1,0:T(8,128)(2,1)S(1)}, u32[]{:S(2)}, u32[]{:S(2)}) %collective-permute-start.5) | collective-permute-done | bytes 98336 | tf_op jit(solution)/shard_map/ppermute | solution.py:360
  44.3 0.1 shard_map.91
  44.5 5.5 %collective-permute-start.7 = (bf16[456,128]{1,0:T(8,128)(2,1)S(1)}, bf16[456,128]{1,0:T(8,128)(2,1)S(1)}, u32[]{:S(2)}, u32[]{:S(2)}) collective-permute-start(bf16[456,128]{1,0:T(8,128)(2,1)S(1)} %get-tuple-element.14), channel_id=1, source_target_pairs={{0,1},{2,3},{1,0},{3,2},{4,5},{6,7},{5,4},{7,6},{8,9},{10,11},{9,8... | collective-permute-start | bytes 350216 | tf_op jit(solution)/shard_map/ppermute | solution.py:360
  50.0 0.0 collective-permute-done.11.col_near
  50.0 0.7 %collective-permute-start.8 = (bf16[456,128]{1,0:T(8,128)(2,1)S(1)}, bf16[456,128]{1,0:T(8,128)(2,1)S(1)}, u32[]{:S(2)}, u32[]{:S(2)}) collective-permute-start(bf16[456,128]{1,0:T(8,128)(2,1)S(1)} %get-tuple-element.15), channel_id=1, source_target_pairs={{1,2},{2,1},{5,6},{6,5},{9,10},{10,9},{13,14},{14,13},{17,18},{18,... | collective-permute-start | bytes 350216 | tf_op jit(solution)/shard_map/ppermute | solution.py:360
  50.7 0.0 collective-permute-done.12.col_far
  50.7 0.0 copy-done.1
  50.7 0.0 copy-done.2
  50.7 0.0 copy-done.3
  50.7 0.0 copy-done.4
  50.7 0.0 copy-start.7
  50.8 0.0 copy-start.8
  50.8 3.9 %own_block.1 = (bf16[18,2,2,80,128]{4,3,2,1,0:T(8,128)(2,1)S(1)}, bf16[1536,256]{1,0:T(8,128)(2,1)S(1)}, bf16[256,256]{1,0:T(8,128)(2,1)S(1)}, bf16[1152,256]{1,0:T(8,128)(2,1)S(1)}, bf16[256,256]{1,0:T(8,128)(2,1)S(1)}) custom-call(bf16[64,64,128]{2,1,0:T(8,128)(2,1)S(1)} %copy-done, bf16[6,64,128]{2,1,0:T(8,128)(2,1)S(1)} %collective-permute-done.9.row_near, ...), custom_call_target="tpu_custom_call" | custom-call | flops 3774873600 | bytes 8388608 | tf_op jit(solution)/shard_map/own_block/pallas_call | solution.py:529
  54.7 0.0 collective-permute-done.2.direct
  54.7 0.0 collective-permute-done.7.col_near
  54.7 0.0 collective-permute-done.8.col_far
  54.7 0.0 collective-permute-done.4.relayed
  54.7 8.7 %main_block.1 = f32[64,64,128]{2,1,0:T(8,128)} custom-call(bf16[1600,128]{1,0:T(8,128)(2,1)S(1)} %select_select_fusion.frame, bf16[52,48,128]{2,1,0:T(8,128)(2,1)S(1)} %bitcast.29, bf16[52,48,128]{2,1,0:T(8,128)(2,1)S(1)} %collective-permute-done.2.direct, bf16[52,48,128]{2,1,0:T(8,128)(2,1)S(1)} %collective-permute-done.4.relayed, ...), custom_call_target="tpu_custom_call" | custom-call | flops 7549747200 | bytes 16777216 | tf_op jit(solution)/shard_map/main_block/pallas_call | solution.py:532
  (18 shorter events, 0.3 us)
Async XLA Ops:
  0.0 3.6 %copy-start = (bf16[64,64,128]{2,1,0:T(8,128)(2,1)S(1)}, bf16[64,64,128]{2,1,0:T(8,128)(2,1)}, u32[]{:S(2)}) copy-start(bf16[64,64,128]{2,1,0:T(8,128)(2,1)} %tile.1) | copy-start | bytes 3145732
  2.3 9.4 %collective-permute-start = (bf16[1600,128]{1,0:T(8,128)(2,1)S(1)}, bf16[1600,128]{1,0:T(8,128)(2,1)}, u32[]{:S(2)}, u32[]{:S(2)}) collective-permute-start(bf16[1600,128]{1,0:T(8,128)(2,1)S(1)} %pad_maximum_fusion), channel_id=1, source_target_pairs={{1,4},{2,8},{4,1},{7,13},{8,2},{11,14},{13,7},{14,11},{3,15},{6,10... | collective-permute-start | bytes 1228808 | tf_op jit(solution)/shard_map/ppermute | solution.py:454
  3.9 29.8 %collective-permute-start.3 = (bf16[52,48,128]{2,1,0:T(8,128)(2,1)S(1)}, bf16[52,48,128]{2,1,0:T(8,128)(2,1)}, u32[]{:S(2)}, u32[]{:S(2)}) collective-permute-start(bf16[52,48,128]{2,1,0:T(8,128)(2,1)S(1)} %bitcast.27), channel_id=1, source_target_pairs={{3,15},{6,10},{9,5},{12,0},{19,31},{22,26},{25,21},{28,16}} | collective-permute-start | bytes 1916936 | tf_op jit(solution)/shard_map/ppermute | solution.py:454
  5.2 49.5 %collective-permute-start.2 = (bf16[52,48,128]{2,1,0:T(8,128)(2,1)S(1)}, bf16[52,48,128]{2,1,0:T(8,128)(2,1)S(1)}, u32[]{:S(2)}, u32[]{:S(2)}) collective-permute-start(bf16[52,48,128]{2,1,0:T(8,128)(2,1)S(1)} %bitcast.28), channel_id=1, source_target_pairs={{1,4},{2,8},{4,1},{7,13},{8,2},{11,14},{13,7},{14,11},{17,20},{18,... | collective-permute-start | bytes 1916936 | tf_op jit(solution)/shard_map/ppermute | solution.py:454
  11.7 24.8 %collective-permute-start.1 = (bf16[1600,128]{1,0:T(8,128)(2,1)}, bf16[1600,128]{1,0:T(8,128)(2,1)}, u32[]{:S(2)}, u32[]{:S(2)}) collective-permute-start(bf16[1600,128]{1,0:T(8,128)(2,1)} %collective-permute-done), channel_id=1, source_target_pairs={{15,12},{10,9},{5,6},{0,3},{31,28},{26,25},{21,22},{16,19}} | collective-permute-start | bytes 1228808 | tf_op jit(solution)/shard_map/ppermute | solution.py:454
  18.3 13.4 %collective-permute-start.10 = (bf16[6,64,128]{2,1,0:T(8,128)(2,1)S(1)}, bf16[6,64,128]{2,1,0:T(8,128)(2,1)S(1)}, u32[]{:S(2)}, u32[]{:S(2)}) collective-permute-start(bf16[6,64,128]{2,1,0:T(8,128)(2,1)S(1)} %get-tuple-element.25), channel_id=1, source_target_pairs={{4,8},{8,4},{5,9},{9,5},{6,10},{10,6},{7,11},{11,7},{20,24},{24,20... | collective-permute-start | bytes 294920 | tf_op jit(solution)/shard_map/ppermute | solution.py:360
  19.0 13.6 %collective-permute-start.9 = (bf16[6,64,128]{2,1,0:T(8,128)(2,1)S(1)}, bf16[6,64,128]{2,1,0:T(8,128)(2,1)S(1)}, u32[]{:S(2)}, u32[]{:S(2)}) collective-permute-start(bf16[6,64,128]{2,1,0:T(8,128)(2,1)S(1)} %get-tuple-element.26), channel_id=1, source_target_pairs={{0,4},{8,12},{4,0},{12,8},{1,5},{9,13},{5,1},{13,9},{2,6},{10,14},... | collective-permute-start | bytes 294920 | tf_op jit(solution)/shard_map/ppermute | solution.py:360
  32.8 17.9 %copy-start.1 = (bf16[3,3,128,128]{3,2,1,0:T(8,128)(2,1)S(1)}, bf16[3,3,128,128]{3,2,1,0:T(8,128)(2,1)}, u32[]{:S(2)}) copy-start(bf16[3,3,128,128]{3,2,1,0:T(8,128)(2,1)} %kernel.1) | copy-start | bytes 884740
  32.8 17.9 %copy-start.2 = (bf16[3,3,128,128]{3,2,1,0:T(8,128)(2,1)S(1)}, bf16[3,3,128,128]{3,2,1,0:T(8,128)(2,1)}, u32[]{:S(2)}) copy-start(bf16[3,3,128,128]{3,2,1,0:T(8,128)(2,1)} %far_kernel.1) | copy-start | bytes 884740
  32.8 17.9 %copy-start.3 = (bf16[128,128]{1,0:T(8,128)(2,1)S(1)}, bf16[128,128]{1,0:T(8,128)(2,1)}, u32[]{:S(2)}) copy-start(bf16[128,128]{1,0:T(8,128)(2,1)} %mixer.1) | copy-start | bytes 98308
  32.8 17.9 %copy-start.4 = (bf16[128,128]{1,0:T(8,128)(2,1)S(1)}, bf16[128,128]{1,0:T(8,128)(2,1)}, u32[]{:S(2)}) copy-start(bf16[128,128]{1,0:T(8,128)(2,1)} %far_mixer.1) | copy-start | bytes 98308
  32.8 17.9 %copy-start.5 = (f32[128]{0:T(128)S(1)}, f32[128]{0:T(128)}, u32[]{:S(2)}) copy-start(f32[128]{0:T(128)} %param.13) | copy-start | bytes 1540
  32.8 17.9 %copy-start.6 = (f32[128]{0:T(128)S(1)}, f32[128]{0:T(128)}, u32[]{:S(2)}) copy-start(f32[128]{0:T(128)} %param.11) | copy-start | bytes 1540
  32.9 17.1 %collective-permute-start.11 = (bf16[456,128]{1,0:T(8,128)(2,1)S(1)}, bf16[456,128]{1,0:T(8,128)(2,1)S(1)}, u32[]{:S(2)}, u32[]{:S(2)}) collective-permute-start(bf16[456,128]{1,0:T(8,128)(2,1)S(1)} %get-tuple-element.16), channel_id=1, source_target_pairs={{0,1},{2,3},{1,0},{3,2},{4,5},{6,7},{5,4},{7,6},{8,9},{10,11},{9,8... | collective-permute-start | bytes 350216 | tf_op jit(solution)/shard_map/ppermute | solution.py:360
  32.9 17.7 %collective-permute-start.12 = (bf16[456,128]{1,0:T(8,128)(2,1)S(1)}, bf16[456,128]{1,0:T(8,128)(2,1)S(1)}, u32[]{:S(2)}, u32[]{:S(2)}) collective-permute-start(bf16[456,128]{1,0:T(8,128)(2,1)S(1)} %get-tuple-element.17), channel_id=1, source_target_pairs={{1,2},{2,1},{5,6},{6,5},{9,10},{10,9},{13,14},{14,13},{17,18},{18,... | collective-permute-start | bytes 350216 | tf_op jit(solution)/shard_map/ppermute | solution.py:360
  33.8 21.0 %collective-permute-start.4 = (bf16[52,48,128]{2,1,0:T(8,128)(2,1)}, bf16[52,48,128]{2,1,0:T(8,128)(2,1)S(1)}, u32[]{:S(2)}, u32[]{:S(2)}) collective-permute-start(bf16[52,48,128]{2,1,0:T(8,128)(2,1)} %collective-permute-done.3), channel_id=1, source_target_pairs={{15,12},{10,9},{5,6},{0,3},{31,28},{26,25},{21,22},{16,19}} | collective-permute-start | bytes 1916936 | tf_op jit(solution)/shard_map/ppermute | solution.py:454
  37.8 0.7 %collective-permute-start.6 = (bf16[6,64,128]{2,1,0:T(8,128)(2,1)S(1)}, bf16[6,64,128]{2,1,0:T(8,128)(2,1)S(1)}, u32[]{:S(2)}, u32[]{:S(2)}) collective-permute-start(bf16[6,64,128]{2,1,0:T(8,128)(2,1)S(1)} %get-tuple-element.35), channel_id=1, source_target_pairs={{4,8},{8,4},{5,9},{9,5},{6,10},{10,6},{7,11},{11,7},{20,24},{24,20... | collective-permute-start | bytes 294920 | tf_op jit(solution)/shard_map/ppermute | solution.py:360
  38.5 5.8 %collective-permute-start.5 = (bf16[6,64,128]{2,1,0:T(8,128)(2,1)S(1)}, bf16[6,64,128]{2,1,0:T(8,128)(2,1)S(1)}, u32[]{:S(2)}, u32[]{:S(2)}) collective-permute-start(bf16[6,64,128]{2,1,0:T(8,128)(2,1)S(1)} %get-tuple-element.36), channel_id=1, source_target_pairs={{0,4},{8,12},{4,0},{12,8},{1,5},{9,13},{5,1},{13,9},{2,6},{10,14},... | collective-permute-start | bytes 294920 | tf_op jit(solution)/shard_map/ppermute | solution.py:360
  44.5 10.2 %collective-permute-start.7 = (bf16[456,128]{1,0:T(8,128)(2,1)S(1)}, bf16[456,128]{1,0:T(8,128)(2,1)S(1)}, u32[]{:S(2)}, u32[]{:S(2)}) collective-permute-start(bf16[456,128]{1,0:T(8,128)(2,1)S(1)} %get-tuple-element.14), channel_id=1, source_target_pairs={{0,1},{2,3},{1,0},{3,2},{4,5},{6,7},{5,4},{7,6},{8,9},{10,11},{9,8... | collective-permute-start | bytes 350216 | tf_op jit(solution)/shard_map/ppermute | solution.py:360
  50.0 4.7 %collective-permute-start.8 = (bf16[456,128]{1,0:T(8,128)(2,1)S(1)}, bf16[456,128]{1,0:T(8,128)(2,1)S(1)}, u32[]{:S(2)}, u32[]{:S(2)}) collective-permute-start(bf16[456,128]{1,0:T(8,128)(2,1)S(1)} %get-tuple-element.15), channel_id=1, source_target_pairs={{1,2},{2,1},{5,6},{6,5},{9,10},{10,9},{13,14},{14,13},{17,18},{18,... | collective-permute-start | bytes 350216 | tf_op jit(solution)/shard_map/ppermute | solution.py:360
  50.7 4.0 %copy-start.7 = (f32[128]{0:T(128)S(1)}, f32[128]{0:T(128)}, u32[]{:S(2)}) copy-start(f32[128]{0:T(128)} %param.15) | copy-start | bytes 1540
  50.8 4.0 %copy-start.8 = (f32[128]{0:T(128)S(1)}, f32[128]{0:T(128)}, u32[]{:S(2)}) copy-start(f32[128]{0:T(128)} %param.17) | copy-start | bytes 1540

commit v5 on v4

--- a/solution.py
+++ b/solution.py
@@ -51,11 +51,22 @@
 
 def place_both(out, kernel):
     channels = kernel.shape[2]
+    begin = 0
     for down in range(3):
         for side in range(3):
-            begin = (3 * down + side) * channels
-            out[begin : begin + channels, :channels] = kernel[down, side]
-            out[begin : begin + channels, channels:] = kernel[side, down]
+            if down != side:
+                out[begin : begin + channels, :channels] = kernel[down, side]
+                out[begin : begin + channels, channels:] = kernel[side, down]
+                begin += channels
+    zero = jnp.zeros((channels, channels), BF16)
+    for half in range(2):
+        for down in range(3):
+            for other in range(2):
+                out[
+                    begin : begin + channels,
+                    other * channels : (other + 1) * channels,
+                ] = kernel[down, down] if other == half else zero
+            begin += channels
 
 
 def place_twice(out, matrix):
@@ -311,16 +322,33 @@
             copy(slot, (k - 2) * far_rows).wait()
 
         rows = far_rows * size
-        part = jnp.concatenate(
-            [
-                far_wide[pl.ds(base + tap, far_rows // FAR)].reshape(rows, 3 * channels)
-                for tap in range(3)
-            ],
+        views = [
+            far_wide[pl.ds(base + tap, far_rows // FAR)].reshape(rows, 3 * channels)
+            for tap in range(3)
+        ]
+
+        def pick(tap, side):
+            return views[tap][:, side * channels : (side + 1) * channels]
+
+        cross = jnp.concatenate(
+            [pick(a, b) for a in range(3) for b in range(3) if a != b], axis=1
+        )
+        total = jnp.dot(
+            cross, far_taps[: 6 * channels, :], preferred_element_type=F32
+        )
+        middle = rows // 2
+        line = jnp.concatenate(
+            [pick(a, a)[:middle] for a in range(3)]
+            + [pick(a, a)[middle:] for a in range(3)],
             axis=1,
         )
-        total = jnp.dot(part, far_taps[...], preferred_element_type=F32)
-        active = jnp.maximum(total[:, :channels] + far_bias[...], 0.0)
-        active = active + jnp.maximum(total[:, channels:] + far_bias[...], 0.0)
+        shared = jnp.dot(
+            line, far_taps[6 * channels :, :], preferred_element_type=F32
+        )
+        shared = jnp.concatenate([shared[:, :channels], shared[:, channels:]], axis=0)
+        shared = shared + far_bias[...]
+        active = jnp.maximum(total[:, :channels] + shared, 0.0)
+        active = active + jnp.maximum(total[:, channels:] + shared, 0.0)
         active = active.astype(BF16)
         active = jnp.concatenate([active[: rows // 2], active[rows // 2 :]], axis=1)
         mixed = jnp.dot(active, far_mix[...], preferred_element_type=F32)
@@ -505,7 +533,7 @@
         functools.partial(own_kernel, steps=1),
         out_shape=[
             jax.ShapeDtypeStruct(shape, BF16)
-            for shape in (field, pairs, square, (9 * channels, 2 * channels), square)
+            for shape in (field, pairs, square, pairs, square)
         ],
         in_specs=[whole] * 11,
         out_specs=[whole] * 5,

time: 63.8 us -> 63.6 us (level)
  no operation moved by 1% of the time
where the time goes in v5:
time: 63.6 us; the launch traced here: 63.2 us
  starting transfers between devices  38.6 us (61%)
  Pallas kernels  12.7 us (20%)
  waiting for transfers between devices  7.56 us (12%)
  local copies, waits for them, and re-layouts  2.68 us (4%)
  other arithmetic  1.29 us (2%)
    ppermute x8, starting transfers between devices, swap(): return lax.ppermute(value, axis, pairs + [(j, i) for i, j in pairs])  25.9 us
    ppermute x5, starting transfers between devices, send(): return lax.ppermute(value, pair, route)  12.7 us
    pallas_call x1, Pallas kernels, compute(): pl.pallas_call(functools.partial(main_kernel, steps=1, far_rows=far_rows)...  8.46 us
    ppermute x5, waiting for transfers between devices, send(): return lax.ppermute(value, pair, route)  5.74 us
    pallas_call x1, Pallas kernels, compute(): summed, taps, mix, far_taps, far_mix = own_block(*own_operands)  3.93 us
    transpose x4, local copies, waits for them, and re-layouts, compute(): turn = lambda part: jnp.swapaxes(part, 0, 1)  2.17 us
    ppermute x8, waiting for transfers between devices, swap(): return lax.ppermute(value, axis, pairs + [(j, i) for i, j in pairs])  1.82 us
  transfers between devices with their start and end apart: 13, of which 3 were waited for; matrix products, arithmetic and copies ran while one was open for 3% of the time, Pallas kernels for 7%

profile of v5, /device:TPU:0, one launch (start us, length us, event | category | flops | bytes accessed | tf_op | source)
XLA Modules:
  0.0 63.2 jit_solution(11741472973655626734)
XLA Ops:
  0.0 1.1 %slice_bitcast_fusion.3 = (bf16[52,8,128]{2,0,1:T(8,128)(2,1)S(1)}, bf16[52,8,128]{2,0,1:T(8,128)(2,1)S(1)}) fusion(bf16[64,64,128]{2,1,0:T(8,128)(2,1)} %tile.1), kind=kLoop, calls=%fused_computation.8 | loop fusion | bytes 425984 | tf_op jit(solution)/shard_map/transpose | solution.py:484
  1.1 1.0 %slice_bitcast_fusion.1 = (bf16[6,64,128]{2,0,1:T(8,128)(2,1)S(1)}, bf16[6,64,128]{2,0,1:T(8,128)(2,1)S(1)}) fusion(bf16[64,64,128]{2,1,0:T(8,128)(2,1)} %tile.1), kind=kLoop, calls=%fused_computation.6 | loop fusion | bytes 393216 | tf_op jit(solution)/shard_map/transpose | solution.py:484
  2.3 1.3 %collective-permute-start = (bf16[1600,128]{1,0:T(8,128)(2,1)S(1)}, bf16[1600,128]{1,0:T(8,128)(2,1)}, u32[]{:S(2)}, u32[]{:S(2)}) collective-permute-start(bf16[1600,128]{1,0:T(8,128)(2,1)S(1)} %pad_maximum_fusion), channel_id=1, source_target_pairs={{1,4},{2,8},{4,1},{7,13},{8,2},{11,14},{13,7},{14,11},{3,15},{6,10... | collective-permute-start | bytes 1228808 | tf_op jit(solution)/shard_map/ppermute | solution.py:482
  3.6 0.0 copy-done
  3.6 0.3 slice.55
  3.8 0.1 copy.19
  3.9 1.3 %collective-permute-start.3 = (bf16[52,48,128]{2,1,0:T(8,128)(2,1)S(1)}, bf16[52,48,128]{2,1,0:T(8,128)(2,1)}, u32[]{:S(2)}, u32[]{:S(2)}) collective-permute-start(bf16[52,48,128]{2,1,0:T(8,128)(2,1)S(1)} %bitcast.27), channel_id=1, source_target_pairs={{3,15},{6,10},{9,5},{12,0},{19,31},{22,26},{25,21},{28,16}} | collective-permute-start | bytes 1916936 | tf_op jit(solution)/shard_map/ppermute | solution.py:482
  5.2 0.7 %collective-permute-start.2 = (bf16[52,48,128]{2,1,0:T(8,128)(2,1)S(1)}, bf16[52,48,128]{2,1,0:T(8,128)(2,1)S(1)}, u32[]{:S(2)}, u32[]{:S(2)}) collective-permute-start(bf16[52,48,128]{2,1,0:T(8,128)(2,1)S(1)} %bitcast.28), channel_id=1, source_target_pairs={{1,4},{2,8},{4,1},{7,13},{8,2},{11,14},{13,7},{14,11},{17,20},{18,... | collective-permute-start | bytes 1916936 | tf_op jit(solution)/shard_map/ppermute | solution.py:482
  6.0 5.7 %collective-permute-done = bf16[1600,128]{1,0:T(8,128)(2,1)} collective-permute-done((bf16[1600,128]{1,0:T(8,128)(2,1)S(1)}, bf16[1600,128]{1,0:T(8,128)(2,1)}, u32[]{:S(2)}, u32[]{:S(2)}) %collective-permute-start) | collective-permute-done | bytes 409632 | tf_op jit(solution)/shard_map/ppermute | solution.py:482
  11.7 6.6 %collective-permute-start.1 = (bf16[1600,128]{1,0:T(8,128)(2,1)}, bf16[1600,128]{1,0:T(8,128)(2,1)}, u32[]{:S(2)}, u32[]{:S(2)}) collective-permute-start(bf16[1600,128]{1,0:T(8,128)(2,1)} %collective-permute-done), channel_id=1, source_target_pairs={{15,12},{10,9},{5,6},{0,3},{31,28},{26,25},{21,22},{16,19}} | collective-permute-start | bytes 1228808 | tf_op jit(solution)/shard_map/ppermute | solution.py:482
  18.3 0.7 %collective-permute-start.10 = (bf16[6,64,128]{2,1,0:T(8,128)(2,1)S(1)}, bf16[6,64,128]{2,1,0:T(8,128)(2,1)S(1)}, u32[]{:S(2)}, u32[]{:S(2)}) collective-permute-start(bf16[6,64,128]{2,1,0:T(8,128)(2,1)S(1)} %get-tuple-element.25), channel_id=1, source_target_pairs={{4,8},{8,4},{5,9},{9,5},{6,10},{10,6},{7,11},{11,7},{20,24},{24,20... | collective-permute-start | bytes 294920 | tf_op jit(solution)/shard_map/ppermute | solution.py:388
  19.0 12.7 %collective-permute-start.9 = (bf16[6,64,128]{2,1,0:T(8,128)(2,1)S(1)}, bf16[6,64,128]{2,1,0:T(8,128)(2,1)S(1)}, u32[]{:S(2)}, u32[]{:S(2)}) collective-permute-start(bf16[6,64,128]{2,1,0:T(8,128)(2,1)S(1)} %get-tuple-element.26), channel_id=1, source_target_pairs={{0,4},{8,12},{4,0},{12,8},{1,5},{9,13},{5,1},{13,9},{2,6},{10,14},... | collective-permute-start | bytes 294920 | tf_op jit(solution)/shard_map/ppermute | solution.py:388
  31.7 0.0 collective-permute-done.10.row_far
  31.7 0.9 %collective-permute-done.9.row_near = bf16[6,64,128]{2,1,0:T(8,128)(2,1)S(1)} collective-permute-done((bf16[6,64,128]{2,1,0:T(8,128)(2,1)S(1)}, bf16[6,64,128]{2,1,0:T(8,128)(2,1)S(1)}, u32[]{:S(2)}, u32[]{:S(2)}) %collective-permute-start.9) | collective-permute-done | bytes 98336 | tf_op jit(solution)/shard_map/ppermute | solution.py:388
  32.6 0.1 shard_map.92
  32.8 0.0 copy-start.1
  32.8 0.0 copy-start.2
  32.8 0.0 copy-start.3
  32.8 0.0 copy-start.4
  32.8 0.0 copy-start.5
  32.8 0.0 copy-start.6
  32.9 0.1 collective-permute-start.11
  32.9 0.8 %collective-permute-start.12 = (bf16[456,128]{1,0:T(8,128)(2,1)S(1)}, bf16[456,128]{1,0:T(8,128)(2,1)S(1)}, u32[]{:S(2)}, u32[]{:S(2)}) collective-permute-start(bf16[456,128]{1,0:T(8,128)(2,1)S(1)} %get-tuple-element.17), channel_id=1, source_target_pairs={{1,2},{2,1},{5,6},{6,5},{9,10},{10,9},{13,14},{14,13},{17,18},{18,... | collective-permute-start | bytes 350216 | tf_op jit(solution)/shard_map/ppermute | solution.py:388
  33.7 0.0 collective-permute-done.3
  33.8 2.8 %collective-permute-start.4 = (bf16[52,48,128]{2,1,0:T(8,128)(2,1)}, bf16[52,48,128]{2,1,0:T(8,128)(2,1)S(1)}, u32[]{:S(2)}, u32[]{:S(2)}) collective-permute-start(bf16[52,48,128]{2,1,0:T(8,128)(2,1)} %collective-permute-done.3), channel_id=1, source_target_pairs={{15,12},{10,9},{5,6},{0,3},{31,28},{26,25},{21,22},{16,19}} | collective-permute-start | bytes 1916936 | tf_op jit(solution)/shard_map/ppermute | solution.py:482
  36.5 0.0 collective-permute-done.1
  36.5 1.2 %select_select_fusion.frame = bf16[1600,128]{1,0:T(8,128)(2,1)S(1)} fusion(bf16[1600,128]{1,0:T(8,128)(2,1)} %collective-permute-done.1, bf16[1600,128]{1,0:T(8,128)(2,1)} %collective-permute-done, pred[]{:T(512)S(6)} %eq.14, pred[]{:T(512)S(6)} %eq.13, bf16[416,128]{1,0:T(8,128)(2,1)S(1)} %get-tuple-element.41, bf16[416,128]{1,0:T(8,128)(2,1)S(1)} %get-tuple-element.42, ...), kind=kLoop, calls=%fused_computation.2 | loop fusion | flops 2048000 | bytes 1638402 | tf_op jit(solution)/shard_map/jit(_where)/select_n | solution.py:507
  37.8 0.7 %collective-permute-start.6 = (bf16[6,64,128]{2,1,0:T(8,128)(2,1)S(1)}, bf16[6,64,128]{2,1,0:T(8,128)(2,1)S(1)}, u32[]{:S(2)}, u32[]{:S(2)}) collective-permute-start(bf16[6,64,128]{2,1,0:T(8,128)(2,1)S(1)} %get-tuple-element.35), channel_id=1, source_target_pairs={{4,8},{8,4},{5,9},{9,5},{6,10},{10,6},{7,11},{11,7},{20,24},{24,20... | collective-permute-start | bytes 294920 | tf_op jit(solution)/shard_map/ppermute | solution.py:388
  38.5 0.0 collective-permute-done.6.row_far
  38.5 4.9 %collective-permute-start.5 = (bf16[6,64,128]{2,1,0:T(8,128)(2,1)S(1)}, bf16[6,64,128]{2,1,0:T(8,128)(2,1)S(1)}, u32[]{:S(2)}, u32[]{:S(2)}) collective-permute-start(bf16[6,64,128]{2,1,0:T(8,128)(2,1)S(1)} %get-tuple-element.36), channel_id=1, source_target_pairs={{0,4},{8,12},{4,0},{12,8},{1,5},{9,13},{5,1},{13,9},{2,6},{10,14},... | collective-permute-start | bytes 294920 | tf_op jit(solution)/shard_map/ppermute | solution.py:388
  43.4 0.9 %collective-permute-done.5.row_near = bf16[6,64,128]{2,1,0:T(8,128)(2,1)S(1)} collective-permute-done((bf16[6,64,128]{2,1,0:T(8,128)(2,1)S(1)}, bf16[6,64,128]{2,1,0:T(8,128)(2,1)S(1)}, u32[]{:S(2)}, u32[]{:S(2)}) %collective-permute-start.5) | collective-permute-done | bytes 98336 | tf_op jit(solution)/shard_map/ppermute | solution.py:388
  44.3 0.1 shard_map.91
  44.5 5.5 %collective-permute-start.7 = (bf16[456,128]{1,0:T(8,128)(2,1)S(1)}, bf16[456,128]{1,0:T(8,128)(2,1)S(1)}, u32[]{:S(2)}, u32[]{:S(2)}) collective-permute-start(bf16[456,128]{1,0:T(8,128)(2,1)S(1)} %get-tuple-element.14), channel_id=1, source_target_pairs={{0,1},{2,3},{1,0},{3,2},{4,5},{6,7},{5,4},{7,6},{8,9},{10,11},{9,8... | collective-permute-start | bytes 350216 | tf_op jit(solution)/shard_map/ppermute | solution.py:388
  50.0 0.0 collective-permute-done.11.col_near
  50.0 0.7 %collective-permute-start.8 = (bf16[456,128]{1,0:T(8,128)(2,1)S(1)}, bf16[456,128]{1,0:T(8,128)(2,1)S(1)}, u32[]{:S(2)}, u32[]{:S(2)}) collective-permute-start(bf16[456,128]{1,0:T(8,128)(2,1)S(1)} %get-tuple-element.15), channel_id=1, source_target_pairs={{1,2},{2,1},{5,6},{6,5},{9,10},{10,9},{13,14},{14,13},{17,18},{18,... | collective-permute-start | bytes 350216 | tf_op jit(solution)/shard_map/ppermute | solution.py:388
  50.7 0.0 collective-permute-done.12.col_far
  50.7 0.0 copy-done.1
  50.7 0.0 copy-done.2
  50.7 0.0 copy-done.3
  50.7 0.0 copy-done.4
  50.7 0.0 copy-start.7
  50.8 0.0 copy-start.8
  50.8 3.9 %own_block.1 = (bf16[18,2,2,80,128]{4,3,2,1,0:T(8,128)(2,1)S(1)}, bf16[1536,256]{1,0:T(8,128)(2,1)S(1)}, bf16[256,256]{1,0:T(8,128)(2,1)S(1)}, bf16[1536,256]{1,0:T(8,128)(2,1)S(1)}, bf16[256,256]{1,0:T(8,128)(2,1)S(1)}) custom-call(bf16[64,64,128]{2,1,0:T(8,128)(2,1)S(1)} %copy-done, bf16[6,64,128]{2,1,0:T(8,128)(2,1)S(1)} %collective-permute-done.9.row_near, ...), custom_call_target="tpu_custom_call" | custom-call | flops 3774873600 | bytes 8388608 | tf_op jit(solution)/shard_map/own_block/pallas_call | solution.py:557
  54.7 0.0 collective-permute-done.2.direct
  54.7 0.0 collective-permute-done.7.col_near
  54.7 0.0 collective-permute-done.8.col_far
  54.7 0.0 collective-permute-done.4.relayed
  54.8 8.5 %main_block.1 = f32[64,64,128]{2,1,0:T(8,128)} custom-call(bf16[1600,128]{1,0:T(8,128)(2,1)S(1)} %select_select_fusion.frame, bf16[52,48,128]{2,1,0:T(8,128)(2,1)S(1)} %bitcast.29, bf16[52,48,128]{2,1,0:T(8,128)(2,1)S(1)} %collective-permute-done.2.direct, bf16[52,48,128]{2,1,0:T(8,128)(2,1)S(1)} %collective-permute-done.4.relayed, ...), custom_call_target="tpu_custom_call" | custom-call | flops 7549747200 | bytes 16777216 | tf_op jit(solution)/shard_map/main_block/pallas_call | solution.py:560
  (18 shorter events, 0.3 us)
Async XLA Ops:
  0.0 3.6 %copy-start = (bf16[64,64,128]{2,1,0:T(8,128)(2,1)S(1)}, bf16[64,64,128]{2,1,0:T(8,128)(2,1)}, u32[]{:S(2)}) copy-start(bf16[64,64,128]{2,1,0:T(8,128)(2,1)} %tile.1) | copy-start | bytes 3145732
  2.3 9.4 %collective-permute-start = (bf16[1600,128]{1,0:T(8,128)(2,1)S(1)}, bf16[1600,128]{1,0:T(8,128)(2,1)}, u32[]{:S(2)}, u32[]{:S(2)}) collective-permute-start(bf16[1600,128]{1,0:T(8,128)(2,1)S(1)} %pad_maximum_fusion), channel_id=1, source_target_pairs={{1,4},{2,8},{4,1},{7,13},{8,2},{11,14},{13,7},{14,11},{3,15},{6,10... | collective-permute-start | bytes 1228808 | tf_op jit(solution)/shard_map/ppermute | solution.py:482
  3.9 29.8 %collective-permute-start.3 = (bf16[52,48,128]{2,1,0:T(8,128)(2,1)S(1)}, bf16[52,48,128]{2,1,0:T(8,128)(2,1)}, u32[]{:S(2)}, u32[]{:S(2)}) collective-permute-start(bf16[52,48,128]{2,1,0:T(8,128)(2,1)S(1)} %bitcast.27), channel_id=1, source_target_pairs={{3,15},{6,10},{9,5},{12,0},{19,31},{22,26},{25,21},{28,16}} | collective-permute-start | bytes 1916936 | tf_op jit(solution)/shard_map/ppermute | solution.py:482
  5.2 49.5 %collective-permute-start.2 = (bf16[52,48,128]{2,1,0:T(8,128)(2,1)S(1)}, bf16[52,48,128]{2,1,0:T(8,128)(2,1)S(1)}, u32[]{:S(2)}, u32[]{:S(2)}) collective-permute-start(bf16[52,48,128]{2,1,0:T(8,128)(2,1)S(1)} %bitcast.28), channel_id=1, source_target_pairs={{1,4},{2,8},{4,1},{7,13},{8,2},{11,14},{13,7},{14,11},{17,20},{18,... | collective-permute-start | bytes 1916936 | tf_op jit(solution)/shard_map/ppermute | solution.py:482
  11.7 24.8 %collective-permute-start.1 = (bf16[1600,128]{1,0:T(8,128)(2,1)}, bf16[1600,128]{1,0:T(8,128)(2,1)}, u32[]{:S(2)}, u32[]{:S(2)}) collective-permute-start(bf16[1600,128]{1,0:T(8,128)(2,1)} %collective-permute-done), channel_id=1, source_target_pairs={{15,12},{10,9},{5,6},{0,3},{31,28},{26,25},{21,22},{16,19}} | collective-permute-start | bytes 1228808 | tf_op jit(solution)/shard_map/ppermute | solution.py:482
  18.3 13.4 %collective-permute-start.10 = (bf16[6,64,128]{2,1,0:T(8,128)(2,1)S(1)}, bf16[6,64,128]{2,1,0:T(8,128)(2,1)S(1)}, u32[]{:S(2)}, u32[]{:S(2)}) collective-permute-start(bf16[6,64,128]{2,1,0:T(8,128)(2,1)S(1)} %get-tuple-element.25), channel_id=1, source_target_pairs={{4,8},{8,4},{5,9},{9,5},{6,10},{10,6},{7,11},{11,7},{20,24},{24,20... | collective-permute-start | bytes 294920 | tf_op jit(solution)/shard_map/ppermute | solution.py:388
  19.0 13.6 %collective-permute-start.9 = (bf16[6,64,128]{2,1,0:T(8,128)(2,1)S(1)}, bf16[6,64,128]{2,1,0:T(8,128)(2,1)S(1)}, u32[]{:S(2)}, u32[]{:S(2)}) collective-permute-start(bf16[6,64,128]{2,1,0:T(8,128)(2,1)S(1)} %get-tuple-element.26), channel_id=1, source_target_pairs={{0,4},{8,12},{4,0},{12,8},{1,5},{9,13},{5,1},{13,9},{2,6},{10,14},... | collective-permute-start | bytes 294920 | tf_op jit(solution)/shard_map/ppermute | solution.py:388
  32.8 17.9 %copy-start.1 = (bf16[3,3,128,128]{3,2,1,0:T(8,128)(2,1)S(1)}, bf16[3,3,128,128]{3,2,1,0:T(8,128)(2,1)}, u32[]{:S(2)}) copy-start(bf16[3,3,128,128]{3,2,1,0:T(8,128)(2,1)} %kernel.1) | copy-start | bytes 884740
  32.8 17.9 %copy-start.2 = (bf16[3,3,128,128]{3,2,1,0:T(8,128)(2,1)S(1)}, bf16[3,3,128,128]{3,2,1,0:T(8,128)(2,1)}, u32[]{:S(2)}) copy-start(bf16[3,3,128,128]{3,2,1,0:T(8,128)(2,1)} %far_kernel.1) | copy-start | bytes 884740
  32.8 17.9 %copy-start.3 = (bf16[128,128]{1,0:T(8,128)(2,1)S(1)}, bf16[128,128]{1,0:T(8,128)(2,1)}, u32[]{:S(2)}) copy-start(bf16[128,128]{1,0:T(8,128)(2,1)} %mixer.1) | copy-start | bytes 98308
  32.8 17.9 %copy-start.4 = (bf16[128,128]{1,0:T(8,128)(2,1)S(1)}, bf16[128,128]{1,0:T(8,128)(2,1)}, u32[]{:S(2)}) copy-start(bf16[128,128]{1,0:T(8,128)(2,1)} %far_mixer.1) | copy-start | bytes 98308
  32.8 17.9 %copy-start.5 = (f32[128]{0:T(128)S(1)}, f32[128]{0:T(128)}, u32[]{:S(2)}) copy-start(f32[128]{0:T(128)} %param.13) | copy-start | bytes 1540
  32.8 17.9 %copy-start.6 = (f32[128]{0:T(128)S(1)}, f32[128]{0:T(128)}, u32[]{:S(2)}) copy-start(f32[128]{0:T(128)} %param.11) | copy-start | bytes 1540
  32.9 17.1 %collective-permute-start.11 = (bf16[456,128]{1,0:T(8,128)(2,1)S(1)}, bf16[456,128]{1,0:T(8,128)(2,1)S(1)}, u32[]{:S(2)}, u32[]{:S(2)}) collective-permute-start(bf16[456,128]{1,0:T(8,128)(2,1)S(1)} %get-tuple-element.16), channel_id=1, source_target_pairs={{0,1},{2,3},{1,0},{3,2},{4,5},{6,7},{5,4},{7,6},{8,9},{10,11},{9,8... | collective-permute-start | bytes 350216 | tf_op jit(solution)/shard_map/ppermute | solution.py:388
  32.9 17.7 %collective-permute-start.12 = (bf16[456,128]{1,0:T(8,128)(2,1)S(1)}, bf16[456,128]{1,0:T(8,128)(2,1)S(1)}, u32[]{:S(2)}, u32[]{:S(2)}) collective-permute-start(bf16[456,128]{1,0:T(8,128)(2,1)S(1)} %get-tuple-element.17), channel_id=1, source_target_pairs={{1,2},{2,1},{5,6},{6,5},{9,10},{10,9},{13,14},{14,13},{17,18},{18,... | collective-permute-start | bytes 350216 | tf_op jit(solution)/shard_map/ppermute | solution.py:388
  33.8 21.0 %collective-permute-start.4 = (bf16[52,48,128]{2,1,0:T(8,128)(2,1)}, bf16[52,48,128]{2,1,0:T(8,128)(2,1)S(1)}, u32[]{:S(2)}, u32[]{:S(2)}) collective-permute-start(bf16[52,48,128]{2,1,0:T(8,128)(2,1)} %collective-permute-done.3), channel_id=1, source_target_pairs={{15,12},{10,9},{5,6},{0,3},{31,28},{26,25},{21,22},{16,19}} | collective-permute-start | bytes 1916936 | tf_op jit(solution)/shard_map/ppermute | solution.py:482
  37.8 0.7 %collective-permute-start.6 = (bf16[6,64,128]{2,1,0:T(8,128)(2,1)S(1)}, bf16[6,64,128]{2,1,0:T(8,128)(2,1)S(1)}, u32[]{:S(2)}, u32[]{:S(2)}) collective-permute-start(bf16[6,64,128]{2,1,0:T(8,128)(2,1)S(1)} %get-tuple-element.35), channel_id=1, source_target_pairs={{4,8},{8,4},{5,9},{9,5},{6,10},{10,6},{7,11},{11,7},{20,24},{24,20... | collective-permute-start | bytes 294920 | tf_op jit(solution)/shard_map/ppermute | solution.py:388
  38.5 5.8 %collective-permute-start.5 = (bf16[6,64,128]{2,1,0:T(8,128)(2,1)S(1)}, bf16[6,64,128]{2,1,0:T(8,128)(2,1)S(1)}, u32[]{:S(2)}, u32[]{:S(2)}) collective-permute-start(bf16[6,64,128]{2,1,0:T(8,128)(2,1)S(1)} %get-tuple-element.36), channel_id=1, source_target_pairs={{0,4},{8,12},{4,0},{12,8},{1,5},{9,13},{5,1},{13,9},{2,6},{10,14},... | collective-permute-start | bytes 294920 | tf_op jit(solution)/shard_map/ppermute | solution.py:388
  44.5 10.2 %collective-permute-start.7 = (bf16[456,128]{1,0:T(8,128)(2,1)S(1)}, bf16[456,128]{1,0:T(8,128)(2,1)S(1)}, u32[]{:S(2)}, u32[]{:S(2)}) collective-permute-start(bf16[456,128]{1,0:T(8,128)(2,1)S(1)} %get-tuple-element.14), channel_id=1, source_target_pairs={{0,1},{2,3},{1,0},{3,2},{4,5},{6,7},{5,4},{7,6},{8,9},{10,11},{9,8... | collective-permute-start | bytes 350216 | tf_op jit(solution)/shard_map/ppermute | solution.py:388
  50.0 4.7 %collective-permute-start.8 = (bf16[456,128]{1,0:T(8,128)(2,1)S(1)}, bf16[456,128]{1,0:T(8,128)(2,1)S(1)}, u32[]{:S(2)}, u32[]{:S(2)}) collective-permute-start(bf16[456,128]{1,0:T(8,128)(2,1)S(1)} %get-tuple-element.15), channel_id=1, source_target_pairs={{1,2},{2,1},{5,6},{6,5},{9,10},{10,9},{13,14},{14,13},{17,18},{18,... | collective-permute-start | bytes 350216 | tf_op jit(solution)/shard_map/ppermute | solution.py:388
  50.7 4.0 %copy-start.7 = (f32[128]{0:T(128)S(1)}, f32[128]{0:T(128)}, u32[]{:S(2)}) copy-start(f32[128]{0:T(128)} %param.15) | copy-start | bytes 1540
  50.8 4.0 %copy-start.8 = (f32[128]{0:T(128)S(1)}, f32[128]{0:T(128)}, u32[]{:S(2)}) copy-start(f32[128]{0:T(128)} %param.17) | copy-start | bytes 1540
